TPU v7x, 256 devices: a whole 4x4x8 slice. The times are simulated.
256 devices in a mesh: gx: 8 (over z_lo, core), gy: 8 (over y, z_hi), gz: 4 (over x).
Axes of the slice: x: 4, y: 4, z: 8 (z_hi: 2, z_lo: 4; z = z_hi * 4 + z_lo), core: 2. Of those that a mesh axis runs over, the one named last changes fastest.
Arguments:
- positions: float32 [3, 32, 32, 8, 128], P(None, 'gx', 'gy', 'gz'), may hold values from 0 to 1
- line_vectors: float32 [3, 32, 32, 8, 128], P(None, 'gx', 'gy', 'gz'), may hold values from -3 to 3
- burgers: float32 [3, 32, 32, 8, 128], P(None, 'gx', 'gy', 'gz'), may hold values from -6 to 6
- mobility: float32 [32, 32, 8, 128], P('gx', 'gy', 'gz'), may hold values from 0.25 to 4
- occupancy: int32 [32, 32, 8], P('gx', 'gy', 'gz'), may hold values from 1 to 128
Outputs:
- moved_positions: float32 [3, 32, 32, 8, 128], P(None, 'gx', 'gy', 'gz')
- end_forces: float32 [3, 32, 32, 8, 128], P(None, 'gx', 'gy', 'gz')
All inputs are finite; a program needn't handle non-finite values.
Results may differ from a plain program's by a relative error of at most 0.0001.
Values sent between devices are 32-bit elements; how exact they have to be, the bound alone decides.
No kernel may reach another device: no remote copies, remote signals or barrier semaphores. Data moves between devices by JAX's collectives and lax.ppermute only.
A program may use at most 64 MiB of HBM per device.

v0:
```python
import functools

import jax
import jax.numpy as jnp
from jax import lax
from jax.sharding import Mesh
from jax.sharding import PartitionSpec as P

GX_GY_GZ = ("gx_0", "gx_1", "gy_0", "gy_1", "gz")
GX = ("gx_0", "gx_1")
GY = ("gy_0", "gy_1")


CORE_SQUARED = 0.25
MU_SCALE = 0.05
CROSS_WEIGHT = 0.5
STEP_LIMIT = 0.1
CELL_BLOCK = 4
NEIGHBOUR_SHIFTS = [
    (first, second, third) for first in (-1, 0, 1) for second in (-1, 0, 1) for third in (-1, 0, 1)
]


def extended(block, sides, width):
    for axis, dim in sides:
        count = lax.axis_size(axis)
        forward = [(i, i + 1) for i in range(count - 1)]
        forward.append((count - 1, 0))
        backward = [(target, source) for source, target in forward]
        low = lax.ppermute(
            lax.slice_in_dim(block, block.shape[dim] - width, None, axis=dim), axis, forward
        )
        high = lax.ppermute(lax.slice_in_dim(block, 0, width, axis=dim), axis, backward)
        block = jnp.concatenate([low, block, high], axis=dim)
    return block


def over_axes(x, axes):
    return functools.reduce(lax.pmax, axes, x)


def inner_pairs(left, right):
    return sum((left[k][..., :, None] * right[k][..., None, :] for k in range(3)))


def tile_force(target, source):
    separate = [target[k][..., :, None] - source[k][..., None, :] for k in range(3)]
    radius_sq = (
        separate[0] * separate[0]
        + separate[1] * separate[1]
        + separate[2] * separate[2]
        + CORE_SQUARED
    )
    inverse = lax.rsqrt(radius_sq)
    couple = inner_pairs(target[6:9], source[6:9]) * inner_pairs(target[3:6], source[3:6])
    couple = couple - CROSS_WEIGHT * inner_pairs(target[6:9], source[3:6]) * inner_pairs(
        target[3:6], source[6:9]
    )
    weight = couple * source[9][..., None, :] * inverse * inverse * inverse
    return jnp.stack([jnp.sum(weight * separate[k], axis=-1) for k in range(3)]) * (
        MU_SCALE * target[9]
    )


def local_forces(fields, padded):
    width, count_x, count_y, count_z, slot_count = fields.shape
    pieces = []
    for offset in NEIGHBOUR_SHIFTS:
        source = padded[
            :,
            1 + offset[0] : 1 + offset[0] + count_x,
            1 + offset[1] : 1 + offset[1] + count_y,
            1 + offset[2] : 1 + offset[2] + count_z,
        ]
        shift_vec = jnp.array([float(offset[0]), float(offset[1]), float(offset[2])], jnp.float32)
        moved_src = source[0:3] + shift_vec[:, None, None, None, None]
        pieces.append(jnp.concatenate([moved_src, source[3:]], 0))
    sources = jnp.concatenate(pieces, 4)
    cell_count = count_x * count_y * count_z
    blocks = cell_count // CELL_BLOCK
    targets = jnp.moveaxis(fields.reshape(width, blocks, CELL_BLOCK, slot_count), 1, 0)
    sources = jnp.moveaxis(sources.reshape(width, blocks, CELL_BLOCK, sources.shape[4]), 1, 0)
    result = lax.map(lambda pair: tile_force(pair[0], pair[1]), (targets, sources))
    return jnp.moveaxis(result, 0, 1).reshape(3, count_x, count_y, count_z, slot_count)


def on_device(positions, line_vectors, burgers, mobility, occupancy):
    slots = lax.broadcasted_iota(jnp.int32, mobility.shape, 3)
    live = (slots < occupancy[..., None]).astype(jnp.float32)
    fixed_part = jnp.concatenate([line_vectors, burgers, live[None]], 0)
    fields = jnp.concatenate([positions, fixed_part], 0)
    padded = extended(fields, ((GX, 1), (GY, 2), ("gz", 3)), 1)
    start_forces = local_forces(fields, padded)
    speed0 = mobility[None] * start_forces
    peak = over_axes(jnp.max(jnp.sum(speed0 * speed0, axis=0)), GX_GY_GZ)
    step = STEP_LIMIT * lax.rsqrt(peak + 1e-12)
    predicted = positions + step * speed0
    fields_next = jnp.concatenate([predicted, fixed_part], 0)
    moved_rim = extended(predicted, ((GX, 1), (GY, 2), ("gz", 3)), 1)
    padded_next = jnp.concatenate([moved_rim, padded[3:]], 0)
    end_forces = local_forces(fields_next, padded_next)
    moved_positions = positions + 0.5 * step * (speed0 + mobility[None] * end_forces)
    return (moved_positions, end_forces)


def solution(mesh):
    finer = Mesh(
        mesh.devices.reshape(4, 2, 4, 2, mesh.shape["gz"]), ("gx_0", "gx_1", "gy_0", "gy_1", "gz")
    )
    in_specs = (
        P(None, GX, GY, "gz", None),
        P(None, GX, GY, "gz", None),
        P(None, GX, GY, "gz", None),
        P(GX, GY, "gz", None),
        P(GX, GY, "gz"),
    )
    out_specs = (P(None, GX, GY, "gz", None), P(None, GX, GY, "gz", None))
    return jax.shard_map(
        on_device, mesh=finer, in_specs=in_specs, out_specs=out_specs, check_vma=False
    )
```

profile of v0, /device:TPU:8, one launch (start us, length us, event | category | flops | bytes accessed | tf_op | source)
XLA Modules:
  0.0 368.2 jit_solution(18182778234756152864)
XLA Ops:
  1.7 0.9 pad_maximum_fusion.11
  2.7 4.1 %collective-permute-start.1 = (f32[10,1,4,2,128]{4,3,2,1,0:T(2,128)S(1)}, f32[10,1,4,2,128]{4,3,2,1,0:T(2,128)S(1)}, u32[]{:S(2)}, u32[]{:S(2)}) collective-permute-start(f32[10,1,4,2,128]{4,3,2,1,0:T(2,128)S(1)} %get-tuple-element.211), channel_id=1, source_target_pairs={{32,0},{64,32},{96,64},{128,96},{160,128},{192,160},{224,192},{0,2... | collective-permute-start | bytes 122888 | tf_op jit(solution)/shard_map/ppermute | solution.py:33
  9.4 6.7 %collective-permute-start.2 = (f32[10,6,1,2,128]{4,3,2,1,0:T(2,128)S(1)}, f32[10,6,1,2,128]{4,3,2,1,0:T(2,128)S(1)}, u32[]{:S(2)}, u32[]{:S(2)}) collective-permute-start(f32[10,6,1,2,128]{4,3,2,1,0:T(2,128)S(1)} %get-tuple-element.188), channel_id=1, source_target_pairs={{0,4},{4,8},{8,12},{12,16},{16,20},{20,24},{24,28},{28,0},{1,5},{5... | collective-permute-start | bytes 184328 | tf_op jit(solution)/shard_map/ppermute | solution.py:30
  16.3 0.9 maximum_add_fusion.1
  17.3 1.5 collective-permute-done.2
  18.8 5.9 %collective-permute-done.3 = f32[10,6,1,2,128]{4,3,2,1,0:T(2,128)S(1)} collective-permute-done((f32[10,6,1,2,128]{4,3,2,1,0:T(2,128)S(1)}, f32[10,6,1,2,128]{4,3,2,1,0:T(2,128)S(1)}, u32[]{:S(2)}, u32[]{:S(2)}) %collective-permute-start.3) | collective-permute-done | bytes 61472 | tf_op jit(solution)/shard_map/ppermute | solution.py:33
  24.7 1.0 pad_maximum_fusion.1
  26.0 1.6 collective-permute-start.4
  27.5 1.7 collective-permute-start.5
  29.3 1.2 pad_maximum_fusion.2
  31.2 1.5 collective-permute-done.4
  33.1 1.2 pad_maximum_fusion
  34.3 0.9 fusion.28
  56.6 6.8 %reshape.339 = f32[10,8,4,3456]{3,2,1,0:T(4,128)} reshape(f32[10,4,4,2,3456]{4,3,2,1,0:T(2,128)} %maximum_dynamic-update-slice_fusion) | data formatting | bytes 8847360 | tf_op jit(solution)/shard_map/reshape | solution.py:82
  63.4 4.6 %copy.99 = f32[10,8,4,3456]{3,2,0,1:T(4,128)} copy(f32[10,8,4,3456]{3,2,1,0:T(4,128)} %reshape.339) | data formatting | bytes 8847360 | tf_op jit(solution)/shard_map/reshape | solution.py:82
  68.0 99.8 %while.20 = (s32[]{:T(128)}, f32[8,3,4,128]{3,2,1,0:T(4,128)S(1)}, f32[8,10,4,128]{3,2,0,1:T(4,128)S(1)}, f32[8,10,4,3456]{3,2,1,0:T(4,128)}, s32[]{:T(128)}, /*...) while((s32[]{:T(128)}, f32[8,3,4,128]{3,2,1,0:T(4,128)S(1)}, ...), condition=%wide.region_4.5_spmd, body=%wide.region_0.4_spmd.sunk | while | flops 76090888 | bytes 1780009 | solution.py:83
  68.1 1.1 dynamic-slice_bitcast_fusion.26
  69.2 11.3 %fusion.43 = (f32[4,128]{1,0:T(4,128)S(1)}, f32[4,128]{1,0:T(4,128)S(1)}, f32[4,128]{1,0:T(4,128)S(1)}) fusion(f32[4,3456]{1,0:T(4,128)S(1)} %get-tuple-element.334, f32[4,128]{1,0:T(4,128)S(1)} %get-tuple-element.335, f32[4,3456]{1,0:T(4,128)S(1)} %get-tuple-element.336, f32[4,128]{1,0:T(4,128)S(1)} %get-tuple-element.337, ...), kind=kLoop, calls=%fused_computation.11.clone.1 | loop fusion | flops 76085760 | bytes 577536 | tf_op jit(solution)/shard_map/while/body/eval_jaxpr/reduce_sum | solution.py:60
  80.5 1.1 dynamic-slice_bitcast_fusion.26
  81.7 11.3 %fusion.43 = (f32[4,128]{1,0:T(4,128)S(1)}, f32[4,128]{1,0:T(4,128)S(1)}, f32[4,128]{1,0:T(4,128)S(1)}) fusion(f32[4,3456]{1,0:T(4,128)S(1)} %get-tuple-element.334, f32[4,128]{1,0:T(4,128)S(1)} %get-tuple-element.335, f32[4,3456]{1,0:T(4,128)S(1)} %get-tuple-element.336, f32[4,128]{1,0:T(4,128)S(1)} %get-tuple-element.337, ...), kind=kLoop, calls=%fused_computation.11.clone.1 | loop fusion | flops 76085760 | bytes 577536 | tf_op jit(solution)/shard_map/while/body/eval_jaxpr/reduce_sum | solution.py:60
  93.0 1.1 dynamic-slice_bitcast_fusion.26
  94.2 11.3 %fusion.43 = (f32[4,128]{1,0:T(4,128)S(1)}, f32[4,128]{1,0:T(4,128)S(1)}, f32[4,128]{1,0:T(4,128)S(1)}) fusion(f32[4,3456]{1,0:T(4,128)S(1)} %get-tuple-element.334, f32[4,128]{1,0:T(4,128)S(1)} %get-tuple-element.335, f32[4,3456]{1,0:T(4,128)S(1)} %get-tuple-element.336, f32[4,128]{1,0:T(4,128)S(1)} %get-tuple-element.337, ...), kind=kLoop, calls=%fused_computation.11.clone.1 | loop fusion | flops 76085760 | bytes 577536 | tf_op jit(solution)/shard_map/while/body/eval_jaxpr/reduce_sum | solution.py:60
  105.5 1.1 dynamic-slice_bitcast_fusion.26
  106.6 11.3 %fusion.43 = (f32[4,128]{1,0:T(4,128)S(1)}, f32[4,128]{1,0:T(4,128)S(1)}, f32[4,128]{1,0:T(4,128)S(1)}) fusion(f32[4,3456]{1,0:T(4,128)S(1)} %get-tuple-element.334, f32[4,128]{1,0:T(4,128)S(1)} %get-tuple-element.335, f32[4,3456]{1,0:T(4,128)S(1)} %get-tuple-element.336, f32[4,128]{1,0:T(4,128)S(1)} %get-tuple-element.337, ...), kind=kLoop, calls=%fused_computation.11.clone.1 | loop fusion | flops 76085760 | bytes 577536 | tf_op jit(solution)/shard_map/while/body/eval_jaxpr/reduce_sum | solution.py:60
  117.9 1.1 dynamic-slice_bitcast_fusion.26
  119.1 11.3 %fusion.43 = (f32[4,128]{1,0:T(4,128)S(1)}, f32[4,128]{1,0:T(4,128)S(1)}, f32[4,128]{1,0:T(4,128)S(1)}) fusion(f32[4,3456]{1,0:T(4,128)S(1)} %get-tuple-element.334, f32[4,128]{1,0:T(4,128)S(1)} %get-tuple-element.335, f32[4,3456]{1,0:T(4,128)S(1)} %get-tuple-element.336, f32[4,128]{1,0:T(4,128)S(1)} %get-tuple-element.337, ...), kind=kLoop, calls=%fused_computation.11.clone.1 | loop fusion | flops 76085760 | bytes 577536 | tf_op jit(solution)/shard_map/while/body/eval_jaxpr/reduce_sum | solution.py:60
  130.4 1.1 dynamic-slice_bitcast_fusion.26
  131.6 11.3 %fusion.43 = (f32[4,128]{1,0:T(4,128)S(1)}, f32[4,128]{1,0:T(4,128)S(1)}, f32[4,128]{1,0:T(4,128)S(1)}) fusion(f32[4,3456]{1,0:T(4,128)S(1)} %get-tuple-element.334, f32[4,128]{1,0:T(4,128)S(1)} %get-tuple-element.335, f32[4,3456]{1,0:T(4,128)S(1)} %get-tuple-element.336, f32[4,128]{1,0:T(4,128)S(1)} %get-tuple-element.337, ...), kind=kLoop, calls=%fused_computation.11.clone.1 | loop fusion | flops 76085760 | bytes 577536 | tf_op jit(solution)/shard_map/while/body/eval_jaxpr/reduce_sum | solution.py:60
  142.9 1.1 dynamic-slice_bitcast_fusion.26
  144.0 11.3 %fusion.43 = (f32[4,128]{1,0:T(4,128)S(1)}, f32[4,128]{1,0:T(4,128)S(1)}, f32[4,128]{1,0:T(4,128)S(1)}) fusion(f32[4,3456]{1,0:T(4,128)S(1)} %get-tuple-element.334, f32[4,128]{1,0:T(4,128)S(1)} %get-tuple-element.335, f32[4,3456]{1,0:T(4,128)S(1)} %get-tuple-element.336, f32[4,128]{1,0:T(4,128)S(1)} %get-tuple-element.337, ...), kind=kLoop, calls=%fused_computation.11.clone.1 | loop fusion | flops 76085760 | bytes 577536 | tf_op jit(solution)/shard_map/while/body/eval_jaxpr/reduce_sum | solution.py:60
  155.4 1.1 dynamic-slice_bitcast_fusion.26
  156.5 11.3 %fusion.43 = (f32[4,128]{1,0:T(4,128)S(1)}, f32[4,128]{1,0:T(4,128)S(1)}, f32[4,128]{1,0:T(4,128)S(1)}) fusion(f32[4,3456]{1,0:T(4,128)S(1)} %get-tuple-element.334, f32[4,128]{1,0:T(4,128)S(1)} %get-tuple-element.335, f32[4,3456]{1,0:T(4,128)S(1)} %get-tuple-element.336, f32[4,128]{1,0:T(4,128)S(1)} %get-tuple-element.337, ...), kind=kLoop, calls=%fused_computation.11.clone.1 | loop fusion | flops 76085760 | bytes 577536 | tf_op jit(solution)/shard_map/while/body/eval_jaxpr/reduce_sum | solution.py:60
  168.5 10.4 %pmax.35 = f32[]{:T(128)} all-reduce(f32[]{:T(128)} %reduce_max.9), channel_id=1, replica_groups=mesh['gx_0'=4,'gx_1'=2,'gy_0'=4,'gy_1'=2,'gz'=4] {'gx_0'}, use_global_device_ids=true, to_apply=%region_7.8 | all-reduce | flops 1 | bytes 8 | tf_op jit(solution)/shard_map/pmax | solution.py:39
  178.9 3.1 pmax.36
  182.0 9.9 %pmax.37 = f32[]{:T(128)} all-reduce(f32[]{:T(128)} %pmax.36), channel_id=1, replica_groups=mesh['gx_0'=4,'gx_1'=2,'gy_0'=4,'gy_1'=2,'gz'=4] {'gy_0'}, use_global_device_ids=true, to_apply=%region_9.10 | all-reduce | flops 1 | bytes 8 | tf_op jit(solution)/shard_map/pmax | solution.py:39
  191.9 9.5 %pmax.38 = f32[]{:T(128)} all-reduce(f32[]{:T(128)} %pmax.37), channel_id=1, replica_groups=mesh['gx_0'=4,'gx_1'=2,'gy_0'=4,'gy_1'=2,'gz'=4] {'gy_1'}, use_global_device_ids=true, to_apply=%region_10.11 | all-reduce | flops 1 | bytes 8 | tf_op jit(solution)/shard_map/pmax | solution.py:39
  201.4 11.4 %pmax.39 = f32[]{:T(128)} all-reduce(f32[]{:T(128)} %pmax.38), channel_id=1, replica_groups=mesh['gx_0'=4,'gx_1'=2,'gy_0'=4,'gy_1'=2,'gz'=4] {'gz'}, use_global_device_ids=true, to_apply=%region_11.12 | all-reduce | flops 1 | bytes 8 | tf_op jit(solution)/shard_map/pmax | solution.py:39
  213.5 3.5 collective-permute-start.7
  217.1 1.3 collective-permute-done.6
  218.5 2.9 collective-permute-start.8
  221.4 4.3 %collective-permute-start.9 = (f32[3,6,1,2,128]{4,3,2,1,0:T(2,128)S(1)}, f32[3,6,1,2,128]{4,3,2,1,0:T(2,128)S(1)}, u32[]{:S(2)}, u32[]{:S(2)}) collective-permute-start(f32[3,6,1,2,128]{4,3,2,1,0:T(2,128)S(1)} %get-tuple-element.225), channel_id=1, source_target_pairs={{4,0},{8,4},{12,8},{16,12},{20,16},{24,20},{28,24},{0,28},{5,1},{9... | collective-permute-start | bytes 55304 | tf_op jit(solution)/shard_map/ppermute | solution.py:33
  225.7 1.6 collective-permute-done.8
  227.4 1.7 collective-permute-done.9
  229.5 3.2 collective-permute-start.11
  232.8 2.0 collective-permute-done.10
  256.3 6.8 %reshape.341 = f32[10,8,4,3456]{3,2,1,0:T(4,128)} reshape(f32[10,4,4,2,3456]{4,3,2,1,0:T(2,128)} %maximum_dynamic-update-slice_fusion.26) | data formatting | bytes 8847360 | tf_op jit(solution)/shard_map/reshape | solution.py:82
  263.1 4.6 %copy.98 = f32[10,8,4,3456]{3,2,0,1:T(4,128)} copy(f32[10,8,4,3456]{3,2,1,0:T(4,128)} %reshape.341) | data formatting | bytes 8847360 | tf_op jit(solution)/shard_map/reshape | solution.py:82
  267.7 99.8 %while.21 = (s32[]{:T(128)}, f32[8,3,4,128]{3,2,1,0:T(4,128)S(1)}, f32[8,10,4,128]{3,2,0,1:T(4,128)S(1)}, f32[8,10,4,3456]{3,2,1,0:T(4,128)}, s32[]{:T(128)}, /*...) while((s32[]{:T(128)}, f32[8,3,4,128]{3,2,1,0:T(4,128)S(1)}, ...), condition=%wide.region_16.17_spmd, body=%wide.region_12.16_spmd.sunk | while | flops 76090888 | bytes 1780009 | solution.py:83
  267.7 1.1 dynamic-slice_bitcast_fusion.28
  268.9 11.3 %fusion.46 = (f32[4,128]{1,0:T(4,128)S(1)}, f32[4,128]{1,0:T(4,128)S(1)}, f32[4,128]{1,0:T(4,128)S(1)}) fusion(f32[4,3456]{1,0:T(4,128)S(1)} %get-tuple-element.361, f32[4,128]{1,0:T(4,128)S(1)} %get-tuple-element.362, f32[4,3456]{1,0:T(4,128)S(1)} %get-tuple-element.363, f32[4,128]{1,0:T(4,128)S(1)} %get-tuple-element.364, ...), kind=kLoop, calls=%fused_computation.49.clone.1 | loop fusion | flops 76085760 | bytes 577536 | tf_op jit(solution)/shard_map/while/body/eval_jaxpr/reduce_sum | solution.py:60
  280.2 1.1 dynamic-slice_bitcast_fusion.28
  281.4 11.3 %fusion.46 = (f32[4,128]{1,0:T(4,128)S(1)}, f32[4,128]{1,0:T(4,128)S(1)}, f32[4,128]{1,0:T(4,128)S(1)}) fusion(f32[4,3456]{1,0:T(4,128)S(1)} %get-tuple-element.361, f32[4,128]{1,0:T(4,128)S(1)} %get-tuple-element.362, f32[4,3456]{1,0:T(4,128)S(1)} %get-tuple-element.363, f32[4,128]{1,0:T(4,128)S(1)} %get-tuple-element.364, ...), kind=kLoop, calls=%fused_computation.49.clone.1 | loop fusion | flops 76085760 | bytes 577536 | tf_op jit(solution)/shard_map/while/body/eval_jaxpr/reduce_sum | solution.py:60
  292.7 1.1 dynamic-slice_bitcast_fusion.28
  293.8 11.3 %fusion.46 = (f32[4,128]{1,0:T(4,128)S(1)}, f32[4,128]{1,0:T(4,128)S(1)}, f32[4,128]{1,0:T(4,128)S(1)}) fusion(f32[4,3456]{1,0:T(4,128)S(1)} %get-tuple-element.361, f32[4,128]{1,0:T(4,128)S(1)} %get-tuple-element.362, f32[4,3456]{1,0:T(4,128)S(1)} %get-tuple-element.363, f32[4,128]{1,0:T(4,128)S(1)} %get-tuple-element.364, ...), kind=kLoop, calls=%fused_computation.49.clone.1 | loop fusion | flops 76085760 | bytes 577536 | tf_op jit(solution)/shard_map/while/body/eval_jaxpr/reduce_sum | solution.py:60
  305.2 1.1 dynamic-slice_bitcast_fusion.28
  306.3 11.3 %fusion.46 = (f32[4,128]{1,0:T(4,128)S(1)}, f32[4,128]{1,0:T(4,128)S(1)}, f32[4,128]{1,0:T(4,128)S(1)}) fusion(f32[4,3456]{1,0:T(4,128)S(1)} %get-tuple-element.361, f32[4,128]{1,0:T(4,128)S(1)} %get-tuple-element.362, f32[4,3456]{1,0:T(4,128)S(1)} %get-tuple-element.363, f32[4,128]{1,0:T(4,128)S(1)} %get-tuple-element.364, ...), kind=kLoop, calls=%fused_computation.49.clone.1 | loop fusion | flops 76085760 | bytes 577536 | tf_op jit(solution)/shard_map/while/body/eval_jaxpr/reduce_sum | solution.py:60
  317.6 1.1 dynamic-slice_bitcast_fusion.28
  318.8 11.3 %fusion.46 = (f32[4,128]{1,0:T(4,128)S(1)}, f32[4,128]{1,0:T(4,128)S(1)}, f32[4,128]{1,0:T(4,128)S(1)}) fusion(f32[4,3456]{1,0:T(4,128)S(1)} %get-tuple-element.361, f32[4,128]{1,0:T(4,128)S(1)} %get-tuple-element.362, f32[4,3456]{1,0:T(4,128)S(1)} %get-tuple-element.363, f32[4,128]{1,0:T(4,128)S(1)} %get-tuple-element.364, ...), kind=kLoop, calls=%fused_computation.49.clone.1 | loop fusion | flops 76085760 | bytes 577536 | tf_op jit(solution)/shard_map/while/body/eval_jaxpr/reduce_sum | solution.py:60
  330.1 1.1 dynamic-slice_bitcast_fusion.28
  331.3 11.3 %fusion.46 = (f32[4,128]{1,0:T(4,128)S(1)}, f32[4,128]{1,0:T(4,128)S(1)}, f32[4,128]{1,0:T(4,128)S(1)}) fusion(f32[4,3456]{1,0:T(4,128)S(1)} %get-tuple-element.361, f32[4,128]{1,0:T(4,128)S(1)} %get-tuple-element.362, f32[4,3456]{1,0:T(4,128)S(1)} %get-tuple-element.363, f32[4,128]{1,0:T(4,128)S(1)} %get-tuple-element.364, ...), kind=kLoop, calls=%fused_computation.49.clone.1 | loop fusion | flops 76085760 | bytes 577536 | tf_op jit(solution)/shard_map/while/body/eval_jaxpr/reduce_sum | solution.py:60
  342.6 1.1 dynamic-slice_bitcast_fusion.28
  343.8 11.3 %fusion.46 = (f32[4,128]{1,0:T(4,128)S(1)}, f32[4,128]{1,0:T(4,128)S(1)}, f32[4,128]{1,0:T(4,128)S(1)}) fusion(f32[4,3456]{1,0:T(4,128)S(1)} %get-tuple-element.361, f32[4,128]{1,0:T(4,128)S(1)} %get-tuple-element.362, f32[4,3456]{1,0:T(4,128)S(1)} %get-tuple-element.363, f32[4,128]{1,0:T(4,128)S(1)} %get-tuple-element.364, ...), kind=kLoop, calls=%fused_computation.49.clone.1 | loop fusion | flops 76085760 | bytes 577536 | tf_op jit(solution)/shard_map/while/body/eval_jaxpr/reduce_sum | solution.py:60
  355.1 1.1 dynamic-slice_bitcast_fusion.28
  356.2 11.3 %fusion.46 = (f32[4,128]{1,0:T(4,128)S(1)}, f32[4,128]{1,0:T(4,128)S(1)}, f32[4,128]{1,0:T(4,128)S(1)}) fusion(f32[4,3456]{1,0:T(4,128)S(1)} %get-tuple-element.361, f32[4,128]{1,0:T(4,128)S(1)} %get-tuple-element.362, f32[4,3456]{1,0:T(4,128)S(1)} %get-tuple-element.363, f32[4,128]{1,0:T(4,128)S(1)} %get-tuple-element.364, ...), kind=kLoop, calls=%fused_computation.49.clone.1 | loop fusion | flops 76085760 | bytes 577536 | tf_op jit(solution)/shard_map/while/body/eval_jaxpr/reduce_sum | solution.py:60
  (203 shorter events, 50.4 us)
Async XLA Ops:
  0.6 30.1 %copy-start.24 = (f32[3]{0:T(128)S(1)}, f32[3]{0:T(128)}, u32[]{:S(2)}) copy-start(f32[3]{0:T(128)} %constant.104.clone) | copy-start | bytes 40
  0.6 30.1 %copy-start.21 = (f32[3]{0:T(128)S(1)}, f32[3]{0:T(128)}, u32[]{:S(2)}) copy-start(f32[3]{0:T(128)} %constant.110.clone) | copy-start | bytes 40
  0.7 30.2 %copy-start.25 = (f32[3]{0:T(128)S(1)}, f32[3]{0:T(128)}, u32[]{:S(2)}) copy-start(f32[3]{0:T(128)} %constant.113.clone) | copy-start | bytes 40
  0.7 30.2 %copy-start.26 = (f32[3]{0:T(128)S(1)}, f32[3]{0:T(128)}, u32[]{:S(2)}) copy-start(f32[3]{0:T(128)} %constant.122.clone) | copy-start | bytes 40
  0.7 30.4 %copy-start.22 = (f32[3]{0:T(128)S(1)}, f32[3]{0:T(128)}, u32[]{:S(2)}) copy-start(f32[3]{0:T(128)} %constant.119.clone) | copy-start | bytes 40
  0.7 30.4 %copy-start.23 = (f32[3]{0:T(128)S(1)}, f32[3]{0:T(128)}, u32[]{:S(2)}) copy-start(f32[3]{0:T(128)} %constant.128.clone) | copy-start | bytes 40
  0.7 30.1 %copy-start.2 = (f32[3,4,4,2,128]{4,3,2,1,0:T(2,128)S(1)}, f32[3,4,4,2,128]{4,3,2,1,0:T(2,128)}, u32[]{:S(2)}) copy-start(f32[3,4,4,2,128]{4,3,2,1,0:T(2,128)} %param.63) | copy-start | bytes 147460
  0.7 30.1 %copy-start.1 = (f32[3,4,4,2,128]{4,3,2,1,0:T(2,128)S(1)}, f32[3,4,4,2,128]{4,3,2,1,0:T(2,128)}, u32[]{:S(2)}) copy-start(f32[3,4,4,2,128]{4,3,2,1,0:T(2,128)} %param.64) | copy-start | bytes 147460
  0.7 30.1 %copy-start = (f32[3,4,4,2,128]{4,3,2,1,0:T(2,128)S(1)}, f32[3,4,4,2,128]{4,3,2,1,0:T(2,128)}, u32[]{:S(2)}) copy-start(f32[3,4,4,2,128]{4,3,2,1,0:T(2,128)} %param.65) | copy-start | bytes 147460
  2.6 5.9 %collective-permute-start = (f32[10,1,4,2,128]{4,3,2,1,0:T(2,128)S(1)}, f32[10,1,4,2,128]{4,3,2,1,0:T(2,128)S(1)}, u32[]{:S(2)}, u32[]{:S(2)}) collective-permute-start(f32[10,1,4,2,128]{4,3,2,1,0:T(2,128)S(1)} %get-tuple-element.210), channel_id=1, source_target_pairs={{0,32},{32,64},{64,96},{96,128},{128,160},{160,192},{192,224},{224... | collective-permute-start | bytes 122888 | tf_op jit(solution)/shard_map/ppermute | solution.py:30
  2.7 5.8 %collective-permute-start.1 = (f32[10,1,4,2,128]{4,3,2,1,0:T(2,128)S(1)}, f32[10,1,4,2,128]{4,3,2,1,0:T(2,128)S(1)}, u32[]{:S(2)}, u32[]{:S(2)}) collective-permute-start(f32[10,1,4,2,128]{4,3,2,1,0:T(2,128)S(1)} %get-tuple-element.211), channel_id=1, source_target_pairs={{32,0},{64,32},{96,64},{128,96},{160,128},{192,160},{224,192},{0,2... | collective-permute-start | bytes 122888 | tf_op jit(solution)/shard_map/ppermute | solution.py:33
  9.4 9.3 %collective-permute-start.2 = (f32[10,6,1,2,128]{4,3,2,1,0:T(2,128)S(1)}, f32[10,6,1,2,128]{4,3,2,1,0:T(2,128)S(1)}, u32[]{:S(2)}, u32[]{:S(2)}) collective-permute-start(f32[10,6,1,2,128]{4,3,2,1,0:T(2,128)S(1)} %get-tuple-element.188), channel_id=1, source_target_pairs={{0,4},{4,8},{8,12},{12,16},{16,20},{20,24},{24,28},{28,0},{1,5},{5... | collective-permute-start | bytes 184328 | tf_op jit(solution)/shard_map/ppermute | solution.py:30
  16.2 8.5 %collective-permute-start.3 = (f32[10,6,1,2,128]{4,3,2,1,0:T(2,128)S(1)}, f32[10,6,1,2,128]{4,3,2,1,0:T(2,128)S(1)}, u32[]{:S(2)}, u32[]{:S(2)}) collective-permute-start(f32[10,6,1,2,128]{4,3,2,1,0:T(2,128)S(1)} %get-tuple-element.189), channel_id=1, source_target_pairs={{4,0},{8,4},{12,8},{16,12},{20,16},{24,20},{28,24},{0,28},{5,1},{9... | collective-permute-start | bytes 184328 | tf_op jit(solution)/shard_map/ppermute | solution.py:33
  26.0 6.8 %collective-permute-start.4 = (f32[10,6,6,1,128]{4,3,2,1,0:T(1,128)S(1)}, f32[10,6,6,1,128]{4,3,2,1,0:T(1,128)S(1)}, u32[]{:S(2)}, u32[]{:S(2)}) collective-permute-start(f32[10,6,6,1,128]{4,3,2,1,0:T(1,128)S(1)} %get-tuple-element.173), channel_id=1, source_target_pairs={{0,1},{1,2},{2,3},{3,0},{4,5},{5,6},{6,7},{7,4},{8,9},{9,10},{10,1... | collective-permute-start | bytes 552968 | tf_op jit(solution)/shard_map/ppermute | solution.py:30
  27.5 5.5 %collective-permute-start.5 = (f32[10,6,6,1,128]{4,3,2,1,0:T(1,128)S(1)}, f32[10,6,6,1,128]{4,3,2,1,0:T(1,128)S(1)}, u32[]{:S(2)}, u32[]{:S(2)}) collective-permute-start(f32[10,6,6,1,128]{4,3,2,1,0:T(1,128)S(1)} %get-tuple-element.172), channel_id=1, source_target_pairs={{1,0},{2,1},{3,2},{0,3},{5,4},{6,5},{7,6},{4,7},{9,8},{10,9},{11,1... | collective-permute-start | bytes 552968 | tf_op jit(solution)/shard_map/ppermute | solution.py:33
  30.5 4.8 %copy-start.13 = (f32[3]{0:T(128)S(1)}, f32[3]{0:T(128)}, u32[]{:S(2)}) copy-start(f32[3]{0:T(128)} %constant.106.clone) | copy-start | bytes 40
  30.5 4.8 %copy-start.14 = (f32[3]{0:T(128)S(1)}, f32[3]{0:T(128)}, u32[]{:S(2)}) copy-start(f32[3]{0:T(128)} %constant.109.clone) | copy-start | bytes 40
  30.5 4.8 %copy-start.15 = (f32[3]{0:T(128)S(1)}, f32[3]{0:T(128)}, u32[]{:S(2)}) copy-start(f32[3]{0:T(128)} %constant.112.clone) | copy-start | bytes 40
  30.5 4.8 %copy-start.16 = (f32[3]{0:T(128)S(1)}, f32[3]{0:T(128)}, u32[]{:S(2)}) copy-start(f32[3]{0:T(128)} %constant.115.clone) | copy-start | bytes 40
  30.5 4.8 %copy-start.17 = (f32[3]{0:T(128)S(1)}, f32[3]{0:T(128)}, u32[]{:S(2)}) copy-start(f32[3]{0:T(128)} %constant.118.clone) | copy-start | bytes 40
  30.5 4.8 %copy-start.18 = (f32[3]{0:T(128)S(1)}, f32[3]{0:T(128)}, u32[]{:S(2)}) copy-start(f32[3]{0:T(128)} %constant.121.clone) | copy-start | bytes 40
  30.5 4.8 %copy-start.19 = (f32[3]{0:T(128)S(1)}, f32[3]{0:T(128)}, u32[]{:S(2)}) copy-start(f32[3]{0:T(128)} %constant.124.clone) | copy-start | bytes 40
  30.5 4.7 %copy-start.20 = (f32[3]{0:T(128)S(1)}, f32[3]{0:T(128)}, u32[]{:S(2)}) copy-start(f32[3]{0:T(128)} %constant.127.clone) | copy-start | bytes 40
  30.9 6.1 %copy-start.5 = (f32[3]{0:T(128)S(1)}, f32[3]{0:T(128)}, u32[]{:S(2)}) copy-start(f32[3]{0:T(128)} %constant.105.clone) | copy-start | bytes 40
  30.9 6.1 %copy-start.6 = (f32[3]{0:T(128)S(1)}, f32[3]{0:T(128)}, u32[]{:S(2)}) copy-start(f32[3]{0:T(128)} %constant.108.clone) | copy-start | bytes 40
  30.9 6.1 %copy-start.7 = (f32[3]{0:T(128)S(1)}, f32[3]{0:T(128)}, u32[]{:S(2)}) copy-start(f32[3]{0:T(128)} %constant.111.clone) | copy-start | bytes 40
  31.0 6.1 %copy-start.8 = (f32[3]{0:T(128)S(1)}, f32[3]{0:T(128)}, u32[]{:S(2)}) copy-start(f32[3]{0:T(128)} %constant.114.clone) | copy-start | bytes 40
  31.0 6.0 %copy-start.9 = (f32[3]{0:T(128)S(1)}, f32[3]{0:T(128)}, u32[]{:S(2)}) copy-start(f32[3]{0:T(128)} %constant.117.clone) | copy-start | bytes 40
  31.0 6.0 %copy-start.10 = (f32[3]{0:T(128)S(1)}, f32[3]{0:T(128)}, u32[]{:S(2)}) copy-start(f32[3]{0:T(128)} %constant.120.clone) | copy-start | bytes 40
  31.0 6.0 %copy-start.11 = (f32[3]{0:T(128)S(1)}, f32[3]{0:T(128)}, u32[]{:S(2)}) copy-start(f32[3]{0:T(128)} %constant.123.clone) | copy-start | bytes 40
  31.0 6.0 %copy-start.12 = (f32[3]{0:T(128)S(1)}, f32[3]{0:T(128)}, u32[]{:S(2)}) copy-start(f32[3]{0:T(128)} %constant.126.clone) | copy-start | bytes 40
  68.0 99.8 %copy-start.4 = (f32[4,4,2,128]{3,2,1,0:T(2,128)S(1)}, f32[4,4,2,128]{3,2,1,0:T(2,128)}, u32[]{:S(2)}) copy-start(f32[4,4,2,128]{3,2,1,0:T(2,128)} %param.66) | copy-start | bytes 49156
  68.0 157.6 %copy-start.27 = (f32[3]{0:T(128)S(1)}, f32[3]{0:T(128)}, u32[]{:S(2)}) copy-start(f32[3]{0:T(128)} %constant.107.clone) | copy-start | bytes 40
  68.0 157.6 %copy-start.28 = (f32[3]{0:T(128)S(1)}, f32[3]{0:T(128)}, u32[]{:S(2)}) copy-start(f32[3]{0:T(128)} %constant.125.clone) | copy-start | bytes 40
  213.5 5.0 %collective-permute-start.6 = (f32[3,1,4,2,128]{4,3,2,1,0:T(2,128)S(1)}, f32[3,1,4,2,128]{4,3,2,1,0:T(2,128)S(1)}, u32[]{:S(2)}, u32[]{:S(2)}) collective-permute-start(f32[3,1,4,2,128]{4,3,2,1,0:T(2,128)S(1)} %get-tuple-element.228), channel_id=1, source_target_pairs={{0,32},{32,64},{64,96},{96,128},{128,160},{160,192},{192,224},{224... | collective-permute-start | bytes 36872 | tf_op jit(solution)/shard_map/ppermute | solution.py:30
  213.5 4.9 %collective-permute-start.7 = (f32[3,1,4,2,128]{4,3,2,1,0:T(2,128)S(1)}, f32[3,1,4,2,128]{4,3,2,1,0:T(2,128)S(1)}, u32[]{:S(2)}, u32[]{:S(2)}) collective-permute-start(f32[3,1,4,2,128]{4,3,2,1,0:T(2,128)S(1)} %get-tuple-element.229), channel_id=1, source_target_pairs={{32,0},{64,32},{96,64},{128,96},{160,128},{192,160},{224,192},{0,2... | collective-permute-start | bytes 36872 | tf_op jit(solution)/shard_map/ppermute | solution.py:33
  218.5 8.9 %collective-permute-start.8 = (f32[3,6,1,2,128]{4,3,2,1,0:T(2,128)S(1)}, f32[3,6,1,2,128]{4,3,2,1,0:T(2,128)S(1)}, u32[]{:S(2)}, u32[]{:S(2)}) collective-permute-start(f32[3,6,1,2,128]{4,3,2,1,0:T(2,128)S(1)} %get-tuple-element.224), channel_id=1, source_target_pairs={{0,4},{4,8},{8,12},{12,16},{16,20},{20,24},{24,28},{28,0},{1,5},{5... | collective-permute-start | bytes 55304 | tf_op jit(solution)/shard_map/ppermute | solution.py:30
  221.4 7.7 %collective-permute-start.9 = (f32[3,6,1,2,128]{4,3,2,1,0:T(2,128)S(1)}, f32[3,6,1,2,128]{4,3,2,1,0:T(2,128)S(1)}, u32[]{:S(2)}, u32[]{:S(2)}) collective-permute-start(f32[3,6,1,2,128]{4,3,2,1,0:T(2,128)S(1)} %get-tuple-element.225), channel_id=1, source_target_pairs={{4,0},{8,4},{12,8},{16,12},{20,16},{24,20},{28,24},{0,28},{5,1},{9... | collective-permute-start | bytes 55304 | tf_op jit(solution)/shard_map/ppermute | solution.py:33
  229.4 5.4 %collective-permute-start.10 = (f32[3,6,6,1,128]{4,3,2,1,0:T(1,128)S(1)}, f32[3,6,6,1,128]{4,3,2,1,0:T(1,128)S(1)}, u32[]{:S(2)}, u32[]{:S(2)}) collective-permute-start(f32[3,6,6,1,128]{4,3,2,1,0:T(1,128)S(1)} %get-tuple-element.215), channel_id=1, source_target_pairs={{0,1},{1,2},{2,3},{3,0},{4,5},{5,6},{6,7},{7,4},{8,9},{9,10},{10,1... | collective-permute-start | bytes 165896 | tf_op jit(solution)/shard_map/ppermute | solution.py:30
  229.5 5.4 %collective-permute-start.11 = (f32[3,6,6,1,128]{4,3,2,1,0:T(1,128)S(1)}, f32[3,6,6,1,128]{4,3,2,1,0:T(1,128)S(1)}, u32[]{:S(2)}, u32[]{:S(2)}) collective-permute-start(f32[3,6,6,1,128]{4,3,2,1,0:T(1,128)S(1)} %get-tuple-element.214), channel_id=1, source_target_pairs={{1,0},{2,1},{3,2},{0,3},{5,4},{6,5},{7,6},{4,7},{9,8},{10,9},{11,1... | collective-permute-start | bytes 165896 | tf_op jit(solution)/shard_map/ppermute | solution.py:33
  367.6 0.7 copy-start.3
where the time goes:
time: 373 us; the launch traced here: 368 us
  other arithmetic  233 us (62%)
  blocking collectives  44.2 us (12%)
  local copies, waits for them, and re-layouts  43.5 us (12%)
  starting transfers between devices  28.5 us (8%)
  waiting for transfers between devices  16.6 us (4%)
    reduce_sum x16, other arithmetic, tile_force(): jnp.sum(weight * separate[k], axis=-1)  180 us
    pmax x5, blocking collectives, over_axes(): return functools.reduce(lax.pmax, axes, x)  44.2 us
    unnamed x52, other arithmetic  40.3 us
    reshape x4, local copies, waits for them, and re-layouts, local_forces(): sources.reshape(width, blocks, CELL_BLOCK, sources.shape[4])  22.8 us
    mul x16, local copies, waits for them, and re-layouts, inner_pairs(): left[k][..., :, None] * right[k][..., None, :]  17.9 us
    ppermute x6, starting transfers between devices, extended(): lax.ppermute(lax.slice_in_dim(block, 0, width, axis=dim), axis, backward)  17.1 us
    ppermute x6, starting transfers between devices, extended(): lax.ppermute(lax.slice_in_dim(block, block.shape[dim] - width, None, axis...  11.4 us
    ppermute x6, waiting for transfers between devices, extended(): lax.ppermute(lax.slice_in_dim(block, block.shape[dim] - width, None, axis...  8.66 us
  transfers between devices with their start and end apart: 12, of which 9 were waited for; matrix products, arithmetic and copies ran while one was open for 1% of the time, Pallas kernels for 0%

commit v1 on v0

v1 whole, which is shorter than its diff:
```python
import functools

import jax
import jax.numpy as jnp
from jax import lax
from jax.experimental import pallas as pl
from jax.experimental.pallas import tpu as pltpu
from jax.sharding import Mesh
from jax.sharding import PartitionSpec as P

GX = ("gx_0", "gx_1")
GY = ("gy_0", "gy_1")
EVERY = ("gx_0", "gx_1", "gy_0", "gy_1", "gz")

CORE_SQUARED = 0.25
MU_SCALE = 0.05
CROSS_WEIGHT = 0.5
STEP_LIMIT = 0.1

NX, NY, NZ, SLOTS = 4, 4, 2, 128
PX, PY, PZ = NX + 2, NY + 2, NZ + 2
CELLS = NX * NY * NZ
PADDED = PX * PY * PZ
KF = 32
VF = 40
VROWS = 128
F32 = jnp.float32
BF16 = jnp.bfloat16


def ring(axis):
    count = lax.axis_size(axis)
    forward = [(i, (i + 1) % count) for i in range(count)]
    return forward, [(t, s) for s, t in forward]


def extended(block, sides):
    for axis, dim in sides:
        forward, backward = ring(axis)
        size = block.shape[dim]
        low = lax.ppermute(lax.slice_in_dim(block, size - 1, size, axis=dim), axis, forward)
        high = lax.ppermute(lax.slice_in_dim(block, 0, 1, axis=dim), axis, backward)
        block = jnp.concatenate([low, block, high], axis=dim)
    return block


def parts3(v):
    high = v.astype(BF16).astype(F32)
    rest = v - high
    mid = rest.astype(BF16).astype(F32)
    return high, mid, rest - mid


def distance_features(coords, source):
    one = jnp.ones_like(coords[0])
    square = coords[0] * coords[0] + coords[1] * coords[1] + coords[2] * coords[2]
    rows = []
    for x in coords:
        h, m, l = parts3(x)
        if source:
            h, m, l = -2.0 * h, -2.0 * m, -2.0 * l
            rows += [h, h, m, m, h, l]
        else:
            rows += [h, m, h, m, l, h]
    if source:
        rows += [*parts3(square), one, one, one]
    else:
        rows += [one, one, one, *parts3(square + CORE_SQUARED)]
    return rows + [jnp.zeros_like(one)] * (KF - len(rows))


def prepare_sources(pad_ref, shift, pf, vf):
    sub = lax.broadcasted_iota(jnp.int32, (8, SLOTS), 0)
    y_in = (sub >> 2).astype(F32)
    z_in = (sub & 3).astype(F32)

    def group(g, carry):
        rows = pl.ds(pl.multiple_of(g * 8, 8), 8)
        x0 = (g // 3).astype(F32) - float(PX // 2)
        y0 = ((g % 3) * 2).astype(F32) - float(PY // 2)
        pos = [pad_ref[a, rows, :] for a in range(3)]
        if shift is not None:
            padv_ref, step = shift
            pos = [pos[a] + step * padv_ref[a, rows, :] for a in range(3)]
        coords = [pos[0] + x0, pos[1] + (y_in + y0), pos[2] + (z_in - float(PZ // 2))]
        for f, row in enumerate(distance_features(coords, True)):
            pf[pl.ds(g * (8 * KF) + f, 8, stride=KF), :] = row
        line = [pad_ref[3 + a, rows, :] for a in range(3)]
        live = pad_ref[9, rows, :]
        burg = [pad_ref[6 + a, rows, :] * live for a in range(3)]
        outer = [[burg[m] * line[n] for n in range(3)] for m in range(3)]
        for m in range(3):
            for n in range(3):
                b = outer[m][n] - CROSS_WEIGHT * outer[n][m]
                f = 3 * m + n
                vf[pl.ds(g * (8 * VF) + f, 8, stride=VF), :] = b
                for a in range(3):
                    at = g * (8 * VF) + 9 * (a + 1) + f
                    vf[pl.ds(at, 8, stride=VF), :] = b * coords[a]
        return carry

    lax.fori_loop(0, PADDED // 8, group, 0)


def lay_out_sources(pf, vf, pt, vt):
    def column(c, carry):
        at = pl.multiple_of(c * 128, 128)
        pt[pl.ds(at, 128), :] = pf[pl.ds(at, 128), :].T.astype(BF16)
        x, y = c // PY, c % PY
        lanes = pl.ds(pl.multiple_of(y * SLOTS, SLOTS), SLOTS)
        for z in range(PZ):
            v = vf[pl.ds(pl.multiple_of(c * (PZ * VF) + z * VF, 8), VF), :]
            rows = [*parts3(v), jnp.zeros((VROWS - 3 * VF, SLOTS), F32)]
            vt[x, z, :, lanes] = jnp.concatenate(rows, 0).astype(BF16)
        return carry

    lax.fori_loop(0, PX * PY, column, 0)


def prepare_targets(loc_ref, shift, qf):
    sub = lax.broadcasted_iota(jnp.int32, (8, SLOTS), 0)
    y_in = (sub >> 1).astype(F32)
    z_in = (sub & 1).astype(F32)
    every = []
    for g in range(CELLS // 8):
        rows = pl.ds(g * 8, 8)
        pos = [loc_ref[a, rows, :] for a in range(3)]
        if shift is not None:
            speed_ref, step = shift
            pos = [pos[a] + step * speed_ref[a, rows, :] for a in range(3)]
        coords = [
            pos[0] + float(g + 1 - PX // 2),
            pos[1] + (y_in + float(1 - PY // 2)),
            pos[2] + (z_in + float(1 - PZ // 2)),
        ]
        for f, row in enumerate(distance_features(coords, False)):
            qf[pl.ds(g * (8 * KF) + f, 8, stride=KF), :] = row
        every.append(coords)
    return every


def pair_sums(pt, vt, qf, tf):
    span = 3 * SLOTS
    diag = lax.broadcasted_iota(jnp.int32, (SLOTS, SLOTS), 0) == lax.broadcasted_iota(
        jnp.int32, (SLOTS, SLOTS), 1
    )
    zero = jnp.zeros((KF, 2 * SLOTS), BF16)
    half = jnp.zeros((KF, SLOTS), BF16)

    def split(s):
        inverse = lax.rsqrt(s)
        g = inverse * inverse * inverse
        return g

    def parts2(g):
        high = g.astype(BF16)
        return high, (g - high.astype(F32)).astype(BF16)

    def target(c, carry):
        x, y = c // NY, c % NY
        q0 = qf[pl.ds(pl.multiple_of(c * (2 * KF), 8), KF), :].astype(BF16)
        q1 = qf[pl.ds(pl.multiple_of(c * (2 * KF) + KF, 8), KF), :].astype(BF16)
        both = jnp.concatenate([q0, q1], 1)
        ends = [jnp.concatenate([q0, half], 1), jnp.concatenate([half, q1], 1)]
        weights = [
            jnp.concatenate([zero, both, zero, zero], 0),
            jnp.concatenate([zero, zero, both, zero], 0),
            jnp.concatenate([ends[0], zero, zero, ends[1]], 0),
        ]
        lanes = pl.ds(pl.multiple_of(y * SLOTS, SLOTS), span)
        total = jnp.zeros((VROWS, 2 * SLOTS), F32)
        for dx in range(3):
            rows = pl.ds(pl.multiple_of(((x + dx) * PY + y) * SLOTS, SLOTS), span)
            source = pt[rows, :]
            for tile in range(3):
                s = jnp.dot(source, weights[tile], preferred_element_type=F32)
                g = split(s)
                if dx == 1 and tile < 2:
                    mid = g[SLOTS : 2 * SLOTS]
                    own = jnp.where(diag, 0.0, mid[:, tile * SLOTS : (tile + 1) * SLOTS])
                    other = mid[:, (1 - tile) * SLOTS : (2 - tile) * SLOTS]
                    mid = jnp.concatenate([own, other] if tile == 0 else [other, own], 1)
                    g = jnp.concatenate([g[:SLOTS], mid, g[2 * SLOTS :]], 0)
                high, low = parts2(g)
                if tile < 2:
                    v = vt[x + dx, tile + 1, :, lanes]
                    total = total + jnp.dot(v, high, preferred_element_type=F32)
                    total = total + jnp.dot(v, low, preferred_element_type=F32)
                else:
                    ends_sum = []
                    for t in range(2):
                        v = vt[x + dx, 3 * t, :, lanes]
                        col = slice(t * SLOTS, (t + 1) * SLOTS)
                        ends_sum.append(
                            jnp.dot(v, high[:, col], preferred_element_type=F32)
                            + jnp.dot(v, low[:, col], preferred_element_type=F32)
                        )
                    total = total + jnp.concatenate(ends_sum, 1)
        sums = total[0:VF] + total[VF : 2 * VF] + total[2 * VF : 3 * VF]
        for t in range(2):
            at = pl.multiple_of(c * (2 * VF) + t * VF, 8)
            tf[pl.ds(at, VF), :] = sums[:, t * SLOTS : (t + 1) * SLOTS]
        return carry

    lax.fori_loop(0, NX * NY, target, 0)


def forces_of(g, coords, loc_ref, tf):
    rows = pl.ds(g * 8, 8)
    line = [loc_ref[3 + a, rows, :] for a in range(3)]
    burg = [loc_ref[6 + a, rows, :] for a in range(3)]
    live = loc_ref[9, rows, :]
    sums = [jnp.zeros((8, SLOTS), F32) for _ in range(4)]
    for m in range(3):
        for n in range(3):
            a = burg[m] * line[n]
            for k in range(4):
                at = g * (8 * VF) + 9 * k + 3 * m + n
                sums[k] = sums[k] + a * tf[pl.ds(at, 8, stride=VF), :]
    scale = MU_SCALE * live
    return [scale * (coords[k] * sums[0] - sums[k + 1]) for k in range(3)]


def start_kernel(pad_ref, loc_ref, mob_ref, speed_ref, peak_ref, pf, vf, pt, vt, qf, tf):
    prepare_sources(pad_ref, None, pf, vf)
    lay_out_sources(pf, vf, pt, vt)
    every = prepare_targets(loc_ref, None, qf)
    pair_sums(pt, vt, qf, tf)
    peak = jnp.zeros((8, SLOTS), F32)
    for g in range(CELLS // 8):
        rows = pl.ds(g * 8, 8)
        force = forces_of(g, every[g], loc_ref, tf)
        mobility = mob_ref[rows, :]
        speed = [mobility * f for f in force]
        for a in range(3):
            speed_ref[a, rows, :] = speed[a]
        peak = jnp.maximum(
            peak, speed[0] * speed[0] + speed[1] * speed[1] + speed[2] * speed[2]
        )
    top = jnp.max(jnp.max(peak, axis=0, keepdims=True), axis=1, keepdims=True)
    peak_ref[...] = jnp.broadcast_to(top, peak_ref.shape)


def end_kernel(
    pad_ref, loc_ref, mob_ref, padv_ref, speed_ref, peak_ref, moved_ref, force_ref,
    pf, vf, pt, vt, qf, tf,
):
    peak = jnp.max(jnp.max(peak_ref[...], axis=0, keepdims=True), axis=1, keepdims=True)
    step = STEP_LIMIT * lax.rsqrt(jnp.broadcast_to(peak, (8, SLOTS)) + 1e-12)
    prepare_sources(pad_ref, (padv_ref, step), pf, vf)
    lay_out_sources(pf, vf, pt, vt)
    every = prepare_targets(loc_ref, (speed_ref, step), qf)
    pair_sums(pt, vt, qf, tf)
    for g in range(CELLS // 8):
        rows = pl.ds(g * 8, 8)
        force = forces_of(g, every[g], loc_ref, tf)
        mobility = mob_ref[rows, :]
        for a in range(3):
            force_ref[a, rows, :] = force[a]
            moved_ref[a, rows, :] = loc_ref[a, rows, :] + 0.5 * step * (
                speed_ref[a, rows, :] + mobility * force[a]
            )


def call(kernel, out_shapes, operands, name):
    whole = pl.BlockSpec(memory_space=pltpu.VMEM)
    return pl.pallas_call(
        kernel,
        out_shape=out_shapes,
        in_specs=[whole] * len(operands),
        out_specs=[whole] * len(out_shapes),
        scratch_shapes=[
            pltpu.VMEM((PADDED * KF, SLOTS), F32),
            pltpu.VMEM((PADDED * VF, SLOTS), F32),
            pltpu.VMEM((PX * PY * SLOTS, 128), BF16),
            pltpu.VMEM((PX, PZ, VROWS, PY * SLOTS), BF16),
            pltpu.VMEM((CELLS * KF, SLOTS), F32),
            pltpu.VMEM((CELLS * VF, SLOTS), F32),
        ],
        compiler_params=pltpu.CompilerParams(vmem_limit_bytes=48 << 20),
        name=name,
    )(*operands)


def on_device(positions, line_vectors, burgers, mobility, occupancy):
    slots = lax.broadcasted_iota(jnp.int32, mobility.shape, 3)
    live = (slots < occupancy[..., None]).astype(F32)
    fields = jnp.concatenate([positions, line_vectors, burgers, live[None]], 0)
    sides = ((GX, 1), (GY, 2), ("gz", 3))
    pad = extended(fields, sides).reshape(10, PADDED, SLOTS)
    loc = fields.reshape(10, CELLS, SLOTS)
    mob = mobility.reshape(CELLS, SLOTS)
    devices = lax.axis_size(EVERY)
    vec = jax.ShapeDtypeStruct((3, CELLS, SLOTS), F32)
    speed, peaks = call(
        start_kernel,
        [vec, jax.ShapeDtypeStruct((devices, SLOTS), F32)],
        [pad, loc, mob],
        "start_forces",
    )
    peaks = lax.all_to_all(peaks.reshape(devices, 1, SLOTS), EVERY, 0, 0)
    peaks = peaks.reshape(devices, SLOTS)
    padv = extended(speed.reshape(3, NX, NY, NZ, SLOTS), sides).reshape(3, PADDED, SLOTS)
    moved, force = call(
        end_kernel, [vec, vec], [pad, loc, mob, padv, speed, peaks], "end_forces"
    )
    shape = (3, NX, NY, NZ, SLOTS)
    return moved.reshape(shape), force.reshape(shape)


def solution(mesh):
    finer = Mesh(
        mesh.devices.reshape(4, 2, 4, 2, mesh.shape["gz"]), ("gx_0", "gx_1", "gy_0", "gy_1", "gz")
    )
    in_specs = (
        P(None, GX, GY, "gz", None),
        P(None, GX, GY, "gz", None),
        P(None, GX, GY, "gz", None),
        P(GX, GY, "gz", None),
        P(GX, GY, "gz"),
    )
    out_specs = (P(None, GX, GY, "gz", None), P(None, GX, GY, "gz", None))
    return jax.shard_map(
        on_device, mesh=finer, in_specs=in_specs, out_specs=out_specs, check_vma=False
    )
```

time: 373 us -> 154 us (0.41)
  other arithmetic: 233 us -> 2 us
  Pallas kernels: 0 us -> 86.4 us
  blocking collectives: 44.2 us -> 0 us
  local copies, waits for them, and re-layouts: 43.5 us -> 1.28 us
  starting transfers between devices: 28.5 us -> 38.2 us
  waiting for transfers between devices: 16.6 us -> 23.6 us
    reduce_sum x17 -> x0, other arithmetic: 180 us -> none  [the longest x16 180 us: tile_force(): jnp.sum(weight * separate[k], axis=-1)]
    pallas_call x0 -> x2, Pallas kernels: none -> 86.4 us  [call(): pl.pallas_call(kernel, out_shape=out_shapes, in_specs=[whole] * len(opera...]
    pmax x5 -> x0, blocking collectives: 44.2 us -> none  [over_axes(): return functools.reduce(lax.pmax, axes, x)]
    unnamed x52 -> x0, other arithmetic: 40.3 us -> none
    reshape x4 -> x0, local copies, waits for them, and re-layouts: 22.8 us -> none  [local_forces(): sources.reshape(width, blocks, CELL_BLOCK, sources.shape[4])]
    mul x16 -> x0, local copies, waits for them, and re-layouts: 17.9 us -> none  [inner_pairs(): left[k][..., :, None] * right[k][..., None, :]]
    all_to_all x0 -> x1, starting transfers between devices: none -> 10 us  [on_device(): peaks = lax.all_to_all(peaks.reshape(devices, 1, SLOTS), EVERY, 0, 0)]
    all_to_all x0 -> x1, waiting for transfers between devices: none -> 5.89 us  [on_device(): peaks = lax.all_to_all(peaks.reshape(devices, 1, SLOTS), EVERY, 0, 0)]
  transfers between devices with their start and end apart: 12 -> 13, of which waited for: 9 -> 9; matrix products, arithmetic and copies ran while one was open for 1% -> 0% of each run, Pallas kernels for 0% -> 0%
where the time goes in v1:
time: 154 us; the launch traced here: 152 us
  Pallas kernels  86.4 us (56%)
  starting transfers between devices  38.2 us (25%)
  waiting for transfers between devices  23.6 us (15%)
  other arithmetic  2 us (1%)
    pallas_call x2, Pallas kernels, call(): pl.pallas_call(kernel, out_shape=out_shapes, in_specs=[whole] * len(opera...  86.4 us
    ppermute x6, starting transfers between devices, extended(): high = lax.ppermute(lax.slice_in_dim(block, 0, 1, axis=dim), axis, backward)  16.3 us
    ppermute x6, starting transfers between devices, extended(): lax.ppermute(lax.slice_in_dim(block, size - 1, size, axis=dim), axis, for...  11.9 us
    ppermute x6, waiting for transfers between devices, extended(): lax.ppermute(lax.slice_in_dim(block, size - 1, size, axis=dim), axis, for...  11.1 us
    all_to_all x1, starting transfers between devices, on_device(): peaks = lax.all_to_all(peaks.reshape(devices, 1, SLOTS), EVERY, 0, 0)  10 us
    ppermute x6, waiting for transfers between devices, extended(): high = lax.ppermute(lax.slice_in_dim(block, 0, 1, axis=dim), axis, backward)  6.62 us
    all_to_all x1, waiting for transfers between devices, on_device(): peaks = lax.all_to_all(peaks.reshape(devices, 1, SLOTS), EVERY, 0, 0)  5.89 us
  transfers between devices with their start and end apart: 13, of which 9 were waited for; matrix products, arithmetic and copies ran while one was open for 0% of the time, Pallas kernels for 0%

profile of v1, /device:TPU:8, one launch (start us, length us, event | category | flops | bytes accessed | tf_op | source)
XLA Modules:
  0.0 152.3 jit_solution(18436083857309899139)
XLA Ops:
  0.6 0.8 copy.11
  1.4 0.1 compare_convert_fusion
  1.5 0.0 copy-start.1
  1.5 0.0 copy-start.2
  1.5 0.0 copy-start.3
  1.5 0.9 pad_maximum_fusion.14
  2.4 0.1 collective-permute-start
  2.5 4.1 %collective-permute-start.1 = (f32[10,1,4,2,128]{4,3,2,1,0:T(2,128)S(1)}, f32[10,1,4,2,128]{4,3,2,1,0:T(2,128)S(1)}, u32[]{:S(2)}, u32[]{:S(2)}) collective-permute-start(f32[10,1,4,2,128]{4,3,2,1,0:T(2,128)S(1)} %get-tuple-element.15), channel_id=1, source_target_pairs={{32,0},{64,32},{96,64},{128,96},{160,128},{192,160},{224,192},{0,2... | collective-permute-start | bytes 122888 | tf_op jit(solution)/shard_map/ppermute | solution.py:42
  6.6 1.7 %collective-permute-done = f32[10,1,4,2,128]{4,3,2,1,0:T(2,128)S(1)} collective-permute-done((f32[10,1,4,2,128]{4,3,2,1,0:T(2,128)S(1)}, f32[10,1,4,2,128]{4,3,2,1,0:T(2,128)S(1)}, u32[]{:S(2)}, u32[]{:S(2)}) %collective-permute-start) | collective-permute-done | bytes 40992 | tf_op jit(solution)/shard_map/ppermute | solution.py:41
  8.4 0.0 collective-permute-done.1
  8.4 0.0 copy-done.1
  8.4 0.0 copy-done.2
  8.4 0.0 copy-done.3
  8.4 0.1 pad_maximum_fusion.10
  8.4 6.7 %collective-permute-start.2 = (f32[10,6,1,2,128]{4,3,2,1,0:T(2,128)S(1)}, f32[10,6,1,2,128]{4,3,2,1,0:T(2,128)S(1)}, u32[]{:S(2)}, u32[]{:S(2)}) collective-permute-start(f32[10,6,1,2,128]{4,3,2,1,0:T(2,128)S(1)} %get-tuple-element.12), channel_id=1, source_target_pairs={{0,4},{4,8},{8,12},{12,16},{16,20},{20,24},{24,28},{28,0},{1,5},{5... | collective-permute-start | bytes 184328 | tf_op jit(solution)/shard_map/ppermute | solution.py:41
  15.2 0.2 collective-permute-start.3
  15.4 0.1 lt.30
  15.4 2.3 %collective-permute-done.2 = f32[10,6,1,2,128]{4,3,2,1,0:T(2,128)S(1)} collective-permute-done((f32[10,6,1,2,128]{4,3,2,1,0:T(2,128)S(1)}, f32[10,6,1,2,128]{4,3,2,1,0:T(2,128)S(1)}, u32[]{:S(2)}, u32[]{:S(2)}) %collective-permute-start.2) | collective-permute-done | bytes 61472 | tf_op jit(solution)/shard_map/ppermute | solution.py:41
  17.8 5.9 %collective-permute-done.3 = f32[10,6,1,2,128]{4,3,2,1,0:T(2,128)S(1)} collective-permute-done((f32[10,6,1,2,128]{4,3,2,1,0:T(2,128)S(1)}, f32[10,6,1,2,128]{4,3,2,1,0:T(2,128)S(1)}, u32[]{:S(2)}, u32[]{:S(2)}) %collective-permute-start.3) | collective-permute-done | bytes 61472 | tf_op jit(solution)/shard_map/ppermute | solution.py:42
  23.7 0.2 pad_maximum_fusion.1
  23.8 0.3 fusion.1
  24.1 1.6 %collective-permute-start.4 = (f32[10,6,6,1,128]{4,3,2,1,0:T(1,128)S(1)}, f32[10,6,6,1,128]{4,3,2,1,0:T(1,128)S(1)}, u32[]{:S(2)}, u32[]{:S(2)}) collective-permute-start(f32[10,6,6,1,128]{4,3,2,1,0:T(1,128)S(1)} %get-tuple-element.10), channel_id=1, source_target_pairs={{0,1},{1,2},{2,3},{3,0},{4,5},{5,6},{6,7},{7,4},{8,9},{9,10},{10,1... | collective-permute-start | bytes 552968 | tf_op jit(solution)/shard_map/ppermute | solution.py:41
  25.7 1.7 %collective-permute-start.5 = (f32[10,6,6,1,128]{4,3,2,1,0:T(1,128)S(1)}, f32[10,6,6,1,128]{4,3,2,1,0:T(1,128)S(1)}, u32[]{:S(2)}, u32[]{:S(2)}) collective-permute-start(f32[10,6,6,1,128]{4,3,2,1,0:T(1,128)S(1)} %get-tuple-element.11), channel_id=1, source_target_pairs={{1,0},{2,1},{3,2},{0,3},{5,4},{6,5},{7,6},{4,7},{9,8},{10,9},{11,1... | collective-permute-start | bytes 552968 | tf_op jit(solution)/shard_map/ppermute | solution.py:42
  27.5 0.1 fusion
  27.5 0.0 copy-start
  27.6 3.4 %collective-permute-done.4 = f32[10,6,6,1,128]{4,3,2,1,0:T(1,128)S(1)} collective-permute-done((f32[10,6,6,1,128]{4,3,2,1,0:T(1,128)S(1)}, f32[10,6,6,1,128]{4,3,2,1,0:T(1,128)S(1)}, u32[]{:S(2)}, u32[]{:S(2)}) %collective-permute-start.4) | collective-permute-done | bytes 184352 | tf_op jit(solution)/shard_map/ppermute | solution.py:41
  31.0 0.3 collective-permute-done.5
  31.3 0.5 pad_maximum_fusion
  31.8 0.0 copy-done
  31.8 43.2 %start_forces.1 = (f32[3,32,128]{2,1,0:T(8,128)S(1)}, f32[256,128]{1,0:T(8,128)}) custom-call(f32[10,144,128]{2,1,0:T(8,128)S(1)} %bitcast.13, f32[10,32,128]{2,1,0:T(8,128)S(1)} %pad_maximum_fusion.3.loc_ref, f32[32,128]{1,0:T(8,128)S(1)} %bitcast.21), custom_call_target="tpu_custom_call" | custom-call | tf_op jit(solution)/shard_map/start_forces/pallas_call | solution.py:267
  74.9 0.0 collective-permute-start.6
  74.9 3.5 %collective-permute-start.7 = (f32[3,1,4,2,128]{4,3,2,1,0:T(2,128)S(1)}, f32[3,1,4,2,128]{4,3,2,1,0:T(2,128)S(1)}, u32[]{:S(2)}, u32[]{:S(2)}) collective-permute-start(f32[3,1,4,2,128]{4,3,2,1,0:T(2,128)S(1)} %get-tuple-element.21), channel_id=1, source_target_pairs={{32,0},{64,32},{96,64},{128,96},{160,128},{192,160},{224,192},{0,2... | collective-permute-start | bytes 36872 | tf_op jit(solution)/shard_map/ppermute | solution.py:42
  78.5 1.4 collective-permute-done.6
  79.9 0.0 collective-permute-done.7
  79.9 2.0 %collective-permute-start.8 = (f32[3,6,1,2,128]{4,3,2,1,0:T(2,128)S(1)}, f32[3,6,1,2,128]{4,3,2,1,0:T(2,128)S(1)}, u32[]{:S(2)}, u32[]{:S(2)}) collective-permute-start(f32[3,6,1,2,128]{4,3,2,1,0:T(2,128)S(1)} %get-tuple-element.18), channel_id=1, source_target_pairs={{0,4},{4,8},{8,12},{12,16},{16,20},{20,24},{24,28},{28,0},{1,5},{5... | collective-permute-start | bytes 55304 | tf_op jit(solution)/shard_map/ppermute | solution.py:41
  81.9 5.0 %collective-permute-start.9 = (f32[3,6,1,2,128]{4,3,2,1,0:T(2,128)S(1)}, f32[3,6,1,2,128]{4,3,2,1,0:T(2,128)S(1)}, u32[]{:S(2)}, u32[]{:S(2)}) collective-permute-start(f32[3,6,1,2,128]{4,3,2,1,0:T(2,128)S(1)} %get-tuple-element.19), channel_id=1, source_target_pairs={{4,0},{8,4},{12,8},{16,12},{20,16},{24,20},{28,24},{0,28},{5,1},{9... | collective-permute-start | bytes 55304 | tf_op jit(solution)/shard_map/ppermute | solution.py:42
  86.8 10.0 %all-to-all-start = ((f32[256,1,128]{2,1,0:T(1,128)}), f32[256,1,128]{2,1,0:T(1,128)S(1)}, u32[]{:S(2)}, u32[]{:S(2)}) async-start(f32[256,1,128]{2,1,0:T(1,128)} %bitcast.8), calls=%async_computation | async-start | bytes 262144 | tf_op jit(solution)/shard_map/all_to_all | solution.py:301
  96.9 0.0 collective-permute-done.8
  96.9 0.0 collective-permute-done.9
  96.9 0.1 pad_maximum_fusion.4
  96.9 0.1 fusion.2
  97.0 1.5 %collective-permute-start.10 = (f32[3,6,6,1,128]{4,3,2,1,0:T(1,128)S(1)}, f32[3,6,6,1,128]{4,3,2,1,0:T(1,128)S(1)}, u32[]{:S(2)}, u32[]{:S(2)}) collective-permute-start(f32[3,6,6,1,128]{4,3,2,1,0:T(1,128)S(1)} %get-tuple-element.16), channel_id=1, source_target_pairs={{0,1},{1,2},{2,3},{3,0},{4,5},{5,6},{6,7},{7,4},{8,9},{9,10},{10,1... | collective-permute-start | bytes 165896 | tf_op jit(solution)/shard_map/ppermute | solution.py:41
  98.6 1.8 %collective-permute-start.11 = (f32[3,6,6,1,128]{4,3,2,1,0:T(1,128)S(1)}, f32[3,6,6,1,128]{4,3,2,1,0:T(1,128)S(1)}, u32[]{:S(2)}, u32[]{:S(2)}) collective-permute-start(f32[3,6,6,1,128]{4,3,2,1,0:T(1,128)S(1)} %get-tuple-element.17), channel_id=1, source_target_pairs={{1,0},{2,1},{3,2},{0,3},{5,4},{6,5},{7,6},{4,7},{9,8},{10,9},{11,1... | collective-permute-start | bytes 165896 | tf_op jit(solution)/shard_map/ppermute | solution.py:42
  100.3 2.2 %collective-permute-done.10 = f32[3,6,6,1,128]{4,3,2,1,0:T(1,128)S(1)} collective-permute-done((f32[3,6,6,1,128]{4,3,2,1,0:T(1,128)S(1)}, f32[3,6,6,1,128]{4,3,2,1,0:T(1,128)S(1)}, u32[]{:S(2)}, u32[]{:S(2)}) %collective-permute-start.10) | collective-permute-done | bytes 55328 | tf_op jit(solution)/shard_map/ppermute | solution.py:41
  102.6 0.4 collective-permute-done.11
  103.0 0.2 pad_maximum_fusion.2
  103.1 5.9 %all-to-all-done = f32[256,1,128]{2,1,0:T(1,128)S(1)} async-done(((f32[256,1,128]{2,1,0:T(1,128)}), f32[256,1,128]{2,1,0:T(1,128)S(1)}, u32[]{:S(2)}, u32[]{:S(2)}) %all-to-all-start) | async-done | bytes 131104 | tf_op jit(solution)/shard_map/all_to_all | solution.py:301
  109.0 43.2 %end_forces.1 = (f32[3,32,128]{2,1,0:T(8,128)}, f32[3,32,128]{2,1,0:T(8,128)}) custom-call(f32[10,144,128]{2,1,0:T(8,128)S(1)} %bitcast.14, f32[10,32,128]{2,1,0:T(8,128)S(1)} %pad_maximum_fusion.3.loc_ref, f32[32,128]{1,0:T(8,128)S(1)} %bitcast.22, f32[3,144,128]{2,1,0:T(8,128)S(1)} %bitcast.19, f32[3,32,128]{2,1,0:T(8,128)S(1)} %get-tuple-element.6.speed_ref, ...), custom_call_target="tpu_custom_call" | custom-call | tf_op jit(solution)/shard_map/end_forces/pallas_call | solution.py:267
  (3 shorter events, 0.0 us)
Async XLA Ops:
  1.5 6.8 %copy-start.1 = (f32[3,4,4,2,128]{4,3,2,1,0:T(2,128)S(1)}, f32[3,4,4,2,128]{4,3,2,1,0:T(2,128)}, u32[]{:S(2)}) copy-start(f32[3,4,4,2,128]{4,3,2,1,0:T(2,128)} %param.7) | copy-start | bytes 147460
  1.5 6.8 %copy-start.2 = (f32[3,4,4,2,128]{4,3,2,1,0:T(2,128)S(1)}, f32[3,4,4,2,128]{4,3,2,1,0:T(2,128)}, u32[]{:S(2)}) copy-start(f32[3,4,4,2,128]{4,3,2,1,0:T(2,128)} %param.6) | copy-start | bytes 147460
  1.5 6.8 %copy-start.3 = (f32[3,4,4,2,128]{4,3,2,1,0:T(2,128)S(1)}, f32[3,4,4,2,128]{4,3,2,1,0:T(2,128)}, u32[]{:S(2)}) copy-start(f32[3,4,4,2,128]{4,3,2,1,0:T(2,128)} %param.5) | copy-start | bytes 147460
  2.4 5.9 %collective-permute-start = (f32[10,1,4,2,128]{4,3,2,1,0:T(2,128)S(1)}, f32[10,1,4,2,128]{4,3,2,1,0:T(2,128)S(1)}, u32[]{:S(2)}, u32[]{:S(2)}) collective-permute-start(f32[10,1,4,2,128]{4,3,2,1,0:T(2,128)S(1)} %get-tuple-element.14), channel_id=1, source_target_pairs={{0,32},{32,64},{64,96},{96,128},{128,160},{160,192},{192,224},{224... | collective-permute-start | bytes 122888 | tf_op jit(solution)/shard_map/ppermute | solution.py:41
  2.5 5.8 %collective-permute-start.1 = (f32[10,1,4,2,128]{4,3,2,1,0:T(2,128)S(1)}, f32[10,1,4,2,128]{4,3,2,1,0:T(2,128)S(1)}, u32[]{:S(2)}, u32[]{:S(2)}) collective-permute-start(f32[10,1,4,2,128]{4,3,2,1,0:T(2,128)S(1)} %get-tuple-element.15), channel_id=1, source_target_pairs={{32,0},{64,32},{96,64},{128,96},{160,128},{192,160},{224,192},{0,2... | collective-permute-start | bytes 122888 | tf_op jit(solution)/shard_map/ppermute | solution.py:42
  8.4 9.3 %collective-permute-start.2 = (f32[10,6,1,2,128]{4,3,2,1,0:T(2,128)S(1)}, f32[10,6,1,2,128]{4,3,2,1,0:T(2,128)S(1)}, u32[]{:S(2)}, u32[]{:S(2)}) collective-permute-start(f32[10,6,1,2,128]{4,3,2,1,0:T(2,128)S(1)} %get-tuple-element.12), channel_id=1, source_target_pairs={{0,4},{4,8},{8,12},{12,16},{16,20},{20,24},{24,28},{28,0},{1,5},{5... | collective-permute-start | bytes 184328 | tf_op jit(solution)/shard_map/ppermute | solution.py:41
  15.2 8.5 %collective-permute-start.3 = (f32[10,6,1,2,128]{4,3,2,1,0:T(2,128)S(1)}, f32[10,6,1,2,128]{4,3,2,1,0:T(2,128)S(1)}, u32[]{:S(2)}, u32[]{:S(2)}) collective-permute-start(f32[10,6,1,2,128]{4,3,2,1,0:T(2,128)S(1)} %get-tuple-element.13), channel_id=1, source_target_pairs={{4,0},{8,4},{12,8},{16,12},{20,16},{24,20},{28,24},{0,28},{5,1},{9... | collective-permute-start | bytes 184328 | tf_op jit(solution)/shard_map/ppermute | solution.py:42
  24.1 6.8 %collective-permute-start.4 = (f32[10,6,6,1,128]{4,3,2,1,0:T(1,128)S(1)}, f32[10,6,6,1,128]{4,3,2,1,0:T(1,128)S(1)}, u32[]{:S(2)}, u32[]{:S(2)}) collective-permute-start(f32[10,6,6,1,128]{4,3,2,1,0:T(1,128)S(1)} %get-tuple-element.10), channel_id=1, source_target_pairs={{0,1},{1,2},{2,3},{3,0},{4,5},{5,6},{6,7},{7,4},{8,9},{9,10},{10,1... | collective-permute-start | bytes 552968 | tf_op jit(solution)/shard_map/ppermute | solution.py:41
  25.7 5.5 %collective-permute-start.5 = (f32[10,6,6,1,128]{4,3,2,1,0:T(1,128)S(1)}, f32[10,6,6,1,128]{4,3,2,1,0:T(1,128)S(1)}, u32[]{:S(2)}, u32[]{:S(2)}) collective-permute-start(f32[10,6,6,1,128]{4,3,2,1,0:T(1,128)S(1)} %get-tuple-element.11), channel_id=1, source_target_pairs={{1,0},{2,1},{3,2},{0,3},{5,4},{6,5},{7,6},{4,7},{9,8},{10,9},{11,1... | collective-permute-start | bytes 552968 | tf_op jit(solution)/shard_map/ppermute | solution.py:42
  27.5 4.2 %copy-start = (f32[4,4,2,128]{3,2,1,0:T(2,128)S(1)}, f32[4,4,2,128]{3,2,1,0:T(2,128)}, u32[]{:S(2)}) copy-start(f32[4,4,2,128]{3,2,1,0:T(2,128)} %param.8) | copy-start | bytes 49156
  74.9 4.9 %collective-permute-start.6 = (f32[3,1,4,2,128]{4,3,2,1,0:T(2,128)S(1)}, f32[3,1,4,2,128]{4,3,2,1,0:T(2,128)S(1)}, u32[]{:S(2)}, u32[]{:S(2)}) collective-permute-start(f32[3,1,4,2,128]{4,3,2,1,0:T(2,128)S(1)} %get-tuple-element.20), channel_id=1, source_target_pairs={{0,32},{32,64},{64,96},{96,128},{128,160},{160,192},{192,224},{224... | collective-permute-start | bytes 36872 | tf_op jit(solution)/shard_map/ppermute | solution.py:41
  74.9 4.9 %collective-permute-start.7 = (f32[3,1,4,2,128]{4,3,2,1,0:T(2,128)S(1)}, f32[3,1,4,2,128]{4,3,2,1,0:T(2,128)S(1)}, u32[]{:S(2)}, u32[]{:S(2)}) collective-permute-start(f32[3,1,4,2,128]{4,3,2,1,0:T(2,128)S(1)} %get-tuple-element.21), channel_id=1, source_target_pairs={{32,0},{64,32},{96,64},{128,96},{160,128},{192,160},{224,192},{0,2... | collective-permute-start | bytes 36872 | tf_op jit(solution)/shard_map/ppermute | solution.py:42
  79.9 17.0 %collective-permute-start.8 = (f32[3,6,1,2,128]{4,3,2,1,0:T(2,128)S(1)}, f32[3,6,1,2,128]{4,3,2,1,0:T(2,128)S(1)}, u32[]{:S(2)}, u32[]{:S(2)}) collective-permute-start(f32[3,6,1,2,128]{4,3,2,1,0:T(2,128)S(1)} %get-tuple-element.18), channel_id=1, source_target_pairs={{0,4},{4,8},{8,12},{12,16},{16,20},{20,24},{24,28},{28,0},{1,5},{5... | collective-permute-start | bytes 55304 | tf_op jit(solution)/shard_map/ppermute | solution.py:41
  81.9 15.0 %collective-permute-start.9 = (f32[3,6,1,2,128]{4,3,2,1,0:T(2,128)S(1)}, f32[3,6,1,2,128]{4,3,2,1,0:T(2,128)S(1)}, u32[]{:S(2)}, u32[]{:S(2)}) collective-permute-start(f32[3,6,1,2,128]{4,3,2,1,0:T(2,128)S(1)} %get-tuple-element.19), channel_id=1, source_target_pairs={{4,0},{8,4},{12,8},{16,12},{20,16},{24,20},{28,24},{0,28},{5,1},{9... | collective-permute-start | bytes 55304 | tf_op jit(solution)/shard_map/ppermute | solution.py:42
  86.8 22.2 %all-to-all-start = ((f32[256,1,128]{2,1,0:T(1,128)}), f32[256,1,128]{2,1,0:T(1,128)S(1)}, u32[]{:S(2)}, u32[]{:S(2)}) async-start(f32[256,1,128]{2,1,0:T(1,128)} %bitcast.8), calls=%async_computation | async-start | bytes 262144 | tf_op jit(solution)/shard_map/all_to_all | solution.py:301
  97.0 5.5 %collective-permute-start.10 = (f32[3,6,6,1,128]{4,3,2,1,0:T(1,128)S(1)}, f32[3,6,6,1,128]{4,3,2,1,0:T(1,128)S(1)}, u32[]{:S(2)}, u32[]{:S(2)}) collective-permute-start(f32[3,6,6,1,128]{4,3,2,1,0:T(1,128)S(1)} %get-tuple-element.16), channel_id=1, source_target_pairs={{0,1},{1,2},{2,3},{3,0},{4,5},{5,6},{6,7},{7,4},{8,9},{9,10},{10,1... | collective-permute-start | bytes 165896 | tf_op jit(solution)/shard_map/ppermute | solution.py:41
  98.6 4.4 %collective-permute-start.11 = (f32[3,6,6,1,128]{4,3,2,1,0:T(1,128)S(1)}, f32[3,6,6,1,128]{4,3,2,1,0:T(1,128)S(1)}, u32[]{:S(2)}, u32[]{:S(2)}) collective-permute-start(f32[3,6,6,1,128]{4,3,2,1,0:T(1,128)S(1)} %get-tuple-element.17), channel_id=1, source_target_pairs={{1,0},{2,1},{3,2},{0,3},{5,4},{6,5},{7,6},{4,7},{9,8},{10,9},{11,1... | collective-permute-start | bytes 165896 | tf_op jit(solution)/shard_map/ppermute | solution.py:42

commit v2 on v1

--- a/solution.py
+++ b/solution.py
@@ -21,8 +21,10 @@
 PX, PY, PZ = NX + 2, NY + 2, NZ + 2
 CELLS = NX * NY * NZ
 PADDED = PX * PY * PZ
+UNROLL_L, UNROLL_P = 6, 1
 KF = 32
 VF = 40
+FAR = 3e38
 VROWS = 128
 F32 = jnp.float32
 BF16 = jnp.bfloat16
@@ -86,8 +88,7 @@
         for f, row in enumerate(distance_features(coords, True)):
             pf[pl.ds(g * (8 * KF) + f, 8, stride=KF), :] = row
         line = [pad_ref[3 + a, rows, :] for a in range(3)]
-        live = pad_ref[9, rows, :]
-        burg = [pad_ref[6 + a, rows, :] * live for a in range(3)]
+        burg = [pad_ref[6 + a, rows, :] for a in range(3)]
         outer = [[burg[m] * line[n] for n in range(3)] for m in range(3)]
         for m in range(3):
             for n in range(3):
@@ -99,7 +100,7 @@
                     vf[pl.ds(at, 8, stride=VF), :] = b * coords[a]
         return carry
 
-    lax.fori_loop(0, PADDED // 8, group, 0)
+    lax.fori_loop(0, PADDED // 8, group, 0, unroll=UNROLL_P)
 
 
 def lay_out_sources(pf, vf, pt, vt):
@@ -114,7 +115,7 @@
             vt[x, z, :, lanes] = jnp.concatenate(rows, 0).astype(BF16)
         return carry
 
-    lax.fori_loop(0, PX * PY, column, 0)
+    lax.fori_loop(0, PX * PY, column, 0, unroll=UNROLL_L)
 
 
 def prepare_targets(loc_ref, shift, qf):
@@ -139,77 +140,125 @@
     return every
 
 
+def parts2(s):
+    inverse = lax.rsqrt(s)
+    g = inverse * inverse * inverse
+    high = g.astype(BF16)
+    return high, (g - high.astype(F32)).astype(BF16)
+
+
+def without_self(s):
+    same = lax.broadcasted_iota(jnp.int32, s.shape, 0) == lax.broadcasted_iota(
+        jnp.int32, s.shape, 1
+    )
+    return jnp.where(same, FAR, s)
+
+
 def pair_sums(pt, vt, qf, tf):
-    span = 3 * SLOTS
-    diag = lax.broadcasted_iota(jnp.int32, (SLOTS, SLOTS), 0) == lax.broadcasted_iota(
-        jnp.int32, (SLOTS, SLOTS), 1
-    )
     zero = jnp.zeros((KF, 2 * SLOTS), BF16)
-    half = jnp.zeros((KF, SLOTS), BF16)
-
-    def split(s):
-        inverse = lax.rsqrt(s)
-        g = inverse * inverse * inverse
-        return g
-
-    def parts2(g):
-        high = g.astype(BF16)
-        return high, (g - high.astype(F32)).astype(BF16)
+    block = jnp.zeros((SLOTS, SLOTS), BF16)
 
     def target(c, carry):
-        x, y = c // NY, c % NY
-        q0 = qf[pl.ds(pl.multiple_of(c * (2 * KF), 8), KF), :].astype(BF16)
-        q1 = qf[pl.ds(pl.multiple_of(c * (2 * KF) + KF, 8), KF), :].astype(BF16)
-        both = jnp.concatenate([q0, q1], 1)
-        ends = [jnp.concatenate([q0, half], 1), jnp.concatenate([half, q1], 1)]
-        weights = [
-            jnp.concatenate([zero, both, zero, zero], 0),
-            jnp.concatenate([zero, zero, both, zero], 0),
-            jnp.concatenate([ends[0], zero, zero, ends[1]], 0),
-        ]
-        lanes = pl.ds(pl.multiple_of(y * SLOTS, SLOTS), span)
-        total = jnp.zeros((VROWS, 2 * SLOTS), F32)
+        x, y = c // (NY // 2), (c % (NY // 2)) * 2
+
+        def query(col, t):
+            at = pl.multiple_of(c * (4 * KF) + (2 * col + t) * KF, 8)
+            return qf[pl.ds(at, KF), :].astype(BF16)
+
+        def weights(s, left, right):
+            rows = [zero] * PZ
+            rows[s] = jnp.concatenate([left, right], 1)
+            return jnp.concatenate(rows, 0)
+
+        q = [[query(col, t) for t in range(2)] for col in range(2)]
+        w_mid = [[weights(s, *q[col]) for s in (1, 2)] for col in range(2)]
+        w_end = [weights(3 * t, q[0][t], q[1][t]) for t in range(2)]
+
+        def lanes(k, n):
+            return pl.ds(pl.multiple_of((y + k) * SLOTS, SLOTS), n * SLOTS)
+
+        def rows(dx, k, n):
+            return pl.ds(pl.multiple_of(((x + dx) * PY + y + k) * SLOTS, SLOTS), n * SLOTS)
+
+        totals = {}
+
+        def add(key, value):
+            totals[key] = totals[key] + value if key in totals else value
+
+        def mid_distances(dx, col):
+            source = pt[rows(dx, col, 3), :]
+            return [jnp.dot(source, w, preferred_element_type=F32) for w in w_mid[col]]
+
+        def mid_sums(dx, col, pair):
+            if dx == 1:
+                cut = []
+                for t, s in enumerate(pair):
+                    at = s[SLOTS : 2 * SLOTS]
+                    left, right = at[:, :SLOTS], at[:, SLOTS:]
+                    if t == 0:
+                        left = without_self(left)
+                    else:
+                        right = without_self(right)
+                    at = jnp.concatenate([left, right], 1)
+                    cut.append(jnp.concatenate([s[:SLOTS], at, s[2 * SLOTS :]], 0))
+                pair = cut
+            g = [parts2(s) for s in pair]
+            high = jnp.concatenate([g[0][0], g[1][0]], 0)
+            low = jnp.concatenate([g[0][1], g[1][1]], 0)
+            v = jnp.concatenate([vt[x + dx, s, :, lanes(col, 3)] for s in (1, 2)], 1)
+            add(("mid", col), jnp.dot(v, high, preferred_element_type=F32))
+            add(("mid_low", col), jnp.dot(v[: 2 * VF], low, preferred_element_type=F32))
+
+        def end_distances(dx, t):
+            return jnp.dot(pt[rows(dx, 0, 4), :], w_end[t], preferred_element_type=F32)
+
+        def end_sums(dx, t, s):
+            left = parts2(s[: 3 * SLOTS, :SLOTS])
+            right = parts2(s[SLOTS:, SLOTS:])
+            high, low = [
+                jnp.concatenate(
+                    [jnp.concatenate([a, block], 0), jnp.concatenate([block, b], 0)], 1
+                )
+                for a, b in zip(left, right)
+            ]
+            v = vt[x + dx, 3 * t, :, lanes(0, 4)]
+            add(("end", t), jnp.dot(v, high, preferred_element_type=F32))
+            add(("end_low", t), jnp.dot(v[: 2 * VF], low, preferred_element_type=F32))
+
+        waiting = None
         for dx in range(3):
-            rows = pl.ds(pl.multiple_of(((x + dx) * PY + y) * SLOTS, SLOTS), span)
-            source = pt[rows, :]
-            for tile in range(3):
-                s = jnp.dot(source, weights[tile], preferred_element_type=F32)
-                g = split(s)
-                if dx == 1 and tile < 2:
-                    mid = g[SLOTS : 2 * SLOTS]
-                    own = jnp.where(diag, 0.0, mid[:, tile * SLOTS : (tile + 1) * SLOTS])
-                    other = mid[:, (1 - tile) * SLOTS : (2 - tile) * SLOTS]
-                    mid = jnp.concatenate([own, other] if tile == 0 else [other, own], 1)
-                    g = jnp.concatenate([g[:SLOTS], mid, g[2 * SLOTS :]], 0)
-                high, low = parts2(g)
-                if tile < 2:
-                    v = vt[x + dx, tile + 1, :, lanes]
-                    total = total + jnp.dot(v, high, preferred_element_type=F32)
-                    total = total + jnp.dot(v, low, preferred_element_type=F32)
-                else:
-                    ends_sum = []
-                    for t in range(2):
-                        v = vt[x + dx, 3 * t, :, lanes]
-                        col = slice(t * SLOTS, (t + 1) * SLOTS)
-                        ends_sum.append(
-                            jnp.dot(v, high[:, col], preferred_element_type=F32)
-                            + jnp.dot(v, low[:, col], preferred_element_type=F32)
-                        )
-                    total = total + jnp.concatenate(ends_sum, 1)
-        sums = total[0:VF] + total[VF : 2 * VF] + total[2 * VF : 3 * VF]
-        for t in range(2):
-            at = pl.multiple_of(c * (2 * VF) + t * VF, 8)
-            tf[pl.ds(at, VF), :] = sums[:, t * SLOTS : (t + 1) * SLOTS]
+            for k in range(2):
+                for first, then in ((mid_distances, mid_sums), (end_distances, end_sums)):
+                    made = (then, dx, k, first(dx, k))
+                    if waiting is not None:
+                        waiting[0](*waiting[1:])
+                    waiting = made
+        waiting[0](*waiting[1:])
+
+        def whole(kind, k):
+            high, low = totals[(kind, k)], totals[(kind + "_low", k)]
+            total = high[2 * VF : 3 * VF]
+            for part in (low, high):
+                total = total + part[VF : 2 * VF]
+            return total + low[:VF] + high[:VF]
+
+        mids = [whole("mid", k) for k in range(2)]
+        ends = [whole("end", k) for k in range(2)]
+        for col in range(2):
+            for t in range(2):
+                sums = mids[col][:, t * SLOTS : (t + 1) * SLOTS]
+                sums = sums + ends[t][:, col * SLOTS : (col + 1) * SLOTS]
+                at = pl.multiple_of(c * (4 * VF) + (2 * col + t) * VF, 8)
+                tf[pl.ds(at, VF), :] = sums
         return carry
 
-    lax.fori_loop(0, NX * NY, target, 0)
+    lax.fori_loop(0, NX * NY // 2, target, 0)
 
 
 def forces_of(g, coords, loc_ref, tf):
     rows = pl.ds(g * 8, 8)
     line = [loc_ref[3 + a, rows, :] for a in range(3)]
     burg = [loc_ref[6 + a, rows, :] for a in range(3)]
-    live = loc_ref[9, rows, :]
     sums = [jnp.zeros((8, SLOTS), F32) for _ in range(4)]
     for m in range(3):
         for n in range(3):
@@ -217,8 +266,7 @@
             for k in range(4):
                 at = g * (8 * VF) + 9 * k + 3 * m + n
                 sums[k] = sums[k] + a * tf[pl.ds(at, 8, stride=VF), :]
-    scale = MU_SCALE * live
-    return [scale * (coords[k] * sums[0] - sums[k + 1]) for k in range(3)]
+    return [MU_SCALE * (coords[k] * sums[0] - sums[k + 1]) for k in range(3)]
 
 
 def start_kernel(pad_ref, loc_ref, mob_ref, speed_ref, peak_ref, pf, vf, pt, vt, qf, tf):
@@ -285,10 +333,10 @@
 def on_device(positions, line_vectors, burgers, mobility, occupancy):
     slots = lax.broadcasted_iota(jnp.int32, mobility.shape, 3)
     live = (slots < occupancy[..., None]).astype(F32)
-    fields = jnp.concatenate([positions, line_vectors, burgers, live[None]], 0)
+    fields = jnp.concatenate([positions, line_vectors, burgers * live], 0)
     sides = ((GX, 1), (GY, 2), ("gz", 3))
-    pad = extended(fields, sides).reshape(10, PADDED, SLOTS)
-    loc = fields.reshape(10, CELLS, SLOTS)
+    pad = extended(fields, sides).reshape(9, PADDED, SLOTS)
+    loc = fields.reshape(9, CELLS, SLOTS)
     mob = mobility.reshape(CELLS, SLOTS)
     devices = lax.axis_size(EVERY)
     vec = jax.ShapeDtypeStruct((3, CELLS, SLOTS), F32)

time: 154 us -> 116 us (0.75)
  Pallas kernels: 86.4 us -> 48 us
    pallas_call x2, Pallas kernels: 86.4 us -> 48 us  [call(): pl.pallas_call(kernel, out_shape=out_shapes, in_specs=[whole] * len(opera...]
where the time goes in v2:
time: 116 us; the launch traced here: 114 us
  Pallas kernels  48 us (41%)
  starting transfers between devices  38.4 us (33%)
  waiting for transfers between devices  23.2 us (20%)
  other arithmetic  1.89 us (2%)
  local copies, waits for them, and re-layouts  1.42 us (1%)
    pallas_call x2, Pallas kernels, call(): pl.pallas_call(kernel, out_shape=out_shapes, in_specs=[whole] * len(opera...  48 us
    ppermute x6, starting transfers between devices, extended(): high = lax.ppermute(lax.slice_in_dim(block, 0, 1, axis=dim), axis, backward)  16.4 us
    ppermute x6, starting transfers between devices, extended(): lax.ppermute(lax.slice_in_dim(block, size - 1, size, axis=dim), axis, for...  11.8 us
    ppermute x6, waiting for transfers between devices, extended(): lax.ppermute(lax.slice_in_dim(block, size - 1, size, axis=dim), axis, for...  10.7 us
    all_to_all x1, starting transfers between devices, on_device(): peaks = lax.all_to_all(peaks.reshape(devices, 1, SLOTS), EVERY, 0, 0)  10.2 us
    ppermute x6, waiting for transfers between devices, extended(): high = lax.ppermute(lax.slice_in_dim(block, 0, 1, axis=dim), axis, backward)  6.6 us
    all_to_all x1, waiting for transfers between devices, on_device(): peaks = lax.all_to_all(peaks.reshape(devices, 1, SLOTS), EVERY, 0, 0)  5.9 us
  transfers between devices with their start and end apart: 13, of which 9 were waited for; matrix products, arithmetic and copies ran while one was open for 0% of the time, Pallas kernels for 0%

profile of v2, /device:TPU:8, one launch (start us, length us, event | category | flops | bytes accessed | tf_op | source)
XLA Modules:
  0.0 113.7 jit_solution(3203064940061034140)
XLA Ops:
  0.6 0.8 copy.8
  1.4 0.1 compare_convert_fusion
  1.5 0.0 copy-start.1
  1.5 0.0 copy-start.2
  1.5 0.8 broadcast_multiply_fusion
  2.4 0.0 copy-done.1
  2.4 0.0 copy-done.2
  2.4 0.1 pad_maximum_fusion.3
  2.5 0.1 collective-permute-start
  2.6 4.1 %collective-permute-start.1 = (f32[9,1,4,2,128]{4,3,2,1,0:T(2,128)S(1)}, f32[9,1,4,2,128]{4,3,2,1,0:T(2,128)S(1)}, u32[]{:S(2)}, u32[]{:S(2)}) collective-permute-start(f32[9,1,4,2,128]{4,3,2,1,0:T(2,128)S(1)} %get-tuple-element.15), channel_id=1, source_target_pairs={{32,0},{64,32},{96,64},{128,96},{160,128},{192,160},{224,192},{0,2... | collective-permute-start | bytes 110600 | tf_op jit(solution)/shard_map/ppermute | solution.py:44
  6.7 1.7 %collective-permute-done = f32[9,1,4,2,128]{4,3,2,1,0:T(2,128)S(1)} collective-permute-done((f32[9,1,4,2,128]{4,3,2,1,0:T(2,128)S(1)}, f32[9,1,4,2,128]{4,3,2,1,0:T(2,128)S(1)}, u32[]{:S(2)}, u32[]{:S(2)}) %collective-permute-start) | collective-permute-done | bytes 36896 | tf_op jit(solution)/shard_map/ppermute | solution.py:43
  8.4 0.0 collective-permute-done.1
  8.4 0.1 pad_maximum_fusion.9
  8.4 6.7 %collective-permute-start.2 = (f32[9,6,1,2,128]{4,3,2,1,0:T(2,128)S(1)}, f32[9,6,1,2,128]{4,3,2,1,0:T(2,128)S(1)}, u32[]{:S(2)}, u32[]{:S(2)}) collective-permute-start(f32[9,6,1,2,128]{4,3,2,1,0:T(2,128)S(1)} %get-tuple-element.12), channel_id=1, source_target_pairs={{0,4},{4,8},{8,12},{12,16},{16,20},{20,24},{24,28},{28,0},{1,5},{5... | collective-permute-start | bytes 165896 | tf_op jit(solution)/shard_map/ppermute | solution.py:43
  15.2 0.2 collective-permute-start.3
  15.3 2.1 %collective-permute-done.2 = f32[9,6,1,2,128]{4,3,2,1,0:T(2,128)S(1)} collective-permute-done((f32[9,6,1,2,128]{4,3,2,1,0:T(2,128)S(1)}, f32[9,6,1,2,128]{4,3,2,1,0:T(2,128)S(1)}, u32[]{:S(2)}, u32[]{:S(2)}) %collective-permute-start.2) | collective-permute-done | bytes 55328 | tf_op jit(solution)/shard_map/ppermute | solution.py:43
  17.5 5.9 %collective-permute-done.3 = f32[9,6,1,2,128]{4,3,2,1,0:T(2,128)S(1)} collective-permute-done((f32[9,6,1,2,128]{4,3,2,1,0:T(2,128)S(1)}, f32[9,6,1,2,128]{4,3,2,1,0:T(2,128)S(1)}, u32[]{:S(2)}, u32[]{:S(2)}) %collective-permute-start.3) | collective-permute-done | bytes 55328 | tf_op jit(solution)/shard_map/ppermute | solution.py:44
  23.3 0.2 pad_maximum_fusion.1
  23.5 0.3 fusion
  23.8 1.6 %collective-permute-start.4 = (f32[9,6,6,1,128]{4,3,2,1,0:T(1,128)S(1)}, f32[9,6,6,1,128]{4,3,2,1,0:T(1,128)S(1)}, u32[]{:S(2)}, u32[]{:S(2)}) collective-permute-start(f32[9,6,6,1,128]{4,3,2,1,0:T(1,128)S(1)} %get-tuple-element.10), channel_id=1, source_target_pairs={{0,1},{1,2},{2,3},{3,0},{4,5},{5,6},{6,7},{7,4},{8,9},{9,10},{10,1... | collective-permute-start | bytes 497672 | tf_op jit(solution)/shard_map/ppermute | solution.py:43
  25.3 1.7 %collective-permute-start.5 = (f32[9,6,6,1,128]{4,3,2,1,0:T(1,128)S(1)}, f32[9,6,6,1,128]{4,3,2,1,0:T(1,128)S(1)}, u32[]{:S(2)}, u32[]{:S(2)}) collective-permute-start(f32[9,6,6,1,128]{4,3,2,1,0:T(1,128)S(1)} %get-tuple-element.11), channel_id=1, source_target_pairs={{1,0},{2,1},{3,2},{0,3},{5,4},{6,5},{7,6},{4,7},{9,8},{10,9},{11,1... | collective-permute-start | bytes 497672 | tf_op jit(solution)/shard_map/ppermute | solution.py:44
  27.1 3.3 %collective-permute-done.4 = f32[9,6,6,1,128]{4,3,2,1,0:T(1,128)S(1)} collective-permute-done((f32[9,6,6,1,128]{4,3,2,1,0:T(1,128)S(1)}, f32[9,6,6,1,128]{4,3,2,1,0:T(1,128)S(1)}, u32[]{:S(2)}, u32[]{:S(2)}) %collective-permute-start.4) | collective-permute-done | bytes 165920 | tf_op jit(solution)/shard_map/ppermute | solution.py:43
  30.4 0.3 collective-permute-done.5
  30.7 0.0 copy-start
  30.7 0.5 pad_maximum_fusion
  31.1 0.3 copy-done
  31.4 23.9 %start_forces.1 = (f32[3,32,128]{2,1,0:T(8,128)S(1)}, f32[256,128]{1,0:T(8,128)}) custom-call(f32[9,144,128]{2,1,0:T(8,128)S(1)} %bitcast.14, f32[9,32,128]{2,1,0:T(8,128)S(1)} %bitcast.16, f32[32,128]{1,0:T(8,128)S(1)} %bitcast.24), custom_call_target="tpu_custom_call" | custom-call | tf_op jit(solution)/shard_map/start_forces/pallas_call | solution.py:315
  55.3 0.0 collective-permute-start.6
  55.3 3.5 %collective-permute-start.7 = (f32[3,1,4,2,128]{4,3,2,1,0:T(2,128)S(1)}, f32[3,1,4,2,128]{4,3,2,1,0:T(2,128)S(1)}, u32[]{:S(2)}, u32[]{:S(2)}) collective-permute-start(f32[3,1,4,2,128]{4,3,2,1,0:T(2,128)S(1)} %get-tuple-element.21), channel_id=1, source_target_pairs={{32,0},{64,32},{96,64},{128,96},{160,128},{192,160},{224,192},{0,2... | collective-permute-start | bytes 36872 | tf_op jit(solution)/shard_map/ppermute | solution.py:44
  58.9 1.4 %collective-permute-done.6 = f32[3,1,4,2,128]{4,3,2,1,0:T(2,128)S(1)} collective-permute-done((f32[3,1,4,2,128]{4,3,2,1,0:T(2,128)S(1)}, f32[3,1,4,2,128]{4,3,2,1,0:T(2,128)S(1)}, u32[]{:S(2)}, u32[]{:S(2)}) %collective-permute-start.6) | collective-permute-done | bytes 12320 | tf_op jit(solution)/shard_map/ppermute | solution.py:43
  60.3 0.0 collective-permute-done.7
  60.3 1.9 %collective-permute-start.8 = (f32[3,6,1,2,128]{4,3,2,1,0:T(2,128)S(1)}, f32[3,6,1,2,128]{4,3,2,1,0:T(2,128)S(1)}, u32[]{:S(2)}, u32[]{:S(2)}) collective-permute-start(f32[3,6,1,2,128]{4,3,2,1,0:T(2,128)S(1)} %get-tuple-element.18), channel_id=1, source_target_pairs={{0,4},{4,8},{8,12},{12,16},{16,20},{20,24},{24,28},{28,0},{1,5},{5... | collective-permute-start | bytes 55304 | tf_op jit(solution)/shard_map/ppermute | solution.py:43
  62.2 5.0 %collective-permute-start.9 = (f32[3,6,1,2,128]{4,3,2,1,0:T(2,128)S(1)}, f32[3,6,1,2,128]{4,3,2,1,0:T(2,128)S(1)}, u32[]{:S(2)}, u32[]{:S(2)}) collective-permute-start(f32[3,6,1,2,128]{4,3,2,1,0:T(2,128)S(1)} %get-tuple-element.19), channel_id=1, source_target_pairs={{4,0},{8,4},{12,8},{16,12},{20,16},{24,20},{28,24},{0,28},{5,1},{9... | collective-permute-start | bytes 55304 | tf_op jit(solution)/shard_map/ppermute | solution.py:44
  67.2 10.2 %all-to-all-start = ((f32[256,1,128]{2,1,0:T(1,128)}), f32[256,1,128]{2,1,0:T(1,128)S(1)}, u32[]{:S(2)}, u32[]{:S(2)}) async-start(f32[256,1,128]{2,1,0:T(1,128)} %bitcast.6), calls=%async_computation | async-start | bytes 262144 | tf_op jit(solution)/shard_map/all_to_all | solution.py:349
  77.4 0.0 collective-permute-done.8
  77.4 0.0 collective-permute-done.9
  77.5 0.1 pad_maximum_fusion.4
  77.5 0.1 fusion.2
  77.6 1.5 %collective-permute-start.10 = (f32[3,6,6,1,128]{4,3,2,1,0:T(1,128)S(1)}, f32[3,6,6,1,128]{4,3,2,1,0:T(1,128)S(1)}, u32[]{:S(2)}, u32[]{:S(2)}) collective-permute-start(f32[3,6,6,1,128]{4,3,2,1,0:T(1,128)S(1)} %get-tuple-element.16), channel_id=1, source_target_pairs={{0,1},{1,2},{2,3},{3,0},{4,5},{5,6},{6,7},{7,4},{8,9},{9,10},{10,1... | collective-permute-start | bytes 165896 | tf_op jit(solution)/shard_map/ppermute | solution.py:43
  79.2 1.8 %collective-permute-start.11 = (f32[3,6,6,1,128]{4,3,2,1,0:T(1,128)S(1)}, f32[3,6,6,1,128]{4,3,2,1,0:T(1,128)S(1)}, u32[]{:S(2)}, u32[]{:S(2)}) collective-permute-start(f32[3,6,6,1,128]{4,3,2,1,0:T(1,128)S(1)} %get-tuple-element.17), channel_id=1, source_target_pairs={{1,0},{2,1},{3,2},{0,3},{5,4},{6,5},{7,6},{4,7},{9,8},{10,9},{11,1... | collective-permute-start | bytes 165896 | tf_op jit(solution)/shard_map/ppermute | solution.py:44
  80.9 2.2 %collective-permute-done.10 = f32[3,6,6,1,128]{4,3,2,1,0:T(1,128)S(1)} collective-permute-done((f32[3,6,6,1,128]{4,3,2,1,0:T(1,128)S(1)}, f32[3,6,6,1,128]{4,3,2,1,0:T(1,128)S(1)}, u32[]{:S(2)}, u32[]{:S(2)}) %collective-permute-start.10) | collective-permute-done | bytes 55328 | tf_op jit(solution)/shard_map/ppermute | solution.py:43
  83.2 0.4 collective-permute-done.11
  83.6 0.2 pad_maximum_fusion.2
  83.7 5.9 %all-to-all-done = f32[256,1,128]{2,1,0:T(1,128)S(1)} async-done(((f32[256,1,128]{2,1,0:T(1,128)}), f32[256,1,128]{2,1,0:T(1,128)S(1)}, u32[]{:S(2)}, u32[]{:S(2)}) %all-to-all-start) | async-done | bytes 131104 | tf_op jit(solution)/shard_map/all_to_all | solution.py:349
  89.6 24.0 %end_forces.1 = (f32[3,32,128]{2,1,0:T(8,128)}, f32[3,32,128]{2,1,0:T(8,128)}) custom-call(f32[9,144,128]{2,1,0:T(8,128)S(1)} %bitcast.15, f32[9,32,128]{2,1,0:T(8,128)S(1)} %bitcast.17, f32[32,128]{1,0:T(8,128)S(1)} %bitcast.25, f32[3,144,128]{2,1,0:T(8,128)S(1)} %bitcast.22, f32[3,32,128]{2,1,0:T(8,128)S(1)} %get-tuple-element.6.speed_ref, ...), custom_call_target="tpu_custom_call" | custom-call | tf_op jit(solution)/shard_map/end_forces/pallas_call | solution.py:315
  (3 shorter events, 0.0 us)
Async XLA Ops:
  1.5 0.9 copy-start.1
  1.5 0.8 copy-start.2
  2.5 5.9 %collective-permute-start = (f32[9,1,4,2,128]{4,3,2,1,0:T(2,128)S(1)}, f32[9,1,4,2,128]{4,3,2,1,0:T(2,128)S(1)}, u32[]{:S(2)}, u32[]{:S(2)}) collective-permute-start(f32[9,1,4,2,128]{4,3,2,1,0:T(2,128)S(1)} %get-tuple-element.14), channel_id=1, source_target_pairs={{0,32},{32,64},{64,96},{96,128},{128,160},{160,192},{192,224},{224... | collective-permute-start | bytes 110600 | tf_op jit(solution)/shard_map/ppermute | solution.py:43
  2.6 5.8 %collective-permute-start.1 = (f32[9,1,4,2,128]{4,3,2,1,0:T(2,128)S(1)}, f32[9,1,4,2,128]{4,3,2,1,0:T(2,128)S(1)}, u32[]{:S(2)}, u32[]{:S(2)}) collective-permute-start(f32[9,1,4,2,128]{4,3,2,1,0:T(2,128)S(1)} %get-tuple-element.15), channel_id=1, source_target_pairs={{32,0},{64,32},{96,64},{128,96},{160,128},{192,160},{224,192},{0,2... | collective-permute-start | bytes 110600 | tf_op jit(solution)/shard_map/ppermute | solution.py:44
  8.4 9.0 %collective-permute-start.2 = (f32[9,6,1,2,128]{4,3,2,1,0:T(2,128)S(1)}, f32[9,6,1,2,128]{4,3,2,1,0:T(2,128)S(1)}, u32[]{:S(2)}, u32[]{:S(2)}) collective-permute-start(f32[9,6,1,2,128]{4,3,2,1,0:T(2,128)S(1)} %get-tuple-element.12), channel_id=1, source_target_pairs={{0,4},{4,8},{8,12},{12,16},{16,20},{20,24},{24,28},{28,0},{1,5},{5... | collective-permute-start | bytes 165896 | tf_op jit(solution)/shard_map/ppermute | solution.py:43
  15.2 8.2 %collective-permute-start.3 = (f32[9,6,1,2,128]{4,3,2,1,0:T(2,128)S(1)}, f32[9,6,1,2,128]{4,3,2,1,0:T(2,128)S(1)}, u32[]{:S(2)}, u32[]{:S(2)}) collective-permute-start(f32[9,6,1,2,128]{4,3,2,1,0:T(2,128)S(1)} %get-tuple-element.13), channel_id=1, source_target_pairs={{4,0},{8,4},{12,8},{16,12},{20,16},{24,20},{28,24},{0,28},{5,1},{9... | collective-permute-start | bytes 165896 | tf_op jit(solution)/shard_map/ppermute | solution.py:44
  23.8 6.6 %collective-permute-start.4 = (f32[9,6,6,1,128]{4,3,2,1,0:T(1,128)S(1)}, f32[9,6,6,1,128]{4,3,2,1,0:T(1,128)S(1)}, u32[]{:S(2)}, u32[]{:S(2)}) collective-permute-start(f32[9,6,6,1,128]{4,3,2,1,0:T(1,128)S(1)} %get-tuple-element.10), channel_id=1, source_target_pairs={{0,1},{1,2},{2,3},{3,0},{4,5},{5,6},{6,7},{7,4},{8,9},{9,10},{10,1... | collective-permute-start | bytes 497672 | tf_op jit(solution)/shard_map/ppermute | solution.py:43
  25.3 5.3 %collective-permute-start.5 = (f32[9,6,6,1,128]{4,3,2,1,0:T(1,128)S(1)}, f32[9,6,6,1,128]{4,3,2,1,0:T(1,128)S(1)}, u32[]{:S(2)}, u32[]{:S(2)}) collective-permute-start(f32[9,6,6,1,128]{4,3,2,1,0:T(1,128)S(1)} %get-tuple-element.11), channel_id=1, source_target_pairs={{1,0},{2,1},{3,2},{0,3},{5,4},{6,5},{7,6},{4,7},{9,8},{10,9},{11,1... | collective-permute-start | bytes 497672 | tf_op jit(solution)/shard_map/ppermute | solution.py:44
  30.7 0.7 copy-start
  55.3 4.9 %collective-permute-start.6 = (f32[3,1,4,2,128]{4,3,2,1,0:T(2,128)S(1)}, f32[3,1,4,2,128]{4,3,2,1,0:T(2,128)S(1)}, u32[]{:S(2)}, u32[]{:S(2)}) collective-permute-start(f32[3,1,4,2,128]{4,3,2,1,0:T(2,128)S(1)} %get-tuple-element.20), channel_id=1, source_target_pairs={{0,32},{32,64},{64,96},{96,128},{128,160},{160,192},{192,224},{224... | collective-permute-start | bytes 36872 | tf_op jit(solution)/shard_map/ppermute | solution.py:43
  55.3 4.9 %collective-permute-start.7 = (f32[3,1,4,2,128]{4,3,2,1,0:T(2,128)S(1)}, f32[3,1,4,2,128]{4,3,2,1,0:T(2,128)S(1)}, u32[]{:S(2)}, u32[]{:S(2)}) collective-permute-start(f32[3,1,4,2,128]{4,3,2,1,0:T(2,128)S(1)} %get-tuple-element.21), channel_id=1, source_target_pairs={{32,0},{64,32},{96,64},{128,96},{160,128},{192,160},{224,192},{0,2... | collective-permute-start | bytes 36872 | tf_op jit(solution)/shard_map/ppermute | solution.py:44
  60.3 17.1 %collective-permute-start.8 = (f32[3,6,1,2,128]{4,3,2,1,0:T(2,128)S(1)}, f32[3,6,1,2,128]{4,3,2,1,0:T(2,128)S(1)}, u32[]{:S(2)}, u32[]{:S(2)}) collective-permute-start(f32[3,6,1,2,128]{4,3,2,1,0:T(2,128)S(1)} %get-tuple-element.18), channel_id=1, source_target_pairs={{0,4},{4,8},{8,12},{12,16},{16,20},{20,24},{24,28},{28,0},{1,5},{5... | collective-permute-start | bytes 55304 | tf_op jit(solution)/shard_map/ppermute | solution.py:43
  62.2 15.2 %collective-permute-start.9 = (f32[3,6,1,2,128]{4,3,2,1,0:T(2,128)S(1)}, f32[3,6,1,2,128]{4,3,2,1,0:T(2,128)S(1)}, u32[]{:S(2)}, u32[]{:S(2)}) collective-permute-start(f32[3,6,1,2,128]{4,3,2,1,0:T(2,128)S(1)} %get-tuple-element.19), channel_id=1, source_target_pairs={{4,0},{8,4},{12,8},{16,12},{20,16},{24,20},{28,24},{0,28},{5,1},{9... | collective-permute-start | bytes 55304 | tf_op jit(solution)/shard_map/ppermute | solution.py:44
  67.2 22.4 %all-to-all-start = ((f32[256,1,128]{2,1,0:T(1,128)}), f32[256,1,128]{2,1,0:T(1,128)S(1)}, u32[]{:S(2)}, u32[]{:S(2)}) async-start(f32[256,1,128]{2,1,0:T(1,128)} %bitcast.6), calls=%async_computation | async-start | bytes 262144 | tf_op jit(solution)/shard_map/all_to_all | solution.py:349
  77.6 5.5 %collective-permute-start.10 = (f32[3,6,6,1,128]{4,3,2,1,0:T(1,128)S(1)}, f32[3,6,6,1,128]{4,3,2,1,0:T(1,128)S(1)}, u32[]{:S(2)}, u32[]{:S(2)}) collective-permute-start(f32[3,6,6,1,128]{4,3,2,1,0:T(1,128)S(1)} %get-tuple-element.16), channel_id=1, source_target_pairs={{0,1},{1,2},{2,3},{3,0},{4,5},{5,6},{6,7},{7,4},{8,9},{9,10},{10,1... | collective-permute-start | bytes 165896 | tf_op jit(solution)/shard_map/ppermute | solution.py:43
  79.2 4.4 %collective-permute-start.11 = (f32[3,6,6,1,128]{4,3,2,1,0:T(1,128)S(1)}, f32[3,6,6,1,128]{4,3,2,1,0:T(1,128)S(1)}, u32[]{:S(2)}, u32[]{:S(2)}) collective-permute-start(f32[3,6,6,1,128]{4,3,2,1,0:T(1,128)S(1)} %get-tuple-element.17), channel_id=1, source_target_pairs={{1,0},{2,1},{3,2},{0,3},{5,4},{6,5},{7,6},{4,7},{9,8},{10,9},{11,1... | collective-permute-start | bytes 165896 | tf_op jit(solution)/shard_map/ppermute | solution.py:44

commit v3 on v2

v3 whole, which is shorter than its diff:
```python
import functools

import jax
import jax.numpy as jnp
from jax import lax
from jax.experimental import pallas as pl
from jax.experimental.pallas import tpu as pltpu
from jax.sharding import Mesh
from jax.sharding import PartitionSpec as P

GX = ("gx_0", "gx_1")
GY = ("gy_0", "gy_1")
EVERY = ("gx_0", "gx_1", "gy_0", "gy_1", "gz")

CORE_SQUARED = 0.25
MU_SCALE = 0.05
CROSS_WEIGHT = 0.5
STEP_LIMIT = 0.1

NX, NY, NZ, SLOTS = 4, 4, 2, 128
PX, PY, PZ = NX + 2, NY + 2, NZ + 2
CELLS = NX * NY * NZ
PADDED = PX * PY * PZ
KF = 32
VF = 40
FAR = 3e38
VROWS = 128
F32 = jnp.float32
BF16 = jnp.bfloat16


def ring(axis):
    count = lax.axis_size(axis)
    forward = [(i, (i + 1) % count) for i in range(count)]
    return forward, [(t, s) for s, t in forward]


def extended(block, sides):
    for axis, dim in sides:
        forward, backward = ring(axis)
        size = block.shape[dim]
        low = lax.ppermute(lax.slice_in_dim(block, size - 1, size, axis=dim), axis, forward)
        high = lax.ppermute(lax.slice_in_dim(block, 0, 1, axis=dim), axis, backward)
        block = jnp.concatenate([low, block, high], axis=dim)
    return block


def parts3(v):
    high = v.astype(BF16).astype(F32)
    rest = v - high
    mid = rest.astype(BF16).astype(F32)
    return high, mid, rest - mid


def distance_features(coords, source):
    one = jnp.ones_like(coords[0])
    square = coords[0] * coords[0] + coords[1] * coords[1] + coords[2] * coords[2]
    rows = []
    for x in coords:
        h, m, l = parts3(x)
        if source:
            h, m, l = -2.0 * h, -2.0 * m, -2.0 * l
            rows += [h, h, m, m, h, l]
        else:
            rows += [h, m, h, m, l, h]
    if source:
        rows += [*parts3(square), one, one, one]
    else:
        rows += [one, one, one, *parts3(square + CORE_SQUARED)]
    return rows + [jnp.zeros_like(one)] * (KF - len(rows))


def prepare_sources(pad_ref, shift, pf, vf, inner):
    sub = lax.broadcasted_iota(jnp.int32, (8, SLOTS), 0)
    y_in = (sub >> 2).astype(F32)
    z_in = (sub & 3).astype(F32)

    def group(g, carry):
        rows = pl.ds(pl.multiple_of(g * 8, 8), 8)
        if inner:
            x0 = (g // 2).astype(F32) - float(PX // 2)
            y_at = y_in + (((g % 2) * 2 + 1).astype(F32) - float(PY // 2))
        else:
            x0 = g.astype(F32) - float(PX // 2)
            y_at = y_in * float(PY - 1) - float(PY // 2)
        pos = [pad_ref[a, rows, :] for a in range(3)]
        if shift is not None:
            padv_ref, step = shift
            pos = [pos[a] + step * padv_ref[a, rows, :] for a in range(3)]
        coords = [pos[0] + x0, pos[1] + y_at, pos[2] + (z_in - float(PZ // 2))]
        for f, row in enumerate(distance_features(coords, True)):
            pf[pl.ds(g * (8 * KF) + f, 8, stride=KF), :] = row
        line = [pad_ref[3 + a, rows, :] for a in range(3)]
        burg = [pad_ref[6 + a, rows, :] for a in range(3)]
        outer = [[burg[m] * line[n] for n in range(3)] for m in range(3)]
        for m in range(3):
            for n in range(3):
                b = outer[m][n] - CROSS_WEIGHT * outer[n][m]
                f = 3 * m + n
                vf[pl.ds(g * (8 * VF) + f, 8, stride=VF), :] = b
                for a in range(3):
                    at = g * (8 * VF) + 9 * (a + 1) + f
                    vf[pl.ds(at, 8, stride=VF), :] = b * coords[a]
        return carry

    lax.fori_loop(0, pad_ref.shape[1] // 8, group, 0)


def lay_out_sources(pf, vf, pt, vt):
    across = vt.shape[3] // SLOTS

    def column(c, carry):
        at = pl.multiple_of(c * 128, 128)
        pt[pl.ds(at, 128), :] = pf[pl.ds(at, 128), :].T.astype(BF16)
        x, y = c // across, c % across
        lanes = pl.ds(pl.multiple_of(y * SLOTS, SLOTS), SLOTS)
        for z in range(PZ):
            v = vf[pl.ds(pl.multiple_of(c * (PZ * VF) + z * VF, 8), VF), :]
            rows = [*parts3(v), jnp.zeros((VROWS - 3 * VF, SLOTS), F32)]
            vt[x, z, :, lanes] = jnp.concatenate(rows, 0).astype(BF16)
        return carry

    lax.fori_loop(0, PX * across, column, 0, unroll=6)


def prepare_targets(loc_ref, shift, qf):
    sub = lax.broadcasted_iota(jnp.int32, (8, SLOTS), 0)
    y_in = (sub >> 1).astype(F32)
    z_in = (sub & 1).astype(F32)
    every = []
    for g in range(CELLS // 8):
        rows = pl.ds(g * 8, 8)
        pos = [loc_ref[a, rows, :] for a in range(3)]
        if shift is not None:
            speed_ref, step = shift
            pos = [pos[a] + step * speed_ref[a, rows, :] for a in range(3)]
        coords = [
            pos[0] + float(g + 1 - PX // 2),
            pos[1] + (y_in + float(1 - PY // 2)),
            pos[2] + (z_in + float(1 - PZ // 2)),
        ]
        for f, row in enumerate(distance_features(coords, False)):
            qf[pl.ds(g * (8 * KF) + f, 8, stride=KF), :] = row
        every.append(coords)
    return every


def parts2(s):
    inverse = lax.rsqrt(s)
    g = inverse * inverse * inverse
    high = g.astype(BF16)
    return high, (g - high.astype(F32)).astype(BF16)


def without_self(s):
    same = lax.broadcasted_iota(jnp.int32, s.shape, 0) == lax.broadcasted_iota(
        jnp.int32, s.shape, 1
    )
    return jnp.where(same, FAR, s)


def chunks_of(inner):
    chunks = []
    if inner:
        for y in range(NY):
            low, high = max(y - 1, 0), min(y + 1, NY - 1)
            for dx in range(3):
                runs = [(dx, low, high - low + 1, s, True, True) for s in (1, 2)]
                chunks.append(((y, 0), (y, 1), runs))
            if y % 2 == 0:
                continue
            for t in range(2):
                runs = []
                for dx in range(3):
                    if y == 1:
                        runs.append((dx, 0, 2, 3 * t, True, True))
                        runs.append((dx, 2, 1, 3 * t, False, True))
                    else:
                        runs.append((dx, 1, 1, 3 * t, True, False))
                        runs.append((dx, 2, 2, 3 * t, True, True))
                chunks.append(((y - 1, t), (y, t), runs))
    else:
        for h, y in ((0, 0), (1, NY - 1)):
            runs = [(dx, h, 1, s, True, True) for dx in range(3) for s in (1, 2)]
            chunks.append(((y, 0), (y, 1), runs))
        for t in range(2):
            runs = [(dx, 0, 1, 3 * t, True, False) for dx in range(3)]
            runs += [(dx, 1, 1, 3 * t, False, True) for dx in range(3)]
            chunks.append(((0, t), (NY - 1, t), runs))
    return chunks


def pair_sums(pt, vt, qf, tf, inner, before=None):
    across = vt.shape[3] // SLOTS
    zero = jnp.zeros((KF, 2 * SLOTS), BF16)
    block = jnp.zeros((SLOTS, SLOTS), BF16)
    chunks = chunks_of(inner)

    def plane(x, carry):
        def query(y, t):
            at = pl.multiple_of(x * (NY * NZ * KF) + (y * NZ + t) * KF, 8)
            return qf[pl.ds(at, KF), :].astype(BF16)

        def distances(targets, runs):
            q = [query(*target) for target in targets]
            made = []
            for dx, first, count, s, to_left, to_right in runs:
                at = ((x + dx) * across + first) * SLOTS
                source = pt[pl.ds(pl.multiple_of(at, SLOTS), count * SLOTS), :]
                rows = [zero] * PZ
                rows[s] = jnp.concatenate(q, 1)
                if not (to_left and to_right):
                    rows = [r[:, :SLOTS] for r in rows]
                    rows[s] = q[0] if to_left else q[1]
                w = jnp.concatenate(rows, 0)
                made.append(jnp.dot(source, w, preferred_element_type=F32))
            return made

        def weights(targets, runs, made):
            high, low, v = [], [], []
            for (dx, first, count, s, to_left, to_right), r in zip(runs, made):
                both = to_left and to_right
                if dx == 1 and inner and both and s in (1, 2):
                    y = targets[0][0] - first
                    at = r[y * SLOTS : (y + 1) * SLOTS]
                    halves = [at[:, :SLOTS], at[:, SLOTS:]]
                    halves[s - 1] = without_self(halves[s - 1])
                    parts = [r[: y * SLOTS], jnp.concatenate(halves, 1), r[(y + 1) * SLOTS :]]
                    r = jnp.concatenate([p for p in parts if p.shape[0]], 0)
                for into, part in zip((high, low), parts2(r)):
                    if not both:
                        part = jnp.concatenate([part, block] if to_left else [block, part], 1)
                    into.append(part)
                v.append(vt[x + dx, s, :, first * SLOTS : (first + count) * SLOTS])
            return jnp.concatenate(v, 1), jnp.concatenate(high, 0), jnp.concatenate(low, 0)

        totals = {}

        def add(key, value):
            totals[key] = totals[key] + value if key in totals else value

        made = distances(chunks[0][:2], chunks[0][2])
        for n, (left, right, runs) in enumerate(chunks):
            coming = None
            if n + 1 < len(chunks):
                coming = distances(chunks[n + 1][:2], chunks[n + 1][2])
            v, high, low = weights((left, right), runs, made)
            add((left, right, 0), jnp.dot(v, high, preferred_element_type=F32))
            add((left, right, 1), jnp.dot(v[: 2 * VF], low, preferred_element_type=F32))
            made = coming

        cells = {}
        for left, right, kind in totals:
            if kind == 1:
                continue
            high, low = totals[(left, right, 0)], totals[(left, right, 1)]
            total = high[2 * VF : 3 * VF]
            for part in (low, high):
                total = total + part[VF : 2 * VF]
            total = total + low[:VF] + high[:VF]
            for k, cell in enumerate((left, right)):
                part = total[:, k * SLOTS : (k + 1) * SLOTS]
                cells[cell] = cells[cell] + part if cell in cells else part
        for y in range(NY):
            for t in range(NZ):
                at = pl.multiple_of(x * (NY * NZ * VF) + (y * NZ + t) * VF, 8)
                at = pl.ds(at, VF)
                if before is None:
                    tf[at, :] = cells[y, t]
                elif (y, t) in cells:
                    tf[at, :] = before[at, :] + cells[y, t]
                else:
                    tf[at, :] = before[at, :]
        return carry

    lax.fori_loop(0, NX, plane, 0)


def forces_of(g, coords, loc_ref, tf):
    rows = pl.ds(g * 8, 8)
    line = [loc_ref[3 + a, rows, :] for a in range(3)]
    burg = [loc_ref[6 + a, rows, :] for a in range(3)]
    sums = [jnp.zeros((8, SLOTS), F32) for _ in range(4)]
    for m in range(3):
        for n in range(3):
            a = burg[m] * line[n]
            for k in range(4):
                at = g * (8 * VF) + 9 * k + 3 * m + n
                sums[k] = sums[k] + a * tf[pl.ds(at, 8, stride=VF), :]
    return [MU_SCALE * (coords[k] * sums[0] - sums[k + 1]) for k in range(3)]


def step_of(peak_ref):
    peak = jnp.max(jnp.max(peak_ref[...], axis=0, keepdims=True), axis=1, keepdims=True)
    return STEP_LIMIT * lax.rsqrt(jnp.broadcast_to(peak, (8, SLOTS)) + 1e-12)


def start_inner(pad_ref, loc_ref, sums_ref, pf, vf, pt, vt, qf):
    prepare_sources(pad_ref, None, pf, vf, True)
    lay_out_sources(pf, vf, pt, vt)
    prepare_targets(loc_ref, None, qf)
    pair_sums(pt, vt, qf, sums_ref, True)


def end_inner(pad_ref, loc_ref, padv_ref, speed_ref, peak_ref, sums_ref, pf, vf, pt, vt, qf):
    step = step_of(peak_ref)
    prepare_sources(pad_ref, (padv_ref, step), pf, vf, True)
    lay_out_sources(pf, vf, pt, vt)
    prepare_targets(loc_ref, (speed_ref, step), qf)
    pair_sums(pt, vt, qf, sums_ref, True)


def start_outer(
    rim_ref, loc_ref, mob_ref, sums_ref, speed_ref, peak_ref, pf, vf, pt, vt, qf, tf
):
    prepare_sources(rim_ref, None, pf, vf, False)
    lay_out_sources(pf, vf, pt, vt)
    every = prepare_targets(loc_ref, None, qf)
    pair_sums(pt, vt, qf, tf, False, sums_ref)
    peak = jnp.zeros((8, SLOTS), F32)
    for g in range(CELLS // 8):
        rows = pl.ds(g * 8, 8)
        force = forces_of(g, every[g], loc_ref, tf)
        mobility = mob_ref[rows, :]
        speed = [mobility * f for f in force]
        for a in range(3):
            speed_ref[a, rows, :] = speed[a]
        peak = jnp.maximum(
            peak, speed[0] * speed[0] + speed[1] * speed[1] + speed[2] * speed[2]
        )
    top = jnp.max(jnp.max(peak, axis=0, keepdims=True), axis=1, keepdims=True)
    peak_ref[...] = jnp.broadcast_to(top, peak_ref.shape)


def end_outer(
    rim_ref, loc_ref, mob_ref, rimv_ref, speed_ref, peak_ref, sums_ref, moved_ref, force_ref,
    pf, vf, pt, vt, qf, tf,
):
    step = step_of(peak_ref)
    prepare_sources(rim_ref, (rimv_ref, step), pf, vf, False)
    lay_out_sources(pf, vf, pt, vt)
    every = prepare_targets(loc_ref, (speed_ref, step), qf)
    pair_sums(pt, vt, qf, tf, False, sums_ref)
    for g in range(CELLS // 8):
        rows = pl.ds(g * 8, 8)
        force = forces_of(g, every[g], loc_ref, tf)
        mobility = mob_ref[rows, :]
        for a in range(3):
            force_ref[a, rows, :] = force[a]
            moved_ref[a, rows, :] = loc_ref[a, rows, :] + 0.5 * step * (
                speed_ref[a, rows, :] + mobility * force[a]
            )


def call(kernel, out_shapes, operands, name, inner):
    whole = pl.BlockSpec(memory_space=pltpu.VMEM)
    across = NY if inner else PY - NY
    cells = PX * across * PZ
    scratch = [
        pltpu.VMEM((cells * KF, SLOTS), F32),
        pltpu.VMEM((cells * VF, SLOTS), F32),
        pltpu.VMEM((PX * across * SLOTS, 128), BF16),
        pltpu.VMEM((PX, PZ, VROWS, across * SLOTS), BF16),
        pltpu.VMEM((CELLS * KF, SLOTS), F32),
    ]
    if not inner:
        scratch.append(pltpu.VMEM((CELLS * VF, SLOTS), F32))
    return pl.pallas_call(
        kernel,
        out_shape=out_shapes,
        in_specs=[whole] * len(operands),
        out_specs=[whole] * len(out_shapes),
        scratch_shapes=scratch,
        compiler_params=pltpu.CompilerParams(vmem_limit_bytes=48 << 20),
        name=name,
    )(*operands)


VEC = jax.ShapeDtypeStruct((3, CELLS, SLOTS), F32)
SUMS = jax.ShapeDtypeStruct((CELLS * VF, SLOTS), F32)


def widened(block):
    block = extended(block, ((GX, 1), ("gz", 3)))
    forward, backward = ring(GY)
    low = lax.ppermute(block[:, :, NY - 1 :], GY, forward)
    high = lax.ppermute(block[:, :, :1], GY, backward)
    rim = jnp.concatenate([low, high], 2)
    count = block.shape[0]
    return block.reshape(count, PX * NY * PZ, SLOTS), rim.reshape(count, PX * 2 * PZ, SLOTS)


def on_device(positions, line_vectors, burgers, mobility, occupancy):
    slots = lax.broadcasted_iota(jnp.int32, mobility.shape, 3)
    live = (slots < occupancy[..., None]).astype(F32)
    fields = jnp.concatenate([positions, line_vectors, burgers * live], 0)
    pad, rim = widened(fields)
    loc = fields.reshape(9, CELLS, SLOTS)
    mob = mobility.reshape(CELLS, SLOTS)
    devices = lax.axis_size(EVERY)
    peaks = jax.ShapeDtypeStruct((devices, SLOTS), F32)
    (sums,) = call(start_inner, [SUMS], [pad, loc], "start_inner", True)
    speed, peaks = call(
        start_outer, [VEC, peaks], [rim, loc, mob, sums], "start_outer", False
    )
    peaks = lax.all_to_all(peaks.reshape(devices, 1, SLOTS), EVERY, 0, 0)
    peaks = peaks.reshape(devices, SLOTS)
    padv, rimv = widened(speed.reshape(3, NX, NY, NZ, SLOTS))
    (sums,) = call(end_inner, [SUMS], [pad, loc, padv, speed, peaks], "end_inner", True)
    moved, force = call(
        end_outer, [VEC, VEC], [rim, loc, mob, rimv, speed, peaks, sums], "end_outer", False
    )
    shape = (3, NX, NY, NZ, SLOTS)
    return moved.reshape(shape), force.reshape(shape)


def solution(mesh):
    finer = Mesh(
        mesh.devices.reshape(4, 2, 4, 2, mesh.shape["gz"]), ("gx_0", "gx_1", "gy_0", "gy_1", "gz")
    )
    in_specs = (
        P(None, GX, GY, "gz", None),
        P(None, GX, GY, "gz", None),
        P(None, GX, GY, "gz", None),
        P(GX, GY, "gz", None),
        P(GX, GY, "gz"),
    )
    out_specs = (P(None, GX, GY, "gz", None), P(None, GX, GY, "gz", None))
    return jax.shard_map(
        on_device, mesh=finer, in_specs=in_specs, out_specs=out_specs, check_vma=False
    )
```

time: 116 us -> 107 us (0.922); the launches traced: 114 us -> 107 us
  waiting for transfers between devices: 23.2 us -> 14.2 us
  starting transfers between devices: 38.4 us -> 40.1 us
    ppermute x0 -> x4, starting transfers between devices: none -> 13.8 us  [the longest x2 13.2 us: widened(): low = lax.ppermute(block[:, :, NY - 1:], GY, forward)]
    ppermute x6 -> x4, starting transfers between devices: 11.8 us -> 3.22 us  [extended(): lax.ppermute(lax.slice_in_dim(block, size - 1, size, axis=dim), axis, for...]
    ppermute x0 -> x4, waiting for transfers between devices: none -> 8.11 us  [the longest x2 6.02 us: widened(): high = lax.ppermute(block[:, :, :1], GY, backward)]
    ppermute x6 -> x4, waiting for transfers between devices: 6.6 us -> 0.1 us  [extended(): high = lax.ppermute(lax.slice_in_dim(block, 0, 1, axis=dim), axis, backward)]
    all_to_all x1, waiting for transfers between devices: 5.9 us -> 0.01 us  [on_device(): peaks = lax.all_to_all(peaks.reshape(devices, 1, SLOTS), EVERY, 0, 0)]
    ppermute x6 -> x4, starting transfers between devices: 16.4 us -> 11.2 us  [extended(): high = lax.ppermute(lax.slice_in_dim(block, 0, 1, axis=dim), axis, backward)]
    ppermute x6 -> x4, waiting for transfers between devices: 10.7 us -> 5.98 us  [extended(): lax.ppermute(lax.slice_in_dim(block, size - 1, size, axis=dim), axis, for...]
    all_to_all x1, starting transfers between devices: 10.2 us -> 11.9 us  [on_device(): peaks = lax.all_to_all(peaks.reshape(devices, 1, SLOTS), EVERY, 0, 0)]
  transfers between devices with their start and end apart: 13 -> 13, of which waited for: 9 -> 6; matrix products, arithmetic and copies ran while one was open for 0% -> 0% of each run, Pallas kernels for 0% -> 17%
where the time goes in v3:
time: 107 us
  Pallas kernels  48.6 us (45%)
  starting transfers between devices  40.1 us (37%)
  waiting for transfers between devices  14.2 us (13%)
  local copies, waits for them, and re-layouts  1.73 us (2%)
  other arithmetic  1.63 us (2%)
    pallas_call x4, Pallas kernels, call(): pl.pallas_call(kernel, out_shape=out_shapes, in_specs=[whole] * len(opera...  48.6 us
    ppermute x2, starting transfers between devices, widened(): low = lax.ppermute(block[:, :, NY - 1:], GY, forward)  13.2 us
    all_to_all x1, starting transfers between devices, on_device(): peaks = lax.all_to_all(peaks.reshape(devices, 1, SLOTS), EVERY, 0, 0)  11.9 us
    ppermute x4, starting transfers between devices, extended(): high = lax.ppermute(lax.slice_in_dim(block, 0, 1, axis=dim), axis, backward)  11.2 us
    ppermute x2, waiting for transfers between devices, widened(): high = lax.ppermute(block[:, :, :1], GY, backward)  6.02 us
    ppermute x4, waiting for transfers between devices, extended(): lax.ppermute(lax.slice_in_dim(block, size - 1, size, axis=dim), axis, for...  5.98 us
    ppermute x4, starting transfers between devices, extended(): lax.ppermute(lax.slice_in_dim(block, size - 1, size, axis=dim), axis, for...  3.22 us
  transfers between devices with their start and end apart: 13, of which 6 were waited for; matrix products, arithmetic and copies ran while one was open for 0% of the time, Pallas kernels for 17%

profile of v3, /device:TPU:8, one launch (start us, length us, event | category | flops | bytes accessed | tf_op | source)
XLA Modules:
  0.0 107.1 jit_solution(5462957013845184765)
XLA Ops:
  0.6 0.8 copy.8
  1.4 0.1 compare_convert_fusion
  1.5 0.0 copy-start.1
  1.5 0.0 copy-start.2
  1.5 0.8 broadcast_multiply_fusion
  2.4 0.0 copy-done.1
  2.4 0.0 copy-done.2
  2.4 0.1 pad_maximum_fusion.3
  2.5 0.1 collective-permute-start
  2.6 4.1 %collective-permute-start.1 = (f32[9,1,4,2,128]{4,3,2,1,0:T(2,128)S(1)}, f32[9,1,4,2,128]{4,3,2,1,0:T(2,128)S(1)}, u32[]{:S(2)}, u32[]{:S(2)}) collective-permute-start(f32[9,1,4,2,128]{4,3,2,1,0:T(2,128)S(1)} %get-tuple-element.17), channel_id=1, source_target_pairs={{32,0},{64,32},{96,64},{128,96},{160,128},{192,160},{224,192},{0,2... | collective-permute-start | bytes 110600 | tf_op jit(solution)/shard_map/ppermute | solution.py:43
  6.7 1.7 %collective-permute-done = f32[9,1,4,2,128]{4,3,2,1,0:T(2,128)S(1)} collective-permute-done((f32[9,1,4,2,128]{4,3,2,1,0:T(2,128)S(1)}, f32[9,1,4,2,128]{4,3,2,1,0:T(2,128)S(1)}, u32[]{:S(2)}, u32[]{:S(2)}) %collective-permute-start) | collective-permute-done | bytes 36896 | tf_op jit(solution)/shard_map/ppermute | solution.py:42
  8.4 0.0 collective-permute-done.1
  8.4 0.1 pad_maximum_fusion.1
  8.5 0.2 fusion.1
  8.7 1.6 %collective-permute-start.2 = (f32[9,6,4,1,128]{4,3,2,1,0:T(1,128)S(1)}, f32[9,6,4,1,128]{4,3,2,1,0:T(1,128)S(1)}, u32[]{:S(2)}, u32[]{:S(2)}) collective-permute-start(f32[9,6,4,1,128]{4,3,2,1,0:T(1,128)S(1)} %get-tuple-element.12), channel_id=1, source_target_pairs={{0,1},{1,2},{2,3},{3,0},{4,5},{5,6},{6,7},{7,4},{8,9},{9,10},{10,1... | collective-permute-start | bytes 331784 | tf_op jit(solution)/shard_map/ppermute | solution.py:42
  10.2 1.7 %collective-permute-start.3 = (f32[9,6,4,1,128]{4,3,2,1,0:T(1,128)S(1)}, f32[9,6,4,1,128]{4,3,2,1,0:T(1,128)S(1)}, u32[]{:S(2)}, u32[]{:S(2)}) collective-permute-start(f32[9,6,4,1,128]{4,3,2,1,0:T(1,128)S(1)} %get-tuple-element.13), channel_id=1, source_target_pairs={{1,0},{2,1},{3,2},{0,3},{5,4},{6,5},{7,6},{4,7},{9,8},{10,9},{11,1... | collective-permute-start | bytes 331784 | tf_op jit(solution)/shard_map/ppermute | solution.py:43
  12.0 2.9 %collective-permute-done.2 = f32[9,6,4,1,128]{4,3,2,1,0:T(1,128)S(1)} collective-permute-done((f32[9,6,4,1,128]{4,3,2,1,0:T(1,128)S(1)}, f32[9,6,4,1,128]{4,3,2,1,0:T(1,128)S(1)}, u32[]{:S(2)}, u32[]{:S(2)}) %collective-permute-start.2) | collective-permute-done | bytes 110624 | tf_op jit(solution)/shard_map/ppermute | solution.py:42
  14.9 0.1 collective-permute-done.3
  15.0 0.3 pad_maximum_fusion
  15.3 6.7 %collective-permute-start.4 = (f32[9,6,1,4,128]{4,3,2,1,0:T(4,128)S(1)}, f32[9,6,1,4,128]{4,3,2,1,0:T(4,128)S(1)}, u32[]{:S(2)}, u32[]{:S(2)}) collective-permute-start(f32[9,6,1,4,128]{4,3,2,1,0:T(4,128)S(1)} %get-tuple-element.10), channel_id=1, source_target_pairs={{0,4},{4,8},{8,12},{12,16},{16,20},{20,24},{24,28},{28,0},{1,5},{5... | collective-permute-start | bytes 331784 | tf_op jit(solution)/shard_map/ppermute | solution.py:386
  22.1 0.2 collective-permute-start.5
  22.3 18.3 %start_inner.1.sums_ref = f32[1280,128]{1,0:T(8,128)S(1)} custom-call(f32[9,96,128]{2,1,0:T(8,128)S(1)} %bitcast.16, f32[9,32,128]{2,1,0:T(8,128)S(1)} %bitcast.18), custom_call_target="tpu_custom_call" | custom-call | tf_op jit(solution)/shard_map/start_inner/pallas_call | solution.py:368
  40.6 0.0 copy-start
  40.6 0.0 collective-permute-done.4
  40.6 0.0 collective-permute-done.5
  40.6 0.1 pad_maximum_fusion.2
  40.7 0.6 copy-done
  41.3 6.0 %start_outer.1 = (f32[3,32,128]{2,1,0:T(8,128)S(1)}, f32[256,128]{1,0:T(8,128)}) custom-call(f32[9,48,128]{2,1,0:T(8,128)S(1)} %bitcast.22, f32[9,32,128]{2,1,0:T(8,128)S(1)} %bitcast.19, f32[32,128]{1,0:T(8,128)S(1)} %bitcast.31, f32[1280,128]{1,0:T(8,128)S(1)} %start_inner.1.sums_ref), custom_call_target="tpu_custom_call" | custom-call | tf_op jit(solution)/shard_map/start_outer/pallas_call | solution.py:368
  47.3 0.0 collective-permute-start.6
  47.3 3.5 %collective-permute-start.7 = (f32[3,1,4,2,128]{4,3,2,1,0:T(2,128)S(1)}, f32[3,1,4,2,128]{4,3,2,1,0:T(2,128)S(1)}, u32[]{:S(2)}, u32[]{:S(2)}) collective-permute-start(f32[3,1,4,2,128]{4,3,2,1,0:T(2,128)S(1)} %get-tuple-element.21), channel_id=1, source_target_pairs={{32,0},{64,32},{96,64},{128,96},{160,128},{192,160},{224,192},{0,2... | collective-permute-start | bytes 36872 | tf_op jit(solution)/shard_map/ppermute | solution.py:43
  50.8 1.4 %collective-permute-done.6 = f32[3,1,4,2,128]{4,3,2,1,0:T(2,128)S(1)} collective-permute-done((f32[3,1,4,2,128]{4,3,2,1,0:T(2,128)S(1)}, f32[3,1,4,2,128]{4,3,2,1,0:T(2,128)S(1)}, u32[]{:S(2)}, u32[]{:S(2)}) %collective-permute-start.6) | collective-permute-done | bytes 12320 | tf_op jit(solution)/shard_map/ppermute | solution.py:42
  52.2 0.0 collective-permute-done.7
  52.2 0.1 fusion.4
  52.3 1.6 %collective-permute-start.8 = (f32[3,6,4,1,128]{4,3,2,1,0:T(1,128)S(1)}, f32[3,6,4,1,128]{4,3,2,1,0:T(1,128)S(1)}, u32[]{:S(2)}, u32[]{:S(2)}) collective-permute-start(f32[3,6,4,1,128]{4,3,2,1,0:T(1,128)S(1)} %get-tuple-element.18), channel_id=1, source_target_pairs={{0,1},{1,2},{2,3},{3,0},{4,5},{5,6},{6,7},{7,4},{8,9},{9,10},{10,1... | collective-permute-start | bytes 110600 | tf_op jit(solution)/shard_map/ppermute | solution.py:42
  53.9 1.7 %collective-permute-start.9 = (f32[3,6,4,1,128]{4,3,2,1,0:T(1,128)S(1)}, f32[3,6,4,1,128]{4,3,2,1,0:T(1,128)S(1)}, u32[]{:S(2)}, u32[]{:S(2)}) collective-permute-start(f32[3,6,4,1,128]{4,3,2,1,0:T(1,128)S(1)} %get-tuple-element.19), channel_id=1, source_target_pairs={{1,0},{2,1},{3,2},{0,3},{5,4},{6,5},{7,6},{4,7},{9,8},{10,9},{11,1... | collective-permute-start | bytes 110600 | tf_op jit(solution)/shard_map/ppermute | solution.py:43
  55.6 11.9 %all-to-all-start = ((f32[256,1,128]{2,1,0:T(1,128)}), f32[256,1,128]{2,1,0:T(1,128)S(1)}, u32[]{:S(2)}, u32[]{:S(2)}) async-start(f32[256,1,128]{2,1,0:T(1,128)} %bitcast.7), calls=%async_computation | async-start | bytes 262144 | tf_op jit(solution)/shard_map/all_to_all | solution.py:406
  67.5 0.0 collective-permute-done.8
  67.5 0.0 collective-permute-done.9
  67.6 0.1 pad_maximum_fusion.4
  67.7 6.4 %collective-permute-start.10 = (f32[3,6,1,4,128]{4,3,2,1,0:T(4,128)S(1)}, f32[3,6,1,4,128]{4,3,2,1,0:T(4,128)S(1)}, u32[]{:S(2)}, u32[]{:S(2)}) collective-permute-start(f32[3,6,1,4,128]{4,3,2,1,0:T(4,128)S(1)} %get-tuple-element.14), channel_id=1, source_target_pairs={{0,4},{4,8},{8,12},{12,16},{16,20},{20,24},{24,28},{28,0},{1,5},{5... | collective-permute-start | bytes 110600 | tf_op jit(solution)/shard_map/ppermute | solution.py:386
  74.1 0.5 collective-permute-start.11
  74.6 2.1 %collective-permute-done.10 = f32[3,6,1,4,128]{4,3,2,1,0:T(4,128)S(1)} collective-permute-done((f32[3,6,1,4,128]{4,3,2,1,0:T(4,128)S(1)}, f32[3,6,1,4,128]{4,3,2,1,0:T(4,128)S(1)}, u32[]{:S(2)}, u32[]{:S(2)}) %collective-permute-start.10) | collective-permute-done | bytes 36896 | tf_op jit(solution)/shard_map/ppermute | solution.py:386
  76.7 6.0 %collective-permute-done.11 = f32[3,6,1,4,128]{4,3,2,1,0:T(4,128)S(1)} collective-permute-done((f32[3,6,1,4,128]{4,3,2,1,0:T(4,128)S(1)}, f32[3,6,1,4,128]{4,3,2,1,0:T(4,128)S(1)}, u32[]{:S(2)}, u32[]{:S(2)}) %collective-permute-start.11) | collective-permute-done | bytes 36896 | tf_op jit(solution)/shard_map/ppermute | solution.py:387
  82.7 0.0 all-to-all-done
  82.7 18.4 %end_inner.1.sums_ref = f32[1280,128]{1,0:T(8,128)S(1)} custom-call(f32[9,96,128]{2,1,0:T(8,128)S(1)} %bitcast.17, f32[9,32,128]{2,1,0:T(8,128)S(1)} %bitcast.20, f32[3,96,128]{2,1,0:T(8,128)S(1)} %bitcast.29, f32[3,32,128]{2,1,0:T(8,128)S(1)} %get-tuple-element.6.speed_ref, f32[256,128]{1,0:T(8,128)S(1)} %bitcast.24), custom_call_target="tpu_custom_call" | custom-call | tf_op jit(solution)/shard_map/end_inner/pallas_call | solution.py:368
  101.1 5.9 %end_outer.1 = (f32[3,32,128]{2,1,0:T(8,128)}, f32[3,32,128]{2,1,0:T(8,128)}) custom-call(f32[9,48,128]{2,1,0:T(8,128)S(1)} %bitcast.23, f32[9,32,128]{2,1,0:T(8,128)S(1)} %bitcast.21, f32[32,128]{1,0:T(8,128)S(1)} %bitcast.32, f32[3,48,128]{2,1,0:T(8,128)S(1)} %bitcast.30, f32[3,32,128]{2,1,0:T(8,128)S(1)} %get-tuple-element.6.speed_ref, ...), custom_call_target="tpu_custom_call" | custom-call | tf_op jit(solution)/shard_map/end_outer/pallas_call | solution.py:368
  (6 shorter events, 0.1 us)
Async XLA Ops:
  1.5 0.9 copy-start.1
  1.5 0.8 copy-start.2
  2.5 5.9 %collective-permute-start = (f32[9,1,4,2,128]{4,3,2,1,0:T(2,128)S(1)}, f32[9,1,4,2,128]{4,3,2,1,0:T(2,128)S(1)}, u32[]{:S(2)}, u32[]{:S(2)}) collective-permute-start(f32[9,1,4,2,128]{4,3,2,1,0:T(2,128)S(1)} %get-tuple-element.16), channel_id=1, source_target_pairs={{0,32},{32,64},{64,96},{96,128},{128,160},{160,192},{192,224},{224... | collective-permute-start | bytes 110600 | tf_op jit(solution)/shard_map/ppermute | solution.py:42
  2.6 5.8 %collective-permute-start.1 = (f32[9,1,4,2,128]{4,3,2,1,0:T(2,128)S(1)}, f32[9,1,4,2,128]{4,3,2,1,0:T(2,128)S(1)}, u32[]{:S(2)}, u32[]{:S(2)}) collective-permute-start(f32[9,1,4,2,128]{4,3,2,1,0:T(2,128)S(1)} %get-tuple-element.17), channel_id=1, source_target_pairs={{32,0},{64,32},{96,64},{128,96},{160,128},{192,160},{224,192},{0,2... | collective-permute-start | bytes 110600 | tf_op jit(solution)/shard_map/ppermute | solution.py:43
  8.7 6.3 %collective-permute-start.2 = (f32[9,6,4,1,128]{4,3,2,1,0:T(1,128)S(1)}, f32[9,6,4,1,128]{4,3,2,1,0:T(1,128)S(1)}, u32[]{:S(2)}, u32[]{:S(2)}) collective-permute-start(f32[9,6,4,1,128]{4,3,2,1,0:T(1,128)S(1)} %get-tuple-element.12), channel_id=1, source_target_pairs={{0,1},{1,2},{2,3},{3,0},{4,5},{5,6},{6,7},{7,4},{8,9},{9,10},{10,1... | collective-permute-start | bytes 331784 | tf_op jit(solution)/shard_map/ppermute | solution.py:42
  10.2 4.7 %collective-permute-start.3 = (f32[9,6,4,1,128]{4,3,2,1,0:T(1,128)S(1)}, f32[9,6,4,1,128]{4,3,2,1,0:T(1,128)S(1)}, u32[]{:S(2)}, u32[]{:S(2)}) collective-permute-start(f32[9,6,4,1,128]{4,3,2,1,0:T(1,128)S(1)} %get-tuple-element.13), channel_id=1, source_target_pairs={{1,0},{2,1},{3,2},{0,3},{5,4},{6,5},{7,6},{4,7},{9,8},{10,9},{11,1... | collective-permute-start | bytes 331784 | tf_op jit(solution)/shard_map/ppermute | solution.py:43
  15.3 25.2 %collective-permute-start.4 = (f32[9,6,1,4,128]{4,3,2,1,0:T(4,128)S(1)}, f32[9,6,1,4,128]{4,3,2,1,0:T(4,128)S(1)}, u32[]{:S(2)}, u32[]{:S(2)}) collective-permute-start(f32[9,6,1,4,128]{4,3,2,1,0:T(4,128)S(1)} %get-tuple-element.10), channel_id=1, source_target_pairs={{0,4},{4,8},{8,12},{12,16},{16,20},{20,24},{24,28},{28,0},{1,5},{5... | collective-permute-start | bytes 331784 | tf_op jit(solution)/shard_map/ppermute | solution.py:386
  22.1 18.5 %collective-permute-start.5 = (f32[9,6,1,4,128]{4,3,2,1,0:T(4,128)S(1)}, f32[9,6,1,4,128]{4,3,2,1,0:T(4,128)S(1)}, u32[]{:S(2)}, u32[]{:S(2)}) collective-permute-start(f32[9,6,1,4,128]{4,3,2,1,0:T(4,128)S(1)} %get-tuple-element.11), channel_id=1, source_target_pairs={{4,0},{8,4},{12,8},{16,12},{20,16},{24,20},{28,24},{0,28},{5,1},{9... | collective-permute-start | bytes 331784 | tf_op jit(solution)/shard_map/ppermute | solution.py:387
  40.6 0.7 copy-start
  47.3 4.9 %collective-permute-start.6 = (f32[3,1,4,2,128]{4,3,2,1,0:T(2,128)S(1)}, f32[3,1,4,2,128]{4,3,2,1,0:T(2,128)S(1)}, u32[]{:S(2)}, u32[]{:S(2)}) collective-permute-start(f32[3,1,4,2,128]{4,3,2,1,0:T(2,128)S(1)} %get-tuple-element.20), channel_id=1, source_target_pairs={{0,32},{32,64},{64,96},{96,128},{128,160},{160,192},{192,224},{224... | collective-permute-start | bytes 36872 | tf_op jit(solution)/shard_map/ppermute | solution.py:42
  47.3 4.9 %collective-permute-start.7 = (f32[3,1,4,2,128]{4,3,2,1,0:T(2,128)S(1)}, f32[3,1,4,2,128]{4,3,2,1,0:T(2,128)S(1)}, u32[]{:S(2)}, u32[]{:S(2)}) collective-permute-start(f32[3,1,4,2,128]{4,3,2,1,0:T(2,128)S(1)} %get-tuple-element.21), channel_id=1, source_target_pairs={{32,0},{64,32},{96,64},{128,96},{160,128},{192,160},{224,192},{0,2... | collective-permute-start | bytes 36872 | tf_op jit(solution)/shard_map/ppermute | solution.py:43
  52.3 15.2 %collective-permute-start.8 = (f32[3,6,4,1,128]{4,3,2,1,0:T(1,128)S(1)}, f32[3,6,4,1,128]{4,3,2,1,0:T(1,128)S(1)}, u32[]{:S(2)}, u32[]{:S(2)}) collective-permute-start(f32[3,6,4,1,128]{4,3,2,1,0:T(1,128)S(1)} %get-tuple-element.18), channel_id=1, source_target_pairs={{0,1},{1,2},{2,3},{3,0},{4,5},{5,6},{6,7},{7,4},{8,9},{9,10},{10,1... | collective-permute-start | bytes 110600 | tf_op jit(solution)/shard_map/ppermute | solution.py:42
  53.9 13.7 %collective-permute-start.9 = (f32[3,6,4,1,128]{4,3,2,1,0:T(1,128)S(1)}, f32[3,6,4,1,128]{4,3,2,1,0:T(1,128)S(1)}, u32[]{:S(2)}, u32[]{:S(2)}) collective-permute-start(f32[3,6,4,1,128]{4,3,2,1,0:T(1,128)S(1)} %get-tuple-element.19), channel_id=1, source_target_pairs={{1,0},{2,1},{3,2},{0,3},{5,4},{6,5},{7,6},{4,7},{9,8},{10,9},{11,1... | collective-permute-start | bytes 110600 | tf_op jit(solution)/shard_map/ppermute | solution.py:43
  55.6 27.1 %all-to-all-start = ((f32[256,1,128]{2,1,0:T(1,128)}), f32[256,1,128]{2,1,0:T(1,128)S(1)}, u32[]{:S(2)}, u32[]{:S(2)}) async-start(f32[256,1,128]{2,1,0:T(1,128)} %bitcast.7), calls=%async_computation | async-start | bytes 262144 | tf_op jit(solution)/shard_map/all_to_all | solution.py:406
  67.7 9.0 %collective-permute-start.10 = (f32[3,6,1,4,128]{4,3,2,1,0:T(4,128)S(1)}, f32[3,6,1,4,128]{4,3,2,1,0:T(4,128)S(1)}, u32[]{:S(2)}, u32[]{:S(2)}) collective-permute-start(f32[3,6,1,4,128]{4,3,2,1,0:T(4,128)S(1)} %get-tuple-element.14), channel_id=1, source_target_pairs={{0,4},{4,8},{8,12},{12,16},{16,20},{20,24},{24,28},{28,0},{1,5},{5... | collective-permute-start | bytes 110600 | tf_op jit(solution)/shard_map/ppermute | solution.py:386
  74.1 8.6 %collective-permute-start.11 = (f32[3,6,1,4,128]{4,3,2,1,0:T(4,128)S(1)}, f32[3,6,1,4,128]{4,3,2,1,0:T(4,128)S(1)}, u32[]{:S(2)}, u32[]{:S(2)}) collective-permute-start(f32[3,6,1,4,128]{4,3,2,1,0:T(4,128)S(1)} %get-tuple-element.15), channel_id=1, source_target_pairs={{4,0},{8,4},{12,8},{16,12},{20,16},{24,20},{28,24},{0,28},{5,1},{9... | collective-permute-start | bytes 110600 | tf_op jit(solution)/shard_map/ppermute | solution.py:387

commit v4 on v3

--- a/solution.py
+++ b/solution.py
@@ -70,26 +70,27 @@
     return rows + [jnp.zeros_like(one)] * (KF - len(rows))
 
 
-def prepare_sources(pad_ref, shift, pf, vf, inner):
+def prepare_sources(pad_ref, shift, pf, vf, rim=None):
     sub = lax.broadcasted_iota(jnp.int32, (8, SLOTS), 0)
-    y_in = (sub >> 2).astype(F32)
+    two = (sub >> 2).astype(F32)
     z_in = (sub & 3).astype(F32)
+    first = 0 if rim is None else rim * PX * PZ
 
     def group(g, carry):
         rows = pl.ds(pl.multiple_of(g * 8, 8), 8)
-        if inner:
-            x0 = (g // 2).astype(F32) - float(PX // 2)
-            y_at = y_in + (((g % 2) * 2 + 1).astype(F32) - float(PY // 2))
+        if rim is None:
+            x_at = (g // 2).astype(F32) - float(PX // 2)
+            y_at = two + (((g % 2) * 2 + 1).astype(F32) - float(PY // 2))
         else:
-            x0 = g.astype(F32) - float(PX // 2)
-            y_at = y_in * float(PY - 1) - float(PY // 2)
+            x_at = two + ((g * 2).astype(F32) - float(PX // 2))
+            y_at = float(rim * (PY - 1) - PY // 2)
         pos = [pad_ref[a, rows, :] for a in range(3)]
         if shift is not None:
             padv_ref, step = shift
             pos = [pos[a] + step * padv_ref[a, rows, :] for a in range(3)]
-        coords = [pos[0] + x0, pos[1] + y_at, pos[2] + (z_in - float(PZ // 2))]
+        coords = [pos[0] + x_at, pos[1] + y_at, pos[2] + (z_in - float(PZ // 2))]
         for f, row in enumerate(distance_features(coords, True)):
-            pf[pl.ds(g * (8 * KF) + f, 8, stride=KF), :] = row
+            pf[pl.ds(first * KF + g * (8 * KF) + f, 8, stride=KF), :] = row
         line = [pad_ref[3 + a, rows, :] for a in range(3)]
         burg = [pad_ref[6 + a, rows, :] for a in range(3)]
         outer = [[burg[m] * line[n] for n in range(3)] for m in range(3)]
@@ -97,22 +98,22 @@
             for n in range(3):
                 b = outer[m][n] - CROSS_WEIGHT * outer[n][m]
                 f = 3 * m + n
-                vf[pl.ds(g * (8 * VF) + f, 8, stride=VF), :] = b
+                vf[pl.ds(first * VF + g * (8 * VF) + f, 8, stride=VF), :] = b
                 for a in range(3):
-                    at = g * (8 * VF) + 9 * (a + 1) + f
+                    at = first * VF + g * (8 * VF) + 9 * (a + 1) + f
                     vf[pl.ds(at, 8, stride=VF), :] = b * coords[a]
         return carry
 
     lax.fori_loop(0, pad_ref.shape[1] // 8, group, 0)
 
 
-def lay_out_sources(pf, vf, pt, vt):
+def lay_out_sources(pf, vf, pt, vt, inner):
     across = vt.shape[3] // SLOTS
 
     def column(c, carry):
         at = pl.multiple_of(c * 128, 128)
         pt[pl.ds(at, 128), :] = pf[pl.ds(at, 128), :].T.astype(BF16)
-        x, y = c // across, c % across
+        x, y = (c // across, c % across) if inner else (c % PX, c // PX)
         lanes = pl.ds(pl.multiple_of(y * SLOTS, SLOTS), SLOTS)
         for z in range(PZ):
             v = vf[pl.ds(pl.multiple_of(c * (PZ * VF) + z * VF, 8), VF), :]
@@ -205,7 +206,8 @@
             q = [query(*target) for target in targets]
             made = []
             for dx, first, count, s, to_left, to_right in runs:
-                at = ((x + dx) * across + first) * SLOTS
+                at = (x + dx) * across + first if inner else first * PX + x + dx
+                at = at * SLOTS
                 source = pt[pl.ds(pl.multiple_of(at, SLOTS), count * SLOTS), :]
                 rows = [zero] * PZ
                 rows[s] = jnp.concatenate(q, 1)
@@ -296,25 +298,27 @@
 
 
 def start_inner(pad_ref, loc_ref, sums_ref, pf, vf, pt, vt, qf):
-    prepare_sources(pad_ref, None, pf, vf, True)
-    lay_out_sources(pf, vf, pt, vt)
+    prepare_sources(pad_ref, None, pf, vf)
+    lay_out_sources(pf, vf, pt, vt, True)
     prepare_targets(loc_ref, None, qf)
     pair_sums(pt, vt, qf, sums_ref, True)
 
 
 def end_inner(pad_ref, loc_ref, padv_ref, speed_ref, peak_ref, sums_ref, pf, vf, pt, vt, qf):
     step = step_of(peak_ref)
-    prepare_sources(pad_ref, (padv_ref, step), pf, vf, True)
-    lay_out_sources(pf, vf, pt, vt)
+    prepare_sources(pad_ref, (padv_ref, step), pf, vf)
+    lay_out_sources(pf, vf, pt, vt, True)
     prepare_targets(loc_ref, (speed_ref, step), qf)
     pair_sums(pt, vt, qf, sums_ref, True)
 
 
 def start_outer(
-    rim_ref, loc_ref, mob_ref, sums_ref, speed_ref, peak_ref, pf, vf, pt, vt, qf, tf
+    low_ref, high_ref, loc_ref, mob_ref, sums_ref, speed_ref, peak_ref,
+    pf, vf, pt, vt, qf, tf,
 ):
-    prepare_sources(rim_ref, None, pf, vf, False)
-    lay_out_sources(pf, vf, pt, vt)
+    prepare_sources(low_ref, None, pf, vf, 0)
+    prepare_sources(high_ref, None, pf, vf, 1)
+    lay_out_sources(pf, vf, pt, vt, False)
     every = prepare_targets(loc_ref, None, qf)
     pair_sums(pt, vt, qf, tf, False, sums_ref)
     peak = jnp.zeros((8, SLOTS), F32)
@@ -333,12 +337,14 @@
 
 
 def end_outer(
-    rim_ref, loc_ref, mob_ref, rimv_ref, speed_ref, peak_ref, sums_ref, moved_ref, force_ref,
+    low_ref, high_ref, loc_ref, mob_ref, lowv_ref, highv_ref, speed_ref, peak_ref, sums_ref,
+    moved_ref, force_ref,
     pf, vf, pt, vt, qf, tf,
 ):
     step = step_of(peak_ref)
-    prepare_sources(rim_ref, (rimv_ref, step), pf, vf, False)
-    lay_out_sources(pf, vf, pt, vt)
+    prepare_sources(low_ref, (lowv_ref, step), pf, vf, 0)
+    prepare_sources(high_ref, (highv_ref, step), pf, vf, 1)
+    lay_out_sources(pf, vf, pt, vt, False)
     every = prepare_targets(loc_ref, (speed_ref, step), qf)
     pair_sums(pt, vt, qf, tf, False, sums_ref)
     for g in range(CELLS // 8):
@@ -385,9 +391,8 @@
     forward, backward = ring(GY)
     low = lax.ppermute(block[:, :, NY - 1 :], GY, forward)
     high = lax.ppermute(block[:, :, :1], GY, backward)
-    rim = jnp.concatenate([low, high], 2)
-    count = block.shape[0]
-    return block.reshape(count, PX * NY * PZ, SLOTS), rim.reshape(count, PX * 2 * PZ, SLOTS)
+    rim = [plane.reshape(-1, PX * PZ, SLOTS) for plane in (low, high)]
+    return block.reshape(-1, PX * NY * PZ, SLOTS), rim
 
 
 def on_device(positions, line_vectors, burgers, mobility, occupancy):
@@ -401,14 +406,14 @@
     peaks = jax.ShapeDtypeStruct((devices, SLOTS), F32)
     (sums,) = call(start_inner, [SUMS], [pad, loc], "start_inner", True)
     speed, peaks = call(
-        start_outer, [VEC, peaks], [rim, loc, mob, sums], "start_outer", False
+        start_outer, [VEC, peaks], [*rim, loc, mob, sums], "start_outer", False
     )
     peaks = lax.all_to_all(peaks.reshape(devices, 1, SLOTS), EVERY, 0, 0)
     peaks = peaks.reshape(devices, SLOTS)
     padv, rimv = widened(speed.reshape(3, NX, NY, NZ, SLOTS))
     (sums,) = call(end_inner, [SUMS], [pad, loc, padv, speed, peaks], "end_inner", True)
     moved, force = call(
-        end_outer, [VEC, VEC], [rim, loc, mob, rimv, speed, peaks, sums], "end_outer", False
+        end_outer, [VEC, VEC], [*rim, loc, mob, *rimv, speed, peaks, sums], "end_outer", False
     )
     shape = (3, NX, NY, NZ, SLOTS)
     return moved.reshape(shape), force.reshape(shape)

time: 107 us -> 108 us (level); the launches traced: 107 us -> 106 us
  waiting for transfers between devices: 14.2 us -> 11.6 us
  starting transfers between devices: 40.1 us -> 41.9 us
    ppermute x2, starting transfers between devices: 13.2 us -> 0.36 us  [widened(): low = lax.ppermute(block[:, :, NY - 1:], GY, forward)]
    ppermute x2, starting transfers between devices: 0.64 us -> 13 us  [widened(): high = lax.ppermute(block[:, :, :1], GY, backward)]
    ppermute x2, waiting for transfers between devices: 6.02 us -> 0.01 us  [widened(): high = lax.ppermute(block[:, :, :1], GY, backward)]
    all_to_all x1, waiting for transfers between devices: 0.01 us -> 5.5 us  [on_device(): peaks = lax.all_to_all(peaks.reshape(devices, 1, SLOTS), EVERY, 0, 0)]
    ppermute x2, waiting for transfers between devices: 2.09 us -> 0.01 us  [widened(): low = lax.ppermute(block[:, :, NY - 1:], GY, forward)]
    all_to_all x1, starting transfers between devices: 11.9 us -> 13.9 us  [on_device(): peaks = lax.all_to_all(peaks.reshape(devices, 1, SLOTS), EVERY, 0, 0)]
  transfers between devices with their start and end apart: 13 -> 13, of which waited for: 6 -> 5; matrix products, arithmetic and copies ran while one was open for 0% -> 0% of each run, Pallas kernels for 17% -> 35%
where the time goes in v4:
time: 108 us; the launch traced here: 106 us
  Pallas kernels  48.6 us (45%)
  starting transfers between devices  41.9 us (39%)
  waiting for transfers between devices  11.6 us (11%)
  other arithmetic  1.52 us (1%)
  local copies, waits for them, and re-layouts  1.18 us (1%)
    pallas_call x4, Pallas kernels, call(): pl.pallas_call(kernel, out_shape=out_shapes, in_specs=[whole] * len(opera...  48.6 us
    all_to_all x1, starting transfers between devices, on_device(): peaks = lax.all_to_all(peaks.reshape(devices, 1, SLOTS), EVERY, 0, 0)  13.9 us
    ppermute x2, starting transfers between devices, widened(): high = lax.ppermute(block[:, :, :1], GY, backward)  13 us
    ppermute x4, starting transfers between devices, extended(): high = lax.ppermute(lax.slice_in_dim(block, 0, 1, axis=dim), axis, backward)  11.2 us
    ppermute x4, waiting for transfers between devices, extended(): lax.ppermute(lax.slice_in_dim(block, size - 1, size, axis=dim), axis, for...  5.97 us
    all_to_all x1, waiting for transfers between devices, on_device(): peaks = lax.all_to_all(peaks.reshape(devices, 1, SLOTS), EVERY, 0, 0)  5.5 us
    ppermute x4, starting transfers between devices, extended(): lax.ppermute(lax.slice_in_dim(block, size - 1, size, axis=dim), axis, for...  3.48 us
  transfers between devices with their start and end apart: 13, of which 5 were waited for; matrix products, arithmetic and copies ran while one was open for 0% of the time, Pallas kernels for 35%

profile of v4, /device:TPU:8, one launch (start us, length us, event | category | flops | bytes accessed | tf_op | source)
XLA Modules:
  0.0 105.6 jit_solution(15592830768264426942)
XLA Ops:
  0.6 0.8 copy.12
  1.4 0.1 compare_convert_fusion
  1.5 0.0 copy-start.1
  1.5 0.0 copy-start.2
  1.5 0.8 broadcast_multiply_fusion
  2.4 0.0 copy-done.1
  2.4 0.0 copy-done.2
  2.4 0.1 pad_maximum_fusion.2
  2.5 0.1 collective-permute-start
  2.6 4.1 %collective-permute-start.1 = (f32[9,1,4,2,128]{4,3,2,1,0:T(2,128)S(1)}, f32[9,1,4,2,128]{4,3,2,1,0:T(2,128)S(1)}, u32[]{:S(2)}, u32[]{:S(2)}) collective-permute-start(f32[9,1,4,2,128]{4,3,2,1,0:T(2,128)S(1)} %get-tuple-element.17), channel_id=1, source_target_pairs={{32,0},{64,32},{96,64},{128,96},{160,128},{192,160},{224,192},{0,2... | collective-permute-start | bytes 110600 | tf_op jit(solution)/shard_map/ppermute | solution.py:43
  6.7 1.7 %collective-permute-done = f32[9,1,4,2,128]{4,3,2,1,0:T(2,128)S(1)} collective-permute-done((f32[9,1,4,2,128]{4,3,2,1,0:T(2,128)S(1)}, f32[9,1,4,2,128]{4,3,2,1,0:T(2,128)S(1)}, u32[]{:S(2)}, u32[]{:S(2)}) %collective-permute-start) | collective-permute-done | bytes 36896 | tf_op jit(solution)/shard_map/ppermute | solution.py:42
  8.4 0.0 collective-permute-done.1
  8.4 0.1 pad_maximum_fusion.1
  8.5 0.2 fusion.1
  8.7 1.6 %collective-permute-start.2 = (f32[9,6,4,1,128]{4,3,2,1,0:T(1,128)S(1)}, f32[9,6,4,1,128]{4,3,2,1,0:T(1,128)S(1)}, u32[]{:S(2)}, u32[]{:S(2)}) collective-permute-start(f32[9,6,4,1,128]{4,3,2,1,0:T(1,128)S(1)} %get-tuple-element.12), channel_id=1, source_target_pairs={{0,1},{1,2},{2,3},{3,0},{4,5},{5,6},{6,7},{7,4},{8,9},{9,10},{10,1... | collective-permute-start | bytes 331784 | tf_op jit(solution)/shard_map/ppermute | solution.py:42
  10.2 1.7 %collective-permute-start.3 = (f32[9,6,4,1,128]{4,3,2,1,0:T(1,128)S(1)}, f32[9,6,4,1,128]{4,3,2,1,0:T(1,128)S(1)}, u32[]{:S(2)}, u32[]{:S(2)}) collective-permute-start(f32[9,6,4,1,128]{4,3,2,1,0:T(1,128)S(1)} %get-tuple-element.13), channel_id=1, source_target_pairs={{1,0},{2,1},{3,2},{0,3},{5,4},{6,5},{7,6},{4,7},{9,8},{10,9},{11,1... | collective-permute-start | bytes 331784 | tf_op jit(solution)/shard_map/ppermute | solution.py:43
  12.0 2.9 %collective-permute-done.2 = f32[9,6,4,1,128]{4,3,2,1,0:T(1,128)S(1)} collective-permute-done((f32[9,6,4,1,128]{4,3,2,1,0:T(1,128)S(1)}, f32[9,6,4,1,128]{4,3,2,1,0:T(1,128)S(1)}, u32[]{:S(2)}, u32[]{:S(2)}) %collective-permute-start.2) | collective-permute-done | bytes 110624 | tf_op jit(solution)/shard_map/ppermute | solution.py:42
  14.9 0.1 collective-permute-done.3
  15.0 0.3 pad_maximum_fusion
  15.3 6.6 %collective-permute-start.5 = (f32[9,6,1,4,128]{4,3,2,1,0:T(4,128)S(1)}, f32[9,6,1,4,128]{4,3,2,1,0:T(4,128)S(1)}, u32[]{:S(2)}, u32[]{:S(2)}) collective-permute-start(f32[9,6,1,4,128]{4,3,2,1,0:T(4,128)S(1)} %get-tuple-element.10), channel_id=1, source_target_pairs={{4,0},{8,4},{12,8},{16,12},{20,16},{24,20},{28,24},{0,28},{5,1},{9... | collective-permute-start | bytes 331784 | tf_op jit(solution)/shard_map/ppermute | solution.py:393
  22.0 0.2 collective-permute-start.4
  22.2 0.0 copy-start
  22.2 18.3 %start_inner.1.sums_ref = f32[1280,128]{1,0:T(8,128)S(1)} custom-call(f32[9,96,128]{2,1,0:T(8,128)S(1)} %bitcast.18, f32[9,32,128]{2,1,0:T(8,128)S(1)} %bitcast.20), custom_call_target="tpu_custom_call" | custom-call | tf_op jit(solution)/shard_map/start_inner/pallas_call | solution.py:374
  40.5 0.0 collective-permute-done.5
  40.5 0.0 collective-permute-done.4
  40.5 0.0 copy-done
  40.5 6.0 %start_outer.1 = (f32[3,32,128]{2,1,0:T(8,128)S(1)}, f32[256,128]{1,0:T(8,128)}) custom-call(f32[9,24,128]{2,1,0:T(8,128)S(1)} %bitcast.31, f32[9,24,128]{2,1,0:T(8,128)S(1)} %bitcast.29, f32[9,32,128]{2,1,0:T(8,128)S(1)} %bitcast.21, f32[32,128]{1,0:T(8,128)S(1)} %bitcast.33, f32[1280,128]{1,0:T(8,128)S(1)} %start_inner.1.sums_ref), custom_call_target="tpu_custom_call" | custom-call | tf_op jit(solution)/shard_map/start_outer/pallas_call | solution.py:374
  46.5 0.3 collective-permute-start.6
  46.8 3.5 %collective-permute-start.7 = (f32[3,1,4,2,128]{4,3,1,0,2:T(2,128)S(1)}, f32[3,1,4,2,128]{4,3,1,0,2:T(2,128)S(1)}, u32[]{:S(2)}, u32[]{:S(2)}) collective-permute-start(f32[3,1,4,2,128]{4,3,1,0,2:T(2,128)S(1)} %copy.20), channel_id=1, source_target_pairs={{32,0},{64,32},{96,64},{128,96},{160,128},{192,160},{224,192},{0,2... | collective-permute-start | bytes 36872 | tf_op jit(solution)/shard_map/ppermute | solution.py:43
  50.3 1.4 %collective-permute-done.6 = f32[3,1,4,2,128]{4,3,1,0,2:T(2,128)S(1)} collective-permute-done((f32[3,1,4,2,128]{4,3,1,0,2:T(2,128)S(1)}, f32[3,1,4,2,128]{4,3,1,0,2:T(2,128)S(1)}, u32[]{:S(2)}, u32[]{:S(2)}) %collective-permute-start.6) | collective-permute-done | bytes 12320 | tf_op jit(solution)/shard_map/ppermute | solution.py:42
  51.7 0.0 collective-permute-done.7
  51.7 0.1 fusion.4
  51.8 1.6 %collective-permute-start.8 = (f32[3,6,4,1,128]{4,3,1,0,2:T(1,128)S(1)}, f32[3,6,4,1,128]{4,3,1,0,2:T(1,128)S(1)}, u32[]{:S(2)}, u32[]{:S(2)}) collective-permute-start(f32[3,6,4,1,128]{4,3,1,0,2:T(1,128)S(1)} %get-tuple-element.18), channel_id=1, source_target_pairs={{0,1},{1,2},{2,3},{3,0},{4,5},{5,6},{6,7},{7,4},{8,9},{9,10},{10,1... | collective-permute-start | bytes 110600 | tf_op jit(solution)/shard_map/ppermute | solution.py:42
  53.4 1.7 %collective-permute-start.9 = (f32[3,6,4,1,128]{4,3,1,0,2:T(1,128)S(1)}, f32[3,6,4,1,128]{4,3,1,0,2:T(1,128)S(1)}, u32[]{:S(2)}, u32[]{:S(2)}) collective-permute-start(f32[3,6,4,1,128]{4,3,1,0,2:T(1,128)S(1)} %get-tuple-element.19), channel_id=1, source_target_pairs={{1,0},{2,1},{3,2},{0,3},{5,4},{6,5},{7,6},{4,7},{9,8},{10,9},{11,1... | collective-permute-start | bytes 110600 | tf_op jit(solution)/shard_map/ppermute | solution.py:43
  55.1 13.9 %all-to-all-start = ((f32[256,1,128]{2,1,0:T(1,128)}), f32[256,1,128]{2,1,0:T(1,128)S(1)}, u32[]{:S(2)}, u32[]{:S(2)}) async-start(f32[256,1,128]{2,1,0:T(1,128)} %bitcast.9), calls=%async_computation | async-start | bytes 262144 | tf_op jit(solution)/shard_map/all_to_all | solution.py:411
  69.0 0.0 collective-permute-done.8
  69.0 0.0 collective-permute-done.9
  69.0 0.1 pad_maximum_fusion.3
  69.2 6.4 %collective-permute-start.11 = (f32[3,6,1,4,128]{4,3,1,0,2:T(4,128)S(1)}, f32[3,6,1,4,128]{4,3,1,0,2:T(4,128)S(1)}, u32[]{:S(2)}, u32[]{:S(2)}) collective-permute-start(f32[3,6,1,4,128]{4,3,1,0,2:T(4,128)S(1)} %get-tuple-element.14), channel_id=1, source_target_pairs={{4,0},{8,4},{12,8},{16,12},{20,16},{24,20},{28,24},{0,28},{5,1},{9... | collective-permute-start | bytes 110600 | tf_op jit(solution)/shard_map/ppermute | solution.py:393
  75.5 0.2 collective-permute-start.10
  75.7 5.5 %all-to-all-done = f32[256,1,128]{2,1,0:T(1,128)S(1)} async-done(((f32[256,1,128]{2,1,0:T(1,128)}), f32[256,1,128]{2,1,0:T(1,128)S(1)}, u32[]{:S(2)}, u32[]{:S(2)}) %all-to-all-start) | async-done | bytes 131104 | tf_op jit(solution)/shard_map/all_to_all | solution.py:411
  81.2 18.4 %end_inner.1.sums_ref = f32[1280,128]{1,0:T(8,128)S(1)} custom-call(f32[9,96,128]{2,1,0:T(8,128)S(1)} %bitcast.19, f32[9,32,128]{2,1,0:T(8,128)S(1)} %bitcast.22, f32[3,96,128]{2,1,0:T(8,128)S(1)} %bitcast.28, f32[3,32,128]{2,1,0:T(8,128)S(1)} %get-tuple-element.6.speed_ref, f32[256,128]{1,0:T(8,128)S(1)} %bitcast.24), custom_call_target="tpu_custom_call" | custom-call | tf_op jit(solution)/shard_map/end_inner/pallas_call | solution.py:374
  99.6 0.0 collective-permute-done.11
  99.6 0.0 collective-permute-done.10
  99.7 6.0 %end_outer.1 = (f32[3,32,128]{2,1,0:T(8,128)}, f32[3,32,128]{2,1,0:T(8,128)}) custom-call(f32[9,24,128]{2,1,0:T(8,128)S(1)} %bitcast.32, f32[9,24,128]{2,1,0:T(8,128)S(1)} %bitcast.30, f32[9,32,128]{2,1,0:T(8,128)S(1)} %bitcast.23, f32[32,128]{1,0:T(8,128)S(1)} %bitcast.34, f32[3,24,128]{2,1,0:T(8,128)S(1)} %bitcast.36, f32[3,24,128]{2,1,0:T(8,128)S(1)} %bitcast.35, ...), custom_call_target="tpu_custom_call" | custom-call | tf_op jit(solution)/shard_map/end_outer/pallas_call | solution.py:374
  (10 shorter events, 0.1 us)
Async XLA Ops:
  1.5 0.9 copy-start.1
  1.5 0.8 copy-start.2
  2.5 5.9 %collective-permute-start = (f32[9,1,4,2,128]{4,3,2,1,0:T(2,128)S(1)}, f32[9,1,4,2,128]{4,3,2,1,0:T(2,128)S(1)}, u32[]{:S(2)}, u32[]{:S(2)}) collective-permute-start(f32[9,1,4,2,128]{4,3,2,1,0:T(2,128)S(1)} %get-tuple-element.16), channel_id=1, source_target_pairs={{0,32},{32,64},{64,96},{96,128},{128,160},{160,192},{192,224},{224... | collective-permute-start | bytes 110600 | tf_op jit(solution)/shard_map/ppermute | solution.py:42
  2.6 5.8 %collective-permute-start.1 = (f32[9,1,4,2,128]{4,3,2,1,0:T(2,128)S(1)}, f32[9,1,4,2,128]{4,3,2,1,0:T(2,128)S(1)}, u32[]{:S(2)}, u32[]{:S(2)}) collective-permute-start(f32[9,1,4,2,128]{4,3,2,1,0:T(2,128)S(1)} %get-tuple-element.17), channel_id=1, source_target_pairs={{32,0},{64,32},{96,64},{128,96},{160,128},{192,160},{224,192},{0,2... | collective-permute-start | bytes 110600 | tf_op jit(solution)/shard_map/ppermute | solution.py:43
  8.7 6.3 %collective-permute-start.2 = (f32[9,6,4,1,128]{4,3,2,1,0:T(1,128)S(1)}, f32[9,6,4,1,128]{4,3,2,1,0:T(1,128)S(1)}, u32[]{:S(2)}, u32[]{:S(2)}) collective-permute-start(f32[9,6,4,1,128]{4,3,2,1,0:T(1,128)S(1)} %get-tuple-element.12), channel_id=1, source_target_pairs={{0,1},{1,2},{2,3},{3,0},{4,5},{5,6},{6,7},{7,4},{8,9},{9,10},{10,1... | collective-permute-start | bytes 331784 | tf_op jit(solution)/shard_map/ppermute | solution.py:42
  10.2 4.7 %collective-permute-start.3 = (f32[9,6,4,1,128]{4,3,2,1,0:T(1,128)S(1)}, f32[9,6,4,1,128]{4,3,2,1,0:T(1,128)S(1)}, u32[]{:S(2)}, u32[]{:S(2)}) collective-permute-start(f32[9,6,4,1,128]{4,3,2,1,0:T(1,128)S(1)} %get-tuple-element.13), channel_id=1, source_target_pairs={{1,0},{2,1},{3,2},{0,3},{5,4},{6,5},{7,6},{4,7},{9,8},{10,9},{11,1... | collective-permute-start | bytes 331784 | tf_op jit(solution)/shard_map/ppermute | solution.py:43
  15.3 25.1 %collective-permute-start.5 = (f32[9,6,1,4,128]{4,3,2,1,0:T(4,128)S(1)}, f32[9,6,1,4,128]{4,3,2,1,0:T(4,128)S(1)}, u32[]{:S(2)}, u32[]{:S(2)}) collective-permute-start(f32[9,6,1,4,128]{4,3,2,1,0:T(4,128)S(1)} %get-tuple-element.10), channel_id=1, source_target_pairs={{4,0},{8,4},{12,8},{16,12},{20,16},{24,20},{28,24},{0,28},{5,1},{9... | collective-permute-start | bytes 331784 | tf_op jit(solution)/shard_map/ppermute | solution.py:393
  22.0 18.5 %collective-permute-start.4 = (f32[9,6,1,4,128]{4,3,2,1,0:T(4,128)S(1)}, f32[9,6,1,4,128]{4,3,2,1,0:T(4,128)S(1)}, u32[]{:S(2)}, u32[]{:S(2)}) collective-permute-start(f32[9,6,1,4,128]{4,3,2,1,0:T(4,128)S(1)} %get-tuple-element.11), channel_id=1, source_target_pairs={{0,4},{4,8},{8,12},{12,16},{16,20},{20,24},{24,28},{28,0},{1,5},{5... | collective-permute-start | bytes 331784 | tf_op jit(solution)/shard_map/ppermute | solution.py:392
  22.2 18.3 %copy-start = (f32[4,4,2,128]{3,2,1,0:T(2,128)S(1)}, f32[4,4,2,128]{3,2,1,0:T(2,128)}, u32[]{:S(2)}) copy-start(f32[4,4,2,128]{3,2,1,0:T(2,128)} %param.8) | copy-start | bytes 49156
  46.5 5.2 %collective-permute-start.6 = (f32[3,1,4,2,128]{4,3,1,0,2:T(2,128)S(1)}, f32[3,1,4,2,128]{4,3,1,0,2:T(2,128)S(1)}, u32[]{:S(2)}, u32[]{:S(2)}) collective-permute-start(f32[3,1,4,2,128]{4,3,1,0,2:T(2,128)S(1)} %copy.19), channel_id=1, source_target_pairs={{0,32},{32,64},{64,96},{96,128},{128,160},{160,192},{192,224},{224... | collective-permute-start | bytes 36872 | tf_op jit(solution)/shard_map/ppermute | solution.py:42
  46.8 4.9 %collective-permute-start.7 = (f32[3,1,4,2,128]{4,3,1,0,2:T(2,128)S(1)}, f32[3,1,4,2,128]{4,3,1,0,2:T(2,128)S(1)}, u32[]{:S(2)}, u32[]{:S(2)}) collective-permute-start(f32[3,1,4,2,128]{4,3,1,0,2:T(2,128)S(1)} %copy.20), channel_id=1, source_target_pairs={{32,0},{64,32},{96,64},{128,96},{160,128},{192,160},{224,192},{0,2... | collective-permute-start | bytes 36872 | tf_op jit(solution)/shard_map/ppermute | solution.py:43
  51.8 17.2 %collective-permute-start.8 = (f32[3,6,4,1,128]{4,3,1,0,2:T(1,128)S(1)}, f32[3,6,4,1,128]{4,3,1,0,2:T(1,128)S(1)}, u32[]{:S(2)}, u32[]{:S(2)}) collective-permute-start(f32[3,6,4,1,128]{4,3,1,0,2:T(1,128)S(1)} %get-tuple-element.18), channel_id=1, source_target_pairs={{0,1},{1,2},{2,3},{3,0},{4,5},{5,6},{6,7},{7,4},{8,9},{9,10},{10,1... | collective-permute-start | bytes 110600 | tf_op jit(solution)/shard_map/ppermute | solution.py:42
  53.4 15.7 %collective-permute-start.9 = (f32[3,6,4,1,128]{4,3,1,0,2:T(1,128)S(1)}, f32[3,6,4,1,128]{4,3,1,0,2:T(1,128)S(1)}, u32[]{:S(2)}, u32[]{:S(2)}) collective-permute-start(f32[3,6,4,1,128]{4,3,1,0,2:T(1,128)S(1)} %get-tuple-element.19), channel_id=1, source_target_pairs={{1,0},{2,1},{3,2},{0,3},{5,4},{6,5},{7,6},{4,7},{9,8},{10,9},{11,1... | collective-permute-start | bytes 110600 | tf_op jit(solution)/shard_map/ppermute | solution.py:43
  55.1 26.1 %all-to-all-start = ((f32[256,1,128]{2,1,0:T(1,128)}), f32[256,1,128]{2,1,0:T(1,128)S(1)}, u32[]{:S(2)}, u32[]{:S(2)}) async-start(f32[256,1,128]{2,1,0:T(1,128)} %bitcast.9), calls=%async_computation | async-start | bytes 262144 | tf_op jit(solution)/shard_map/all_to_all | solution.py:411
  69.2 30.5 %collective-permute-start.11 = (f32[3,6,1,4,128]{4,3,1,0,2:T(4,128)S(1)}, f32[3,6,1,4,128]{4,3,1,0,2:T(4,128)S(1)}, u32[]{:S(2)}, u32[]{:S(2)}) collective-permute-start(f32[3,6,1,4,128]{4,3,1,0,2:T(4,128)S(1)} %get-tuple-element.14), channel_id=1, source_target_pairs={{4,0},{8,4},{12,8},{16,12},{20,16},{24,20},{28,24},{0,28},{5,1},{9... | collective-permute-start | bytes 110600 | tf_op jit(solution)/shard_map/ppermute | solution.py:393
  75.5 24.1 %collective-permute-start.10 = (f32[3,6,1,4,128]{4,3,1,0,2:T(4,128)S(1)}, f32[3,6,1,4,128]{4,3,1,0,2:T(4,128)S(1)}, u32[]{:S(2)}, u32[]{:S(2)}) collective-permute-start(f32[3,6,1,4,128]{4,3,1,0,2:T(4,128)S(1)} %get-tuple-element.15), channel_id=1, source_target_pairs={{0,4},{4,8},{8,12},{12,16},{16,20},{20,24},{24,28},{28,0},{1,5},{5... | collective-permute-start | bytes 110600 | tf_op jit(solution)/shard_map/ppermute | solution.py:392

commit v5 on v3

--- a/solution.py
+++ b/solution.py
@@ -21,6 +21,7 @@
 PX, PY, PZ = NX + 2, NY + 2, NZ + 2
 CELLS = NX * NY * NZ
 PADDED = PX * PY * PZ
+PER_INNER, PER_OUTER = 1, 4
 KF = 32
 VF = 40
 FAR = 3e38
@@ -195,85 +196,81 @@
     zero = jnp.zeros((KF, 2 * SLOTS), BF16)
     block = jnp.zeros((SLOTS, SLOTS), BF16)
     chunks = chunks_of(inner)
-
-    def plane(x, carry):
-        def query(y, t):
-            at = pl.multiple_of(x * (NY * NZ * KF) + (y * NZ + t) * KF, 8)
-            return qf[pl.ds(at, KF), :].astype(BF16)
-
-        def distances(targets, runs):
-            q = [query(*target) for target in targets]
-            made = []
-            for dx, first, count, s, to_left, to_right in runs:
-                at = ((x + dx) * across + first) * SLOTS
-                source = pt[pl.ds(pl.multiple_of(at, SLOTS), count * SLOTS), :]
-                rows = [zero] * PZ
-                rows[s] = jnp.concatenate(q, 1)
-                if not (to_left and to_right):
-                    rows = [r[:, :SLOTS] for r in rows]
-                    rows[s] = q[0] if to_left else q[1]
-                w = jnp.concatenate(rows, 0)
-                made.append(jnp.dot(source, w, preferred_element_type=F32))
-            return made
-
-        def weights(targets, runs, made):
-            high, low, v = [], [], []
-            for (dx, first, count, s, to_left, to_right), r in zip(runs, made):
-                both = to_left and to_right
-                if dx == 1 and inner and both and s in (1, 2):
-                    y = targets[0][0] - first
-                    at = r[y * SLOTS : (y + 1) * SLOTS]
-                    halves = [at[:, :SLOTS], at[:, SLOTS:]]
-                    halves[s - 1] = without_self(halves[s - 1])
-                    parts = [r[: y * SLOTS], jnp.concatenate(halves, 1), r[(y + 1) * SLOTS :]]
-                    r = jnp.concatenate([p for p in parts if p.shape[0]], 0)
-                for into, part in zip((high, low), parts2(r)):
-                    if not both:
-                        part = jnp.concatenate([part, block] if to_left else [block, part], 1)
-                    into.append(part)
-                v.append(vt[x + dx, s, :, first * SLOTS : (first + count) * SLOTS])
-            return jnp.concatenate(v, 1), jnp.concatenate(high, 0), jnp.concatenate(low, 0)
-
+    per = PER_INNER if inner else PER_OUTER
+
+    def query(x, y, t):
+        at = pl.multiple_of(x * (NY * NZ * KF) + (y * NZ + t) * KF, 8)
+        return qf[pl.ds(at, KF), :].astype(BF16)
+
+    def distances(x, left, right, runs):
+        q = [query(x, *left), query(x, *right)]
+        made = []
+        for dx, first, count, s, to_left, to_right in runs:
+            at = ((x + dx) * across + first) * SLOTS
+            source = pt[pl.ds(pl.multiple_of(at, SLOTS), count * SLOTS), :]
+            rows = [zero] * PZ
+            rows[s] = jnp.concatenate(q, 1)
+            if not (to_left and to_right):
+                rows = [r[:, :SLOTS] for r in rows]
+                rows[s] = q[0] if to_left else q[1]
+            w = jnp.concatenate(rows, 0)
+            made.append(jnp.dot(source, w, preferred_element_type=F32))
+        return made
+
+    def weights(x, left, runs, made):
+        high, low, v = [], [], []
+        for (dx, first, count, s, to_left, to_right), r in zip(runs, made):
+            both = to_left and to_right
+            if dx == 1 and inner and both and s in (1, 2):
+                y = left[0] - first
+                at = r[y * SLOTS : (y + 1) * SLOTS]
+                halves = [at[:, :SLOTS], at[:, SLOTS:]]
+                halves[s - 1] = without_self(halves[s - 1])
+                parts = [r[: y * SLOTS], jnp.concatenate(halves, 1), r[(y + 1) * SLOTS :]]
+                r = jnp.concatenate([p for p in parts if p.shape[0]], 0)
+            for into, part in zip((high, low), parts2(r)):
+                if not both:
+                    part = jnp.concatenate([part, block] if to_left else [block, part], 1)
+                into.append(part)
+            v.append(vt[x + dx, s, :, first * SLOTS : (first + count) * SLOTS])
+        return jnp.concatenate(v + v, 1), jnp.concatenate(high + low, 0)
+
+    def step(n, carry):
+        work = [(n * per + k, *chunk) for k in range(per) for chunk in chunks]
         totals = {}
 
         def add(key, value):
             totals[key] = totals[key] + value if key in totals else value
 
-        made = distances(chunks[0][:2], chunks[0][2])
-        for n, (left, right, runs) in enumerate(chunks):
-            coming = None
-            if n + 1 < len(chunks):
-                coming = distances(chunks[n + 1][:2], chunks[n + 1][2])
-            v, high, low = weights((left, right), runs, made)
-            add((left, right, 0), jnp.dot(v, high, preferred_element_type=F32))
-            add((left, right, 1), jnp.dot(v[: 2 * VF], low, preferred_element_type=F32))
+        made = distances(*work[0])
+        for i, (x, left, right, runs) in enumerate(work):
+            coming = distances(*work[i + 1]) if i + 1 < len(work) else None
+            v, weighted = weights(x, left, runs, made)
+            key = (i // len(chunks), left, right)
+            add(key, jnp.dot(v, weighted, preferred_element_type=F32))
             made = coming
 
         cells = {}
-        for left, right, kind in totals:
-            if kind == 1:
-                continue
-            high, low = totals[(left, right, 0)], totals[(left, right, 1)]
-            total = high[2 * VF : 3 * VF]
-            for part in (low, high):
-                total = total + part[VF : 2 * VF]
-            total = total + low[:VF] + high[:VF]
-            for k, cell in enumerate((left, right)):
-                part = total[:, k * SLOTS : (k + 1) * SLOTS]
+        for (k, left, right), parts in totals.items():
+            total = parts[2 * VF : 3 * VF] + parts[VF : 2 * VF] + parts[:VF]
+            for half, cell in enumerate((left, right)):
+                part = total[:, half * SLOTS : (half + 1) * SLOTS]
+                cell = (k, *cell)
                 cells[cell] = cells[cell] + part if cell in cells else part
-        for y in range(NY):
-            for t in range(NZ):
-                at = pl.multiple_of(x * (NY * NZ * VF) + (y * NZ + t) * VF, 8)
-                at = pl.ds(at, VF)
-                if before is None:
-                    tf[at, :] = cells[y, t]
-                elif (y, t) in cells:
-                    tf[at, :] = before[at, :] + cells[y, t]
-                else:
-                    tf[at, :] = before[at, :]
+        for k in range(per):
+            for y in range(NY):
+                for t in range(NZ):
+                    at = (n * per + k) * (NY * NZ * VF) + (y * NZ + t) * VF
+                    at = pl.ds(pl.multiple_of(at, 8), VF)
+                    if before is None:
+                        tf[at, :] = cells[k, y, t]
+                    elif (k, y, t) in cells:
+                        tf[at, :] = before[at, :] + cells[k, y, t]
+                    else:
+                        tf[at, :] = before[at, :]
         return carry
 
-    lax.fori_loop(0, NX, plane, 0)
+    lax.fori_loop(0, NX // per, step, 0)
 
 
 def forces_of(g, coords, loc_ref, tf):

time: 107 us -> 105 us (0.981)
  Pallas kernels: 48.6 us -> 46.3 us
    pallas_call x4, Pallas kernels: 48.6 us -> 46.3 us  [call(): pl.pallas_call(kernel, out_shape=out_shapes, in_specs=[whole] * len(opera...]
where the time goes in v5:
time: 105 us
  Pallas kernels  46.3 us (44%)
  starting transfers between devices  40.1 us (38%)
  waiting for transfers between devices  14.2 us (14%)
  local copies, waits for them, and re-layouts  1.73 us (2%)
  other arithmetic  1.63 us (2%)
    pallas_call x4, Pallas kernels, call(): pl.pallas_call(kernel, out_shape=out_shapes, in_specs=[whole] * len(opera...  46.3 us
    ppermute x2, starting transfers between devices, widened(): low = lax.ppermute(block[:, :, NY - 1:], GY, forward)  13.2 us
    all_to_all x1, starting transfers between devices, on_device(): peaks = lax.all_to_all(peaks.reshape(devices, 1, SLOTS), EVERY, 0, 0)  11.9 us
    ppermute x4, starting transfers between devices, extended(): high = lax.ppermute(lax.slice_in_dim(block, 0, 1, axis=dim), axis, backward)  11.2 us
    ppermute x2, waiting for transfers between devices, widened(): high = lax.ppermute(block[:, :, :1], GY, backward)  6.02 us
    ppermute x4, waiting for transfers between devices, extended(): lax.ppermute(lax.slice_in_dim(block, size - 1, size, axis=dim), axis, for...  5.98 us
    ppermute x4, starting transfers between devices, extended(): lax.ppermute(lax.slice_in_dim(block, size - 1, size, axis=dim), axis, for...  3.21 us
  transfers between devices with their start and end apart: 13, of which 6 were waited for; matrix products, arithmetic and copies ran while one was open for 0% of the time, Pallas kernels for 17%

profile of v5, /device:TPU:8, one launch (start us, length us, event | category | flops | bytes accessed | tf_op | source)
XLA Modules:
  0.0 104.8 jit_solution(466141272258526364)
XLA Ops:
  0.6 0.8 copy.8
  1.4 0.1 compare_convert_fusion
  1.5 0.0 copy-start.1
  1.5 0.0 copy-start.2
  1.5 0.8 broadcast_multiply_fusion
  2.4 0.0 copy-done.1
  2.4 0.0 copy-done.2
  2.4 0.1 pad_maximum_fusion.3
  2.5 0.1 collective-permute-start
  2.6 4.1 %collective-permute-start.1 = (f32[9,1,4,2,128]{4,3,2,1,0:T(2,128)S(1)}, f32[9,1,4,2,128]{4,3,2,1,0:T(2,128)S(1)}, u32[]{:S(2)}, u32[]{:S(2)}) collective-permute-start(f32[9,1,4,2,128]{4,3,2,1,0:T(2,128)S(1)} %get-tuple-element.17), channel_id=1, source_target_pairs={{32,0},{64,32},{96,64},{128,96},{160,128},{192,160},{224,192},{0,2... | collective-permute-start | bytes 110600 | tf_op jit(solution)/shard_map/ppermute | solution.py:44
  6.7 1.7 %collective-permute-done = f32[9,1,4,2,128]{4,3,2,1,0:T(2,128)S(1)} collective-permute-done((f32[9,1,4,2,128]{4,3,2,1,0:T(2,128)S(1)}, f32[9,1,4,2,128]{4,3,2,1,0:T(2,128)S(1)}, u32[]{:S(2)}, u32[]{:S(2)}) %collective-permute-start) | collective-permute-done | bytes 36896 | tf_op jit(solution)/shard_map/ppermute | solution.py:43
  8.4 0.0 collective-permute-done.1
  8.4 0.1 pad_maximum_fusion.1
  8.5 0.2 fusion.1
  8.7 1.6 %collective-permute-start.2 = (f32[9,6,4,1,128]{4,3,2,1,0:T(1,128)S(1)}, f32[9,6,4,1,128]{4,3,2,1,0:T(1,128)S(1)}, u32[]{:S(2)}, u32[]{:S(2)}) collective-permute-start(f32[9,6,4,1,128]{4,3,2,1,0:T(1,128)S(1)} %get-tuple-element.12), channel_id=1, source_target_pairs={{0,1},{1,2},{2,3},{3,0},{4,5},{5,6},{6,7},{7,4},{8,9},{9,10},{10,1... | collective-permute-start | bytes 331784 | tf_op jit(solution)/shard_map/ppermute | solution.py:43
  10.2 1.7 %collective-permute-start.3 = (f32[9,6,4,1,128]{4,3,2,1,0:T(1,128)S(1)}, f32[9,6,4,1,128]{4,3,2,1,0:T(1,128)S(1)}, u32[]{:S(2)}, u32[]{:S(2)}) collective-permute-start(f32[9,6,4,1,128]{4,3,2,1,0:T(1,128)S(1)} %get-tuple-element.13), channel_id=1, source_target_pairs={{1,0},{2,1},{3,2},{0,3},{5,4},{6,5},{7,6},{4,7},{9,8},{10,9},{11,1... | collective-permute-start | bytes 331784 | tf_op jit(solution)/shard_map/ppermute | solution.py:44
  12.0 2.9 %collective-permute-done.2 = f32[9,6,4,1,128]{4,3,2,1,0:T(1,128)S(1)} collective-permute-done((f32[9,6,4,1,128]{4,3,2,1,0:T(1,128)S(1)}, f32[9,6,4,1,128]{4,3,2,1,0:T(1,128)S(1)}, u32[]{:S(2)}, u32[]{:S(2)}) %collective-permute-start.2) | collective-permute-done | bytes 110624 | tf_op jit(solution)/shard_map/ppermute | solution.py:43
  14.9 0.1 collective-permute-done.3
  15.0 0.3 pad_maximum_fusion
  15.3 6.7 %collective-permute-start.4 = (f32[9,6,1,4,128]{4,3,2,1,0:T(4,128)S(1)}, f32[9,6,1,4,128]{4,3,2,1,0:T(4,128)S(1)}, u32[]{:S(2)}, u32[]{:S(2)}) collective-permute-start(f32[9,6,1,4,128]{4,3,2,1,0:T(4,128)S(1)} %get-tuple-element.10), channel_id=1, source_target_pairs={{0,4},{4,8},{8,12},{12,16},{16,20},{20,24},{24,28},{28,0},{1,5},{5... | collective-permute-start | bytes 331784 | tf_op jit(solution)/shard_map/ppermute | solution.py:383
  22.1 0.2 collective-permute-start.5
  22.3 17.7 %start_inner.1.sums_ref = f32[1280,128]{1,0:T(8,128)S(1)} custom-call(f32[9,96,128]{2,1,0:T(8,128)S(1)} %bitcast.16, f32[9,32,128]{2,1,0:T(8,128)S(1)} %bitcast.18), custom_call_target="tpu_custom_call" | custom-call | tf_op jit(solution)/shard_map/start_inner/pallas_call | solution.py:365
  40.0 0.0 copy-start
  40.0 0.0 collective-permute-done.4
  40.0 0.0 collective-permute-done.5
  40.0 0.1 pad_maximum_fusion.2
  40.1 0.6 copy-done
  40.7 5.4 %start_outer.1 = (f32[3,32,128]{2,1,0:T(8,128)S(1)}, f32[256,128]{1,0:T(8,128)}) custom-call(f32[9,48,128]{2,1,0:T(8,128)S(1)} %bitcast.22, f32[9,32,128]{2,1,0:T(8,128)S(1)} %bitcast.19, f32[32,128]{1,0:T(8,128)S(1)} %bitcast.31, f32[1280,128]{1,0:T(8,128)S(1)} %start_inner.1.sums_ref), custom_call_target="tpu_custom_call" | custom-call | tf_op jit(solution)/shard_map/start_outer/pallas_call | solution.py:365
  46.1 0.0 collective-permute-start.6
  46.1 3.5 %collective-permute-start.7 = (f32[3,1,4,2,128]{4,3,2,1,0:T(2,128)S(1)}, f32[3,1,4,2,128]{4,3,2,1,0:T(2,128)S(1)}, u32[]{:S(2)}, u32[]{:S(2)}) collective-permute-start(f32[3,1,4,2,128]{4,3,2,1,0:T(2,128)S(1)} %get-tuple-element.21), channel_id=1, source_target_pairs={{32,0},{64,32},{96,64},{128,96},{160,128},{192,160},{224,192},{0,2... | collective-permute-start | bytes 36872 | tf_op jit(solution)/shard_map/ppermute | solution.py:44
  49.6 1.4 %collective-permute-done.6 = f32[3,1,4,2,128]{4,3,2,1,0:T(2,128)S(1)} collective-permute-done((f32[3,1,4,2,128]{4,3,2,1,0:T(2,128)S(1)}, f32[3,1,4,2,128]{4,3,2,1,0:T(2,128)S(1)}, u32[]{:S(2)}, u32[]{:S(2)}) %collective-permute-start.6) | collective-permute-done | bytes 12320 | tf_op jit(solution)/shard_map/ppermute | solution.py:43
  51.0 0.0 collective-permute-done.7
  51.1 0.1 fusion.4
  51.1 1.6 %collective-permute-start.8 = (f32[3,6,4,1,128]{4,3,2,1,0:T(1,128)S(1)}, f32[3,6,4,1,128]{4,3,2,1,0:T(1,128)S(1)}, u32[]{:S(2)}, u32[]{:S(2)}) collective-permute-start(f32[3,6,4,1,128]{4,3,2,1,0:T(1,128)S(1)} %get-tuple-element.18), channel_id=1, source_target_pairs={{0,1},{1,2},{2,3},{3,0},{4,5},{5,6},{6,7},{7,4},{8,9},{9,10},{10,1... | collective-permute-start | bytes 110600 | tf_op jit(solution)/shard_map/ppermute | solution.py:43
  52.7 1.8 %collective-permute-start.9 = (f32[3,6,4,1,128]{4,3,2,1,0:T(1,128)S(1)}, f32[3,6,4,1,128]{4,3,2,1,0:T(1,128)S(1)}, u32[]{:S(2)}, u32[]{:S(2)}) collective-permute-start(f32[3,6,4,1,128]{4,3,2,1,0:T(1,128)S(1)} %get-tuple-element.19), channel_id=1, source_target_pairs={{1,0},{2,1},{3,2},{0,3},{5,4},{6,5},{7,6},{4,7},{9,8},{10,9},{11,1... | collective-permute-start | bytes 110600 | tf_op jit(solution)/shard_map/ppermute | solution.py:44
  54.4 11.9 %all-to-all-start = ((f32[256,1,128]{2,1,0:T(1,128)}), f32[256,1,128]{2,1,0:T(1,128)S(1)}, u32[]{:S(2)}, u32[]{:S(2)}) async-start(f32[256,1,128]{2,1,0:T(1,128)} %bitcast.7), calls=%async_computation | async-start | bytes 262144 | tf_op jit(solution)/shard_map/all_to_all | solution.py:403
  66.3 0.0 collective-permute-done.8
  66.4 0.0 collective-permute-done.9
  66.4 0.1 pad_maximum_fusion.4
  66.5 6.4 %collective-permute-start.10 = (f32[3,6,1,4,128]{4,3,2,1,0:T(4,128)S(1)}, f32[3,6,1,4,128]{4,3,2,1,0:T(4,128)S(1)}, u32[]{:S(2)}, u32[]{:S(2)}) collective-permute-start(f32[3,6,1,4,128]{4,3,2,1,0:T(4,128)S(1)} %get-tuple-element.14), channel_id=1, source_target_pairs={{0,4},{4,8},{8,12},{12,16},{16,20},{20,24},{24,28},{28,0},{1,5},{5... | collective-permute-start | bytes 110600 | tf_op jit(solution)/shard_map/ppermute | solution.py:383
  72.9 0.5 collective-permute-start.11
  73.4 2.1 %collective-permute-done.10 = f32[3,6,1,4,128]{4,3,2,1,0:T(4,128)S(1)} collective-permute-done((f32[3,6,1,4,128]{4,3,2,1,0:T(4,128)S(1)}, f32[3,6,1,4,128]{4,3,2,1,0:T(4,128)S(1)}, u32[]{:S(2)}, u32[]{:S(2)}) %collective-permute-start.10) | collective-permute-done | bytes 36896 | tf_op jit(solution)/shard_map/ppermute | solution.py:383
  75.5 6.0 %collective-permute-done.11 = f32[3,6,1,4,128]{4,3,2,1,0:T(4,128)S(1)} collective-permute-done((f32[3,6,1,4,128]{4,3,2,1,0:T(4,128)S(1)}, f32[3,6,1,4,128]{4,3,2,1,0:T(4,128)S(1)}, u32[]{:S(2)}, u32[]{:S(2)}) %collective-permute-start.11) | collective-permute-done | bytes 36896 | tf_op jit(solution)/shard_map/ppermute | solution.py:384
  81.5 0.0 all-to-all-done
  81.5 17.8 %end_inner.1.sums_ref = f32[1280,128]{1,0:T(8,128)S(1)} custom-call(f32[9,96,128]{2,1,0:T(8,128)S(1)} %bitcast.17, f32[9,32,128]{2,1,0:T(8,128)S(1)} %bitcast.20, f32[3,96,128]{2,1,0:T(8,128)S(1)} %bitcast.29, f32[3,32,128]{2,1,0:T(8,128)S(1)} %get-tuple-element.6.speed_ref, f32[256,128]{1,0:T(8,128)S(1)} %bitcast.24), custom_call_target="tpu_custom_call" | custom-call | tf_op jit(solution)/shard_map/end_inner/pallas_call | solution.py:365
  99.4 5.4 %end_outer.1 = (f32[3,32,128]{2,1,0:T(8,128)}, f32[3,32,128]{2,1,0:T(8,128)}) custom-call(f32[9,48,128]{2,1,0:T(8,128)S(1)} %bitcast.23, f32[9,32,128]{2,1,0:T(8,128)S(1)} %bitcast.21, f32[32,128]{1,0:T(8,128)S(1)} %bitcast.32, f32[3,48,128]{2,1,0:T(8,128)S(1)} %bitcast.30, f32[3,32,128]{2,1,0:T(8,128)S(1)} %get-tuple-element.6.speed_ref, ...), custom_call_target="tpu_custom_call" | custom-call | tf_op jit(solution)/shard_map/end_outer/pallas_call | solution.py:365
  (6 shorter events, 0.1 us)
Async XLA Ops:
  1.5 0.9 copy-start.1
  1.5 0.8 copy-start.2
  2.5 5.9 %collective-permute-start = (f32[9,1,4,2,128]{4,3,2,1,0:T(2,128)S(1)}, f32[9,1,4,2,128]{4,3,2,1,0:T(2,128)S(1)}, u32[]{:S(2)}, u32[]{:S(2)}) collective-permute-start(f32[9,1,4,2,128]{4,3,2,1,0:T(2,128)S(1)} %get-tuple-element.16), channel_id=1, source_target_pairs={{0,32},{32,64},{64,96},{96,128},{128,160},{160,192},{192,224},{224... | collective-permute-start | bytes 110600 | tf_op jit(solution)/shard_map/ppermute | solution.py:43
  2.6 5.8 %collective-permute-start.1 = (f32[9,1,4,2,128]{4,3,2,1,0:T(2,128)S(1)}, f32[9,1,4,2,128]{4,3,2,1,0:T(2,128)S(1)}, u32[]{:S(2)}, u32[]{:S(2)}) collective-permute-start(f32[9,1,4,2,128]{4,3,2,1,0:T(2,128)S(1)} %get-tuple-element.17), channel_id=1, source_target_pairs={{32,0},{64,32},{96,64},{128,96},{160,128},{192,160},{224,192},{0,2... | collective-permute-start | bytes 110600 | tf_op jit(solution)/shard_map/ppermute | solution.py:44
  8.7 6.3 %collective-permute-start.2 = (f32[9,6,4,1,128]{4,3,2,1,0:T(1,128)S(1)}, f32[9,6,4,1,128]{4,3,2,1,0:T(1,128)S(1)}, u32[]{:S(2)}, u32[]{:S(2)}) collective-permute-start(f32[9,6,4,1,128]{4,3,2,1,0:T(1,128)S(1)} %get-tuple-element.12), channel_id=1, source_target_pairs={{0,1},{1,2},{2,3},{3,0},{4,5},{5,6},{6,7},{7,4},{8,9},{9,10},{10,1... | collective-permute-start | bytes 331784 | tf_op jit(solution)/shard_map/ppermute | solution.py:43
  10.2 4.7 %collective-permute-start.3 = (f32[9,6,4,1,128]{4,3,2,1,0:T(1,128)S(1)}, f32[9,6,4,1,128]{4,3,2,1,0:T(1,128)S(1)}, u32[]{:S(2)}, u32[]{:S(2)}) collective-permute-start(f32[9,6,4,1,128]{4,3,2,1,0:T(1,128)S(1)} %get-tuple-element.13), channel_id=1, source_target_pairs={{1,0},{2,1},{3,2},{0,3},{5,4},{6,5},{7,6},{4,7},{9,8},{10,9},{11,1... | collective-permute-start | bytes 331784 | tf_op jit(solution)/shard_map/ppermute | solution.py:44
  15.3 24.7 %collective-permute-start.4 = (f32[9,6,1,4,128]{4,3,2,1,0:T(4,128)S(1)}, f32[9,6,1,4,128]{4,3,2,1,0:T(4,128)S(1)}, u32[]{:S(2)}, u32[]{:S(2)}) collective-permute-start(f32[9,6,1,4,128]{4,3,2,1,0:T(4,128)S(1)} %get-tuple-element.10), channel_id=1, source_target_pairs={{0,4},{4,8},{8,12},{12,16},{16,20},{20,24},{24,28},{28,0},{1,5},{5... | collective-permute-start | bytes 331784 | tf_op jit(solution)/shard_map/ppermute | solution.py:383
  22.1 17.9 %collective-permute-start.5 = (f32[9,6,1,4,128]{4,3,2,1,0:T(4,128)S(1)}, f32[9,6,1,4,128]{4,3,2,1,0:T(4,128)S(1)}, u32[]{:S(2)}, u32[]{:S(2)}) collective-permute-start(f32[9,6,1,4,128]{4,3,2,1,0:T(4,128)S(1)} %get-tuple-element.11), channel_id=1, source_target_pairs={{4,0},{8,4},{12,8},{16,12},{20,16},{24,20},{28,24},{0,28},{5,1},{9... | collective-permute-start | bytes 331784 | tf_op jit(solution)/shard_map/ppermute | solution.py:384
  40.0 0.7 copy-start
  46.1 4.9 %collective-permute-start.6 = (f32[3,1,4,2,128]{4,3,2,1,0:T(2,128)S(1)}, f32[3,1,4,2,128]{4,3,2,1,0:T(2,128)S(1)}, u32[]{:S(2)}, u32[]{:S(2)}) collective-permute-start(f32[3,1,4,2,128]{4,3,2,1,0:T(2,128)S(1)} %get-tuple-element.20), channel_id=1, source_target_pairs={{0,32},{32,64},{64,96},{96,128},{128,160},{160,192},{192,224},{224... | collective-permute-start | bytes 36872 | tf_op jit(solution)/shard_map/ppermute | solution.py:43
  46.1 4.9 %collective-permute-start.7 = (f32[3,1,4,2,128]{4,3,2,1,0:T(2,128)S(1)}, f32[3,1,4,2,128]{4,3,2,1,0:T(2,128)S(1)}, u32[]{:S(2)}, u32[]{:S(2)}) collective-permute-start(f32[3,1,4,2,128]{4,3,2,1,0:T(2,128)S(1)} %get-tuple-element.21), channel_id=1, source_target_pairs={{32,0},{64,32},{96,64},{128,96},{160,128},{192,160},{224,192},{0,2... | collective-permute-start | bytes 36872 | tf_op jit(solution)/shard_map/ppermute | solution.py:44
  51.1 15.2 %collective-permute-start.8 = (f32[3,6,4,1,128]{4,3,2,1,0:T(1,128)S(1)}, f32[3,6,4,1,128]{4,3,2,1,0:T(1,128)S(1)}, u32[]{:S(2)}, u32[]{:S(2)}) collective-permute-start(f32[3,6,4,1,128]{4,3,2,1,0:T(1,128)S(1)} %get-tuple-element.18), channel_id=1, source_target_pairs={{0,1},{1,2},{2,3},{3,0},{4,5},{5,6},{6,7},{7,4},{8,9},{9,10},{10,1... | collective-permute-start | bytes 110600 | tf_op jit(solution)/shard_map/ppermute | solution.py:43
  52.7 13.7 %collective-permute-start.9 = (f32[3,6,4,1,128]{4,3,2,1,0:T(1,128)S(1)}, f32[3,6,4,1,128]{4,3,2,1,0:T(1,128)S(1)}, u32[]{:S(2)}, u32[]{:S(2)}) collective-permute-start(f32[3,6,4,1,128]{4,3,2,1,0:T(1,128)S(1)} %get-tuple-element.19), channel_id=1, source_target_pairs={{1,0},{2,1},{3,2},{0,3},{5,4},{6,5},{7,6},{4,7},{9,8},{10,9},{11,1... | collective-permute-start | bytes 110600 | tf_op jit(solution)/shard_map/ppermute | solution.py:44
  54.4 27.1 %all-to-all-start = ((f32[256,1,128]{2,1,0:T(1,128)}), f32[256,1,128]{2,1,0:T(1,128)S(1)}, u32[]{:S(2)}, u32[]{:S(2)}) async-start(f32[256,1,128]{2,1,0:T(1,128)} %bitcast.7), calls=%async_computation | async-start | bytes 262144 | tf_op jit(solution)/shard_map/all_to_all | solution.py:403
  66.5 9.0 %collective-permute-start.10 = (f32[3,6,1,4,128]{4,3,2,1,0:T(4,128)S(1)}, f32[3,6,1,4,128]{4,3,2,1,0:T(4,128)S(1)}, u32[]{:S(2)}, u32[]{:S(2)}) collective-permute-start(f32[3,6,1,4,128]{4,3,2,1,0:T(4,128)S(1)} %get-tuple-element.14), channel_id=1, source_target_pairs={{0,4},{4,8},{8,12},{12,16},{16,20},{20,24},{24,28},{28,0},{1,5},{5... | collective-permute-start | bytes 110600 | tf_op jit(solution)/shard_map/ppermute | solution.py:383
  72.9 8.6 %collective-permute-start.11 = (f32[3,6,1,4,128]{4,3,2,1,0:T(4,128)S(1)}, f32[3,6,1,4,128]{4,3,2,1,0:T(4,128)S(1)}, u32[]{:S(2)}, u32[]{:S(2)}) collective-permute-start(f32[3,6,1,4,128]{4,3,2,1,0:T(4,128)S(1)} %get-tuple-element.15), channel_id=1, source_target_pairs={{4,0},{8,4},{12,8},{16,12},{20,16},{24,20},{28,24},{0,28},{5,1},{9... | collective-permute-start | bytes 110600 | tf_op jit(solution)/shard_map/ppermute | solution.py:384

commit v6 on v5

--- a/solution.py
+++ b/solution.py
@@ -292,7 +292,7 @@
     return STEP_LIMIT * lax.rsqrt(jnp.broadcast_to(peak, (8, SLOTS)) + 1e-12)
 
 
-def start_inner(pad_ref, loc_ref, sums_ref, pf, vf, pt, vt, qf):
+def start_inner(pad_ref, loc_ref, mob_ref, sums_ref, pf, vf, pt, vt, qf):
     prepare_sources(pad_ref, None, pf, vf, True)
     lay_out_sources(pf, vf, pt, vt)
     prepare_targets(loc_ref, None, qf)
@@ -388,15 +388,16 @@
 
 
 def on_device(positions, line_vectors, burgers, mobility, occupancy):
-    slots = lax.broadcasted_iota(jnp.int32, mobility.shape, 3)
-    live = (slots < occupancy[..., None]).astype(F32)
-    fields = jnp.concatenate([positions, line_vectors, burgers * live], 0)
+    fields = jnp.concatenate([positions, line_vectors, burgers], 0)
+    row = lax.broadcasted_iota(jnp.int32, fields.shape, 0)
+    slot = lax.broadcasted_iota(jnp.int32, fields.shape, 4)
+    fields = jnp.where((row < 6) | (slot < occupancy[None, ..., None]), fields, 0.0)
     pad, rim = widened(fields)
     loc = fields.reshape(9, CELLS, SLOTS)
     mob = mobility.reshape(CELLS, SLOTS)
     devices = lax.axis_size(EVERY)
     peaks = jax.ShapeDtypeStruct((devices, SLOTS), F32)
-    (sums,) = call(start_inner, [SUMS], [pad, loc], "start_inner", True)
+    (sums,) = call(start_inner, [SUMS], [pad, loc, mob], "start_inner", True)
     speed, peaks = call(
         start_outer, [VEC, peaks], [rim, loc, mob, sums], "start_outer", False
     )

time: 105 us -> 105 us (level)
    select_n x0 -> x2, other arithmetic: none -> 1.09 us  [on_device(): jnp.where((row < 6) | (slot < occupancy[None, ..., None]), fields, 0.0)]
where the time goes in v6:
time: 105 us
  Pallas kernels  46.4 us (44%)
  starting transfers between devices  40.1 us (38%)
  waiting for transfers between devices  14.1 us (13%)
  local copies, waits for them, and re-layouts  1.81 us (2%)
  other arithmetic  1.73 us (2%)
    pallas_call x4, Pallas kernels, call(): pl.pallas_call(kernel, out_shape=out_shapes, in_specs=[whole] * len(opera...  46.4 us
    ppermute x2, starting transfers between devices, widened(): low = lax.ppermute(block[:, :, NY - 1:], GY, forward)  13.2 us
    all_to_all x1, starting transfers between devices, on_device(): peaks = lax.all_to_all(peaks.reshape(devices, 1, SLOTS), EVERY, 0, 0)  11.9 us
    ppermute x4, starting transfers between devices, extended(): high = lax.ppermute(lax.slice_in_dim(block, 0, 1, axis=dim), axis, backward)  11.2 us
    ppermute x2, waiting for transfers between devices, widened(): high = lax.ppermute(block[:, :, :1], GY, backward)  6 us
    ppermute x4, waiting for transfers between devices, extended(): lax.ppermute(lax.slice_in_dim(block, size - 1, size, axis=dim), axis, for...  5.88 us
    ppermute x4, starting transfers between devices, extended(): lax.ppermute(lax.slice_in_dim(block, size - 1, size, axis=dim), axis, for...  3.21 us
  transfers between devices with their start and end apart: 13, of which 6 were waited for; matrix products, arithmetic and copies ran while one was open for 0% of the time, Pallas kernels for 17%

profile of v6, /device:TPU:8, one launch (start us, length us, event | category | flops | bytes accessed | tf_op | source)
XLA Modules:
  0.0 104.9 jit_solution(9770464680761127184)
XLA Ops:
  0.6 0.8 copy.11
  1.4 1.0 or_select_fusion
  2.5 0.1 collective-permute-start
  2.5 4.1 %collective-permute-start.1 = (f32[9,1,4,2,128]{4,3,2,1,0:T(2,128)S(1)}, f32[9,1,4,2,128]{4,3,2,1,0:T(2,128)S(1)}, u32[]{:S(2)}, u32[]{:S(2)}) collective-permute-start(f32[9,1,4,2,128]{4,3,2,1,0:T(2,128)S(1)} %get-tuple-element.17), channel_id=1, source_target_pairs={{32,0},{64,32},{96,64},{128,96},{160,128},{192,160},{224,192},{0,2... | collective-permute-start | bytes 110600 | tf_op jit(solution)/shard_map/ppermute | solution.py:44
  6.7 1.7 %collective-permute-done = f32[9,1,4,2,128]{4,3,2,1,0:T(2,128)S(1)} collective-permute-done((f32[9,1,4,2,128]{4,3,2,1,0:T(2,128)S(1)}, f32[9,1,4,2,128]{4,3,2,1,0:T(2,128)S(1)}, u32[]{:S(2)}, u32[]{:S(2)}) %collective-permute-start) | collective-permute-done | bytes 36896 | tf_op jit(solution)/shard_map/ppermute | solution.py:43
  8.3 0.0 collective-permute-done.1
  8.3 0.1 pad_maximum_fusion.1
  8.5 0.2 fusion.2
  8.6 1.6 %collective-permute-start.2 = (f32[9,6,4,1,128]{4,3,2,1,0:T(1,128)S(1)}, f32[9,6,4,1,128]{4,3,2,1,0:T(1,128)S(1)}, u32[]{:S(2)}, u32[]{:S(2)}) collective-permute-start(f32[9,6,4,1,128]{4,3,2,1,0:T(1,128)S(1)} %get-tuple-element.12), channel_id=1, source_target_pairs={{0,1},{1,2},{2,3},{3,0},{4,5},{5,6},{6,7},{7,4},{8,9},{9,10},{10,1... | collective-permute-start | bytes 331784 | tf_op jit(solution)/shard_map/ppermute | solution.py:43
  10.2 1.7 %collective-permute-start.3 = (f32[9,6,4,1,128]{4,3,2,1,0:T(1,128)S(1)}, f32[9,6,4,1,128]{4,3,2,1,0:T(1,128)S(1)}, u32[]{:S(2)}, u32[]{:S(2)}) collective-permute-start(f32[9,6,4,1,128]{4,3,2,1,0:T(1,128)S(1)} %get-tuple-element.13), channel_id=1, source_target_pairs={{1,0},{2,1},{3,2},{0,3},{5,4},{6,5},{7,6},{4,7},{9,8},{10,9},{11,1... | collective-permute-start | bytes 331784 | tf_op jit(solution)/shard_map/ppermute | solution.py:44
  12.0 0.1 lt.28
  12.1 2.8 %collective-permute-done.2 = f32[9,6,4,1,128]{4,3,2,1,0:T(1,128)S(1)} collective-permute-done((f32[9,6,4,1,128]{4,3,2,1,0:T(1,128)S(1)}, f32[9,6,4,1,128]{4,3,2,1,0:T(1,128)S(1)}, u32[]{:S(2)}, u32[]{:S(2)}) %collective-permute-start.2) | collective-permute-done | bytes 110624 | tf_op jit(solution)/shard_map/ppermute | solution.py:43
  14.9 0.1 collective-permute-done.3
  15.0 0.3 pad_maximum_fusion
  15.3 0.0 copy-start.1
  15.3 0.0 copy-start.2
  15.3 0.0 copy-start.3
  15.4 6.7 %collective-permute-start.4 = (f32[9,6,1,4,128]{4,3,2,1,0:T(4,128)S(1)}, f32[9,6,1,4,128]{4,3,2,1,0:T(4,128)S(1)}, u32[]{:S(2)}, u32[]{:S(2)}) collective-permute-start(f32[9,6,1,4,128]{4,3,2,1,0:T(4,128)S(1)} %get-tuple-element.10), channel_id=1, source_target_pairs={{0,4},{4,8},{8,12},{12,16},{16,20},{20,24},{24,28},{28,0},{1,5},{5... | collective-permute-start | bytes 331784 | tf_op jit(solution)/shard_map/ppermute | solution.py:383
  22.1 0.2 collective-permute-start.5
  22.3 0.0 copy-done.1
  22.3 0.0 copy-done.2
  22.3 0.0 copy-done.3
  22.3 0.0 copy-start
  22.3 0.1 maximum_select_fusion.loc_ref
  22.4 0.6 copy-done
  23.0 17.7 %start_inner.1.sums_ref = f32[1280,128]{1,0:T(8,128)S(1)} custom-call(f32[9,96,128]{2,1,0:T(8,128)S(1)} %bitcast.15, f32[9,32,128]{2,1,0:T(8,128)S(1)} %maximum_select_fusion.loc_ref, f32[32,128]{1,0:T(8,128)S(1)} %bitcast.26), custom_call_target="tpu_custom_call" | custom-call | tf_op jit(solution)/shard_map/start_inner/pallas_call | solution.py:365
  40.7 0.0 collective-permute-done.4
  40.8 0.0 collective-permute-done.5
  40.8 0.1 pad_maximum_fusion.2
  40.8 5.4 %start_outer.1 = (f32[3,32,128]{2,1,0:T(8,128)S(1)}, f32[256,128]{1,0:T(8,128)}) custom-call(f32[9,48,128]{2,1,0:T(8,128)S(1)} %bitcast.17, f32[9,32,128]{2,1,0:T(8,128)S(1)} %maximum_select_fusion.loc_ref, f32[32,128]{1,0:T(8,128)S(1)} %bitcast.27, f32[1280,128]{1,0:T(8,128)S(1)} %start_inner.1.sums_ref), custom_call_target="tpu_custom_call" | custom-call | tf_op jit(solution)/shard_map/start_outer/pallas_call | solution.py:365
  46.2 0.0 collective-permute-start.6
  46.2 3.5 %collective-permute-start.7 = (f32[3,1,4,2,128]{4,3,2,1,0:T(2,128)S(1)}, f32[3,1,4,2,128]{4,3,2,1,0:T(2,128)S(1)}, u32[]{:S(2)}, u32[]{:S(2)}) collective-permute-start(f32[3,1,4,2,128]{4,3,2,1,0:T(2,128)S(1)} %get-tuple-element.21), channel_id=1, source_target_pairs={{32,0},{64,32},{96,64},{128,96},{160,128},{192,160},{224,192},{0,2... | collective-permute-start | bytes 36872 | tf_op jit(solution)/shard_map/ppermute | solution.py:44
  49.8 1.4 %collective-permute-done.6 = f32[3,1,4,2,128]{4,3,2,1,0:T(2,128)S(1)} collective-permute-done((f32[3,1,4,2,128]{4,3,2,1,0:T(2,128)S(1)}, f32[3,1,4,2,128]{4,3,2,1,0:T(2,128)S(1)}, u32[]{:S(2)}, u32[]{:S(2)}) %collective-permute-start.6) | collective-permute-done | bytes 12320 | tf_op jit(solution)/shard_map/ppermute | solution.py:43
  51.1 0.0 collective-permute-done.7
  51.2 0.1 fusion.5
  51.3 1.6 %collective-permute-start.8 = (f32[3,6,4,1,128]{4,3,2,1,0:T(1,128)S(1)}, f32[3,6,4,1,128]{4,3,2,1,0:T(1,128)S(1)}, u32[]{:S(2)}, u32[]{:S(2)}) collective-permute-start(f32[3,6,4,1,128]{4,3,2,1,0:T(1,128)S(1)} %get-tuple-element.18), channel_id=1, source_target_pairs={{0,1},{1,2},{2,3},{3,0},{4,5},{5,6},{6,7},{7,4},{8,9},{9,10},{10,1... | collective-permute-start | bytes 110600 | tf_op jit(solution)/shard_map/ppermute | solution.py:43
  52.8 1.8 %collective-permute-start.9 = (f32[3,6,4,1,128]{4,3,2,1,0:T(1,128)S(1)}, f32[3,6,4,1,128]{4,3,2,1,0:T(1,128)S(1)}, u32[]{:S(2)}, u32[]{:S(2)}) collective-permute-start(f32[3,6,4,1,128]{4,3,2,1,0:T(1,128)S(1)} %get-tuple-element.19), channel_id=1, source_target_pairs={{1,0},{2,1},{3,2},{0,3},{5,4},{6,5},{7,6},{4,7},{9,8},{10,9},{11,1... | collective-permute-start | bytes 110600 | tf_op jit(solution)/shard_map/ppermute | solution.py:44
  54.6 11.9 %all-to-all-start = ((f32[256,1,128]{2,1,0:T(1,128)}), f32[256,1,128]{2,1,0:T(1,128)S(1)}, u32[]{:S(2)}, u32[]{:S(2)}) async-start(f32[256,1,128]{2,1,0:T(1,128)} %bitcast.9), calls=%async_computation | async-start | bytes 262144 | tf_op jit(solution)/shard_map/all_to_all | solution.py:404
  66.5 0.0 collective-permute-done.8
  66.5 0.0 collective-permute-done.9
  66.5 0.1 pad_maximum_fusion.3
  66.7 6.4 %collective-permute-start.10 = (f32[3,6,1,4,128]{4,3,2,1,0:T(4,128)S(1)}, f32[3,6,1,4,128]{4,3,2,1,0:T(4,128)S(1)}, u32[]{:S(2)}, u32[]{:S(2)}) collective-permute-start(f32[3,6,1,4,128]{4,3,2,1,0:T(4,128)S(1)} %get-tuple-element.14), channel_id=1, source_target_pairs={{0,4},{4,8},{8,12},{12,16},{16,20},{20,24},{24,28},{28,0},{1,5},{5... | collective-permute-start | bytes 110600 | tf_op jit(solution)/shard_map/ppermute | solution.py:383
  73.1 0.5 collective-permute-start.11
  73.6 2.1 %collective-permute-done.10 = f32[3,6,1,4,128]{4,3,2,1,0:T(4,128)S(1)} collective-permute-done((f32[3,6,1,4,128]{4,3,2,1,0:T(4,128)S(1)}, f32[3,6,1,4,128]{4,3,2,1,0:T(4,128)S(1)}, u32[]{:S(2)}, u32[]{:S(2)}) %collective-permute-start.10) | collective-permute-done | bytes 36896 | tf_op jit(solution)/shard_map/ppermute | solution.py:383
  75.7 6.0 %collective-permute-done.11 = f32[3,6,1,4,128]{4,3,2,1,0:T(4,128)S(1)} collective-permute-done((f32[3,6,1,4,128]{4,3,2,1,0:T(4,128)S(1)}, f32[3,6,1,4,128]{4,3,2,1,0:T(4,128)S(1)}, u32[]{:S(2)}, u32[]{:S(2)}) %collective-permute-start.11) | collective-permute-done | bytes 36896 | tf_op jit(solution)/shard_map/ppermute | solution.py:384
  81.7 0.0 all-to-all-done
  81.7 17.8 %end_inner.1.sums_ref = f32[1280,128]{1,0:T(8,128)S(1)} custom-call(f32[9,96,128]{2,1,0:T(8,128)S(1)} %bitcast.16, f32[9,32,128]{2,1,0:T(8,128)S(1)} %maximum_select_fusion.loc_ref, f32[3,96,128]{2,1,0:T(8,128)S(1)} %bitcast.24, f32[3,32,128]{2,1,0:T(8,128)S(1)} %get-tuple-element.6.speed_ref, f32[256,128]{1,0:T(8,128)S(1)} %bitcast.19), custom_call_target="tpu_custom_call" | custom-call | tf_op jit(solution)/shard_map/end_inner/pallas_call | solution.py:365
  99.5 5.4 %end_outer.1 = (f32[3,32,128]{2,1,0:T(8,128)}, f32[3,32,128]{2,1,0:T(8,128)}) custom-call(f32[9,48,128]{2,1,0:T(8,128)S(1)} %bitcast.18, f32[9,32,128]{2,1,0:T(8,128)S(1)} %maximum_select_fusion.loc_ref, f32[32,128]{1,0:T(8,128)S(1)} %bitcast.28, f32[3,48,128]{2,1,0:T(8,128)S(1)} %bitcast.25, f32[3,32,128]{2,1,0:T(8,128)S(1)} %get-tuple-element.6.speed_ref, ...), custom_call_target="tpu_custom_call" | custom-call | tf_op jit(solution)/shard_map/end_outer/pallas_call | solution.py:365
  (7 shorter events, 0.1 us)
Async XLA Ops:
  2.5 5.9 %collective-permute-start = (f32[9,1,4,2,128]{4,3,2,1,0:T(2,128)S(1)}, f32[9,1,4,2,128]{4,3,2,1,0:T(2,128)S(1)}, u32[]{:S(2)}, u32[]{:S(2)}) collective-permute-start(f32[9,1,4,2,128]{4,3,2,1,0:T(2,128)S(1)} %get-tuple-element.16), channel_id=1, source_target_pairs={{0,32},{32,64},{64,96},{96,128},{128,160},{160,192},{192,224},{224... | collective-permute-start | bytes 110600 | tf_op jit(solution)/shard_map/ppermute | solution.py:43
  2.5 5.8 %collective-permute-start.1 = (f32[9,1,4,2,128]{4,3,2,1,0:T(2,128)S(1)}, f32[9,1,4,2,128]{4,3,2,1,0:T(2,128)S(1)}, u32[]{:S(2)}, u32[]{:S(2)}) collective-permute-start(f32[9,1,4,2,128]{4,3,2,1,0:T(2,128)S(1)} %get-tuple-element.17), channel_id=1, source_target_pairs={{32,0},{64,32},{96,64},{128,96},{160,128},{192,160},{224,192},{0,2... | collective-permute-start | bytes 110600 | tf_op jit(solution)/shard_map/ppermute | solution.py:44
  8.6 6.3 %collective-permute-start.2 = (f32[9,6,4,1,128]{4,3,2,1,0:T(1,128)S(1)}, f32[9,6,4,1,128]{4,3,2,1,0:T(1,128)S(1)}, u32[]{:S(2)}, u32[]{:S(2)}) collective-permute-start(f32[9,6,4,1,128]{4,3,2,1,0:T(1,128)S(1)} %get-tuple-element.12), channel_id=1, source_target_pairs={{0,1},{1,2},{2,3},{3,0},{4,5},{5,6},{6,7},{7,4},{8,9},{9,10},{10,1... | collective-permute-start | bytes 331784 | tf_op jit(solution)/shard_map/ppermute | solution.py:43
  10.2 4.7 %collective-permute-start.3 = (f32[9,6,4,1,128]{4,3,2,1,0:T(1,128)S(1)}, f32[9,6,4,1,128]{4,3,2,1,0:T(1,128)S(1)}, u32[]{:S(2)}, u32[]{:S(2)}) collective-permute-start(f32[9,6,4,1,128]{4,3,2,1,0:T(1,128)S(1)} %get-tuple-element.13), channel_id=1, source_target_pairs={{1,0},{2,1},{3,2},{0,3},{5,4},{6,5},{7,6},{4,7},{9,8},{10,9},{11,1... | collective-permute-start | bytes 331784 | tf_op jit(solution)/shard_map/ppermute | solution.py:44
  15.3 7.0 %copy-start.1 = (f32[3,4,4,2,128]{4,3,2,1,0:T(2,128)S(1)}, f32[3,4,4,2,128]{4,3,2,1,0:T(2,128)}, u32[]{:S(2)}) copy-start(f32[3,4,4,2,128]{4,3,2,1,0:T(2,128)} %param.7) | copy-start | bytes 147460
  15.3 7.0 %copy-start.2 = (f32[3,4,4,2,128]{4,3,2,1,0:T(2,128)S(1)}, f32[3,4,4,2,128]{4,3,2,1,0:T(2,128)}, u32[]{:S(2)}) copy-start(f32[3,4,4,2,128]{4,3,2,1,0:T(2,128)} %param.6) | copy-start | bytes 147460
  15.3 7.0 %copy-start.3 = (f32[3,4,4,2,128]{4,3,2,1,0:T(2,128)S(1)}, f32[3,4,4,2,128]{4,3,2,1,0:T(2,128)}, u32[]{:S(2)}) copy-start(f32[3,4,4,2,128]{4,3,2,1,0:T(2,128)} %param.5) | copy-start | bytes 147460
  15.4 25.4 %collective-permute-start.4 = (f32[9,6,1,4,128]{4,3,2,1,0:T(4,128)S(1)}, f32[9,6,1,4,128]{4,3,2,1,0:T(4,128)S(1)}, u32[]{:S(2)}, u32[]{:S(2)}) collective-permute-start(f32[9,6,1,4,128]{4,3,2,1,0:T(4,128)S(1)} %get-tuple-element.10), channel_id=1, source_target_pairs={{0,4},{4,8},{8,12},{12,16},{16,20},{20,24},{24,28},{28,0},{1,5},{5... | collective-permute-start | bytes 331784 | tf_op jit(solution)/shard_map/ppermute | solution.py:383
  22.1 18.7 %collective-permute-start.5 = (f32[9,6,1,4,128]{4,3,2,1,0:T(4,128)S(1)}, f32[9,6,1,4,128]{4,3,2,1,0:T(4,128)S(1)}, u32[]{:S(2)}, u32[]{:S(2)}) collective-permute-start(f32[9,6,1,4,128]{4,3,2,1,0:T(4,128)S(1)} %get-tuple-element.11), channel_id=1, source_target_pairs={{4,0},{8,4},{12,8},{16,12},{20,16},{24,20},{28,24},{0,28},{5,1},{9... | collective-permute-start | bytes 331784 | tf_op jit(solution)/shard_map/ppermute | solution.py:384
  22.3 0.7 copy-start
  46.2 4.9 %collective-permute-start.6 = (f32[3,1,4,2,128]{4,3,2,1,0:T(2,128)S(1)}, f32[3,1,4,2,128]{4,3,2,1,0:T(2,128)S(1)}, u32[]{:S(2)}, u32[]{:S(2)}) collective-permute-start(f32[3,1,4,2,128]{4,3,2,1,0:T(2,128)S(1)} %get-tuple-element.20), channel_id=1, source_target_pairs={{0,32},{32,64},{64,96},{96,128},{128,160},{160,192},{192,224},{224... | collective-permute-start | bytes 36872 | tf_op jit(solution)/shard_map/ppermute | solution.py:43
  46.2 4.9 %collective-permute-start.7 = (f32[3,1,4,2,128]{4,3,2,1,0:T(2,128)S(1)}, f32[3,1,4,2,128]{4,3,2,1,0:T(2,128)S(1)}, u32[]{:S(2)}, u32[]{:S(2)}) collective-permute-start(f32[3,1,4,2,128]{4,3,2,1,0:T(2,128)S(1)} %get-tuple-element.21), channel_id=1, source_target_pairs={{32,0},{64,32},{96,64},{128,96},{160,128},{192,160},{224,192},{0,2... | collective-permute-start | bytes 36872 | tf_op jit(solution)/shard_map/ppermute | solution.py:44
  51.3 15.2 %collective-permute-start.8 = (f32[3,6,4,1,128]{4,3,2,1,0:T(1,128)S(1)}, f32[3,6,4,1,128]{4,3,2,1,0:T(1,128)S(1)}, u32[]{:S(2)}, u32[]{:S(2)}) collective-permute-start(f32[3,6,4,1,128]{4,3,2,1,0:T(1,128)S(1)} %get-tuple-element.18), channel_id=1, source_target_pairs={{0,1},{1,2},{2,3},{3,0},{4,5},{5,6},{6,7},{7,4},{8,9},{9,10},{10,1... | collective-permute-start | bytes 110600 | tf_op jit(solution)/shard_map/ppermute | solution.py:43
  52.8 13.7 %collective-permute-start.9 = (f32[3,6,4,1,128]{4,3,2,1,0:T(1,128)S(1)}, f32[3,6,4,1,128]{4,3,2,1,0:T(1,128)S(1)}, u32[]{:S(2)}, u32[]{:S(2)}) collective-permute-start(f32[3,6,4,1,128]{4,3,2,1,0:T(1,128)S(1)} %get-tuple-element.19), channel_id=1, source_target_pairs={{1,0},{2,1},{3,2},{0,3},{5,4},{6,5},{7,6},{4,7},{9,8},{10,9},{11,1... | collective-permute-start | bytes 110600 | tf_op jit(solution)/shard_map/ppermute | solution.py:44
  54.6 27.1 %all-to-all-start = ((f32[256,1,128]{2,1,0:T(1,128)}), f32[256,1,128]{2,1,0:T(1,128)S(1)}, u32[]{:S(2)}, u32[]{:S(2)}) async-start(f32[256,1,128]{2,1,0:T(1,128)} %bitcast.9), calls=%async_computation | async-start | bytes 262144 | tf_op jit(solution)/shard_map/all_to_all | solution.py:404
  66.7 9.0 %collective-permute-start.10 = (f32[3,6,1,4,128]{4,3,2,1,0:T(4,128)S(1)}, f32[3,6,1,4,128]{4,3,2,1,0:T(4,128)S(1)}, u32[]{:S(2)}, u32[]{:S(2)}) collective-permute-start(f32[3,6,1,4,128]{4,3,2,1,0:T(4,128)S(1)} %get-tuple-element.14), channel_id=1, source_target_pairs={{0,4},{4,8},{8,12},{12,16},{16,20},{20,24},{24,28},{28,0},{1,5},{5... | collective-permute-start | bytes 110600 | tf_op jit(solution)/shard_map/ppermute | solution.py:383
  73.1 8.6 %collective-permute-start.11 = (f32[3,6,1,4,128]{4,3,2,1,0:T(4,128)S(1)}, f32[3,6,1,4,128]{4,3,2,1,0:T(4,128)S(1)}, u32[]{:S(2)}, u32[]{:S(2)}) collective-permute-start(f32[3,6,1,4,128]{4,3,2,1,0:T(4,128)S(1)} %get-tuple-element.15), channel_id=1, source_target_pairs={{4,0},{8,4},{12,8},{16,12},{20,16},{24,20},{28,24},{0,28},{5,1},{9... | collective-permute-start | bytes 110600 | tf_op jit(solution)/shard_map/ppermute | solution.py:384

commit v7 on v6

--- a/solution.py
+++ b/solution.py
@@ -292,7 +292,7 @@
     return STEP_LIMIT * lax.rsqrt(jnp.broadcast_to(peak, (8, SLOTS)) + 1e-12)
 
 
-def start_inner(pad_ref, loc_ref, mob_ref, sums_ref, pf, vf, pt, vt, qf):
+def start_inner(pad_ref, loc_ref, sums_ref, pf, vf, pt, vt, qf):
     prepare_sources(pad_ref, None, pf, vf, True)
     lay_out_sources(pf, vf, pt, vt)
     prepare_targets(loc_ref, None, qf)
@@ -308,7 +308,7 @@
 
 
 def start_outer(
-    rim_ref, loc_ref, mob_ref, sums_ref, speed_ref, peak_ref, pf, vf, pt, vt, qf, tf
+    rim_ref, loc_ref, sums_ref, speed_ref, peak_ref, pf, vf, pt, vt, qf, tf
 ):
     prepare_sources(rim_ref, None, pf, vf, False)
     lay_out_sources(pf, vf, pt, vt)
@@ -318,7 +318,7 @@
     for g in range(CELLS // 8):
         rows = pl.ds(g * 8, 8)
         force = forces_of(g, every[g], loc_ref, tf)
-        mobility = mob_ref[rows, :]
+        mobility = loc_ref[9, rows, :]
         speed = [mobility * f for f in force]
         for a in range(3):
             speed_ref[a, rows, :] = speed[a]
@@ -330,7 +330,7 @@
 
 
 def end_outer(
-    rim_ref, loc_ref, mob_ref, rimv_ref, speed_ref, peak_ref, sums_ref, moved_ref, force_ref,
+    rim_ref, loc_ref, rimv_ref, speed_ref, peak_ref, sums_ref, moved_ref, force_ref,
     pf, vf, pt, vt, qf, tf,
 ):
     step = step_of(peak_ref)
@@ -341,7 +341,7 @@
     for g in range(CELLS // 8):
         rows = pl.ds(g * 8, 8)
         force = forces_of(g, every[g], loc_ref, tf)
-        mobility = mob_ref[rows, :]
+        mobility = loc_ref[9, rows, :]
         for a in range(3):
             force_ref[a, rows, :] = force[a]
             moved_ref[a, rows, :] = loc_ref[a, rows, :] + 0.5 * step * (
@@ -393,20 +393,19 @@
     slot = lax.broadcasted_iota(jnp.int32, fields.shape, 4)
     fields = jnp.where((row < 6) | (slot < occupancy[None, ..., None]), fields, 0.0)
     pad, rim = widened(fields)
-    loc = fields.reshape(9, CELLS, SLOTS)
-    mob = mobility.reshape(CELLS, SLOTS)
+    loc = jnp.concatenate([fields, mobility[None]], 0).reshape(10, CELLS, SLOTS)
     devices = lax.axis_size(EVERY)
     peaks = jax.ShapeDtypeStruct((devices, SLOTS), F32)
-    (sums,) = call(start_inner, [SUMS], [pad, loc, mob], "start_inner", True)
+    (sums,) = call(start_inner, [SUMS], [pad, loc], "start_inner", True)
     speed, peaks = call(
-        start_outer, [VEC, peaks], [rim, loc, mob, sums], "start_outer", False
+        start_outer, [VEC, peaks], [rim, loc, sums], "start_outer", False
     )
     peaks = lax.all_to_all(peaks.reshape(devices, 1, SLOTS), EVERY, 0, 0)
     peaks = peaks.reshape(devices, SLOTS)
     padv, rimv = widened(speed.reshape(3, NX, NY, NZ, SLOTS))
     (sums,) = call(end_inner, [SUMS], [pad, loc, padv, speed, peaks], "end_inner", True)
     moved, force = call(
-        end_outer, [VEC, VEC], [rim, loc, mob, rimv, speed, peaks, sums], "end_outer", False
+        end_outer, [VEC, VEC], [rim, loc, rimv, speed, peaks, sums], "end_outer", False
     )
     shape = (3, NX, NY, NZ, SLOTS)
     return moved.reshape(shape), force.reshape(shape)

time: 105 us -> 104 us (level)
  no operation moved by 1% of the time
where the time goes in v7:
time: 104 us
  Pallas kernels  46.3 us (45%)
  starting transfers between devices  40.1 us (39%)
  waiting for transfers between devices  14 us (13%)
  other arithmetic  1.74 us (2%)
  local copies, waits for them, and re-layouts  1.2 us (1%)
    pallas_call x4, Pallas kernels, call(): pl.pallas_call(kernel, out_shape=out_shapes, in_specs=[whole] * len(opera...  46.3 us
    ppermute x2, starting transfers between devices, widened(): low = lax.ppermute(block[:, :, NY - 1:], GY, forward)  13.2 us
    all_to_all x1, starting transfers between devices, on_device(): peaks = lax.all_to_all(peaks.reshape(devices, 1, SLOTS), EVERY, 0, 0)  11.9 us
    ppermute x4, starting transfers between devices, extended(): high = lax.ppermute(lax.slice_in_dim(block, 0, 1, axis=dim), axis, backward)  11.2 us
    ppermute x2, waiting for transfers between devices, widened(): high = lax.ppermute(block[:, :, :1], GY, backward)  6 us
    ppermute x4, waiting for transfers between devices, extended(): lax.ppermute(lax.slice_in_dim(block, size - 1, size, axis=dim), axis, for...  5.78 us
    ppermute x4, starting transfers between devices, extended(): lax.ppermute(lax.slice_in_dim(block, size - 1, size, axis=dim), axis, for...  3.22 us
    ppermute x2, waiting for transfers between devices, widened(): low = lax.ppermute(block[:, :, NY - 1:], GY, forward)  2.09 us
  transfers between devices with their start and end apart: 13, of which 6 were waited for; matrix products, arithmetic and copies ran while one was open for 0% of the time, Pallas kernels for 17%

profile of v7, /device:TPU:8, one launch (start us, length us, event | category | flops | bytes accessed | tf_op | source)
XLA Modules:
  0.0 104.2 jit_solution(13805938407601340451)
XLA Ops:
  0.6 0.8 copy.11
  1.4 1.0 or_select_fusion
  2.5 0.1 collective-permute-start
  2.5 4.1 %collective-permute-start.1 = (f32[9,1,4,2,128]{4,3,2,1,0:T(2,128)S(1)}, f32[9,1,4,2,128]{4,3,2,1,0:T(2,128)S(1)}, u32[]{:S(2)}, u32[]{:S(2)}) collective-permute-start(f32[9,1,4,2,128]{4,3,2,1,0:T(2,128)S(1)} %get-tuple-element.17), channel_id=1, source_target_pairs={{32,0},{64,32},{96,64},{128,96},{160,128},{192,160},{224,192},{0,2... | collective-permute-start | bytes 110600 | tf_op jit(solution)/shard_map/ppermute | solution.py:44
  6.7 0.1 lt.28
  6.8 1.6 %collective-permute-done = f32[9,1,4,2,128]{4,3,2,1,0:T(2,128)S(1)} collective-permute-done((f32[9,1,4,2,128]{4,3,2,1,0:T(2,128)S(1)}, f32[9,1,4,2,128]{4,3,2,1,0:T(2,128)S(1)}, u32[]{:S(2)}, u32[]{:S(2)}) %collective-permute-start) | collective-permute-done | bytes 36896 | tf_op jit(solution)/shard_map/ppermute | solution.py:43
  8.3 0.0 collective-permute-done.1
  8.3 0.1 pad_maximum_fusion.1
  8.5 0.0 copy-start
  8.5 0.0 copy-start.1
  8.5 0.0 copy-start.2
  8.5 0.2 fusion.2
  8.7 1.6 %collective-permute-start.2 = (f32[9,6,4,1,128]{4,3,2,1,0:T(1,128)S(1)}, f32[9,6,4,1,128]{4,3,2,1,0:T(1,128)S(1)}, u32[]{:S(2)}, u32[]{:S(2)}) collective-permute-start(f32[9,6,4,1,128]{4,3,2,1,0:T(1,128)S(1)} %get-tuple-element.12), channel_id=1, source_target_pairs={{0,1},{1,2},{2,3},{3,0},{4,5},{5,6},{6,7},{7,4},{8,9},{9,10},{10,1... | collective-permute-start | bytes 331784 | tf_op jit(solution)/shard_map/ppermute | solution.py:43
  10.2 1.7 %collective-permute-start.3 = (f32[9,6,4,1,128]{4,3,2,1,0:T(1,128)S(1)}, f32[9,6,4,1,128]{4,3,2,1,0:T(1,128)S(1)}, u32[]{:S(2)}, u32[]{:S(2)}) collective-permute-start(f32[9,6,4,1,128]{4,3,2,1,0:T(1,128)S(1)} %get-tuple-element.13), channel_id=1, source_target_pairs={{1,0},{2,1},{3,2},{0,3},{5,4},{6,5},{7,6},{4,7},{9,8},{10,9},{11,1... | collective-permute-start | bytes 331784 | tf_op jit(solution)/shard_map/ppermute | solution.py:44
  12.0 0.0 copy-done
  12.0 0.0 copy-done.1
  12.0 0.0 copy-done.2
  12.0 0.1 maximum_select_fusion
  12.1 2.8 %collective-permute-done.2 = f32[9,6,4,1,128]{4,3,2,1,0:T(1,128)S(1)} collective-permute-done((f32[9,6,4,1,128]{4,3,2,1,0:T(1,128)S(1)}, f32[9,6,4,1,128]{4,3,2,1,0:T(1,128)S(1)}, u32[]{:S(2)}, u32[]{:S(2)}) %collective-permute-start.2) | collective-permute-done | bytes 110624 | tf_op jit(solution)/shard_map/ppermute | solution.py:43
  14.9 0.1 collective-permute-done.3
  15.0 0.3 pad_maximum_fusion
  15.3 0.0 copy-start.3
  15.4 6.7 %collective-permute-start.4 = (f32[9,6,1,4,128]{4,3,2,1,0:T(4,128)S(1)}, f32[9,6,1,4,128]{4,3,2,1,0:T(4,128)S(1)}, u32[]{:S(2)}, u32[]{:S(2)}) collective-permute-start(f32[9,6,1,4,128]{4,3,2,1,0:T(4,128)S(1)} %get-tuple-element.10), channel_id=1, source_target_pairs={{0,4},{4,8},{8,12},{12,16},{16,20},{20,24},{24,28},{28,0},{1,5},{5... | collective-permute-start | bytes 331784 | tf_op jit(solution)/shard_map/ppermute | solution.py:383
  22.1 0.2 collective-permute-start.5
  22.3 0.0 copy-done.3
  22.3 17.7 %start_inner.1.sums_ref = f32[1280,128]{1,0:T(8,128)S(1)} custom-call(f32[9,96,128]{2,1,0:T(8,128)S(1)} %bitcast.15, f32[10,32,128]{2,1,0:T(8,128)S(1)} %pad_maximum_fusion.3.loc_ref), custom_call_target="tpu_custom_call" | custom-call | tf_op jit(solution)/shard_map/start_inner/pallas_call | solution.py:365
  40.1 0.0 collective-permute-done.4
  40.1 0.0 collective-permute-done.5
  40.1 0.1 pad_maximum_fusion.2
  40.1 5.3 %start_outer.1 = (f32[3,32,128]{2,1,0:T(8,128)S(1)}, f32[256,128]{1,0:T(8,128)}) custom-call(f32[9,48,128]{2,1,0:T(8,128)S(1)} %bitcast.17, f32[10,32,128]{2,1,0:T(8,128)S(1)} %pad_maximum_fusion.3.loc_ref, f32[1280,128]{1,0:T(8,128)S(1)} %start_inner.1.sums_ref), custom_call_target="tpu_custom_call" | custom-call | tf_op jit(solution)/shard_map/start_outer/pallas_call | solution.py:365
  45.5 0.0 collective-permute-start.6
  45.5 3.5 %collective-permute-start.7 = (f32[3,1,4,2,128]{4,3,2,1,0:T(2,128)S(1)}, f32[3,1,4,2,128]{4,3,2,1,0:T(2,128)S(1)}, u32[]{:S(2)}, u32[]{:S(2)}) collective-permute-start(f32[3,1,4,2,128]{4,3,2,1,0:T(2,128)S(1)} %get-tuple-element.21), channel_id=1, source_target_pairs={{32,0},{64,32},{96,64},{128,96},{160,128},{192,160},{224,192},{0,2... | collective-permute-start | bytes 36872 | tf_op jit(solution)/shard_map/ppermute | solution.py:44
  49.0 1.4 %collective-permute-done.6 = f32[3,1,4,2,128]{4,3,2,1,0:T(2,128)S(1)} collective-permute-done((f32[3,1,4,2,128]{4,3,2,1,0:T(2,128)S(1)}, f32[3,1,4,2,128]{4,3,2,1,0:T(2,128)S(1)}, u32[]{:S(2)}, u32[]{:S(2)}) %collective-permute-start.6) | collective-permute-done | bytes 12320 | tf_op jit(solution)/shard_map/ppermute | solution.py:43
  50.4 0.0 collective-permute-done.7
  50.5 0.1 fusion.5
  50.5 1.6 %collective-permute-start.8 = (f32[3,6,4,1,128]{4,3,2,1,0:T(1,128)S(1)}, f32[3,6,4,1,128]{4,3,2,1,0:T(1,128)S(1)}, u32[]{:S(2)}, u32[]{:S(2)}) collective-permute-start(f32[3,6,4,1,128]{4,3,2,1,0:T(1,128)S(1)} %get-tuple-element.18), channel_id=1, source_target_pairs={{0,1},{1,2},{2,3},{3,0},{4,5},{5,6},{6,7},{7,4},{8,9},{9,10},{10,1... | collective-permute-start | bytes 110600 | tf_op jit(solution)/shard_map/ppermute | solution.py:43
  52.1 1.7 %collective-permute-start.9 = (f32[3,6,4,1,128]{4,3,2,1,0:T(1,128)S(1)}, f32[3,6,4,1,128]{4,3,2,1,0:T(1,128)S(1)}, u32[]{:S(2)}, u32[]{:S(2)}) collective-permute-start(f32[3,6,4,1,128]{4,3,2,1,0:T(1,128)S(1)} %get-tuple-element.19), channel_id=1, source_target_pairs={{1,0},{2,1},{3,2},{0,3},{5,4},{6,5},{7,6},{4,7},{9,8},{10,9},{11,1... | collective-permute-start | bytes 110600 | tf_op jit(solution)/shard_map/ppermute | solution.py:44
  53.8 11.9 %all-to-all-start = ((f32[256,1,128]{2,1,0:T(1,128)}), f32[256,1,128]{2,1,0:T(1,128)S(1)}, u32[]{:S(2)}, u32[]{:S(2)}) async-start(f32[256,1,128]{2,1,0:T(1,128)} %bitcast.9), calls=%async_computation | async-start | bytes 262144 | tf_op jit(solution)/shard_map/all_to_all | solution.py:403
  65.8 0.0 collective-permute-done.8
  65.8 0.0 collective-permute-done.9
  65.8 0.1 pad_maximum_fusion.4
  65.9 6.4 %collective-permute-start.10 = (f32[3,6,1,4,128]{4,3,2,1,0:T(4,128)S(1)}, f32[3,6,1,4,128]{4,3,2,1,0:T(4,128)S(1)}, u32[]{:S(2)}, u32[]{:S(2)}) collective-permute-start(f32[3,6,1,4,128]{4,3,2,1,0:T(4,128)S(1)} %get-tuple-element.14), channel_id=1, source_target_pairs={{0,4},{4,8},{8,12},{12,16},{16,20},{20,24},{24,28},{28,0},{1,5},{5... | collective-permute-start | bytes 110600 | tf_op jit(solution)/shard_map/ppermute | solution.py:383
  72.4 0.5 collective-permute-start.11
  72.8 2.1 %collective-permute-done.10 = f32[3,6,1,4,128]{4,3,2,1,0:T(4,128)S(1)} collective-permute-done((f32[3,6,1,4,128]{4,3,2,1,0:T(4,128)S(1)}, f32[3,6,1,4,128]{4,3,2,1,0:T(4,128)S(1)}, u32[]{:S(2)}, u32[]{:S(2)}) %collective-permute-start.10) | collective-permute-done | bytes 36896 | tf_op jit(solution)/shard_map/ppermute | solution.py:383
  74.9 6.0 %collective-permute-done.11 = f32[3,6,1,4,128]{4,3,2,1,0:T(4,128)S(1)} collective-permute-done((f32[3,6,1,4,128]{4,3,2,1,0:T(4,128)S(1)}, f32[3,6,1,4,128]{4,3,2,1,0:T(4,128)S(1)}, u32[]{:S(2)}, u32[]{:S(2)}) %collective-permute-start.11) | collective-permute-done | bytes 36896 | tf_op jit(solution)/shard_map/ppermute | solution.py:384
  80.9 0.0 all-to-all-done
  80.9 17.8 %end_inner.1.sums_ref = f32[1280,128]{1,0:T(8,128)S(1)} custom-call(f32[9,96,128]{2,1,0:T(8,128)S(1)} %bitcast.16, f32[10,32,128]{2,1,0:T(8,128)S(1)} %pad_maximum_fusion.3.loc_ref, f32[3,96,128]{2,1,0:T(8,128)S(1)} %bitcast.24, f32[3,32,128]{2,1,0:T(8,128)S(1)} %get-tuple-element.6.speed_ref, f32[256,128]{1,0:T(8,128)S(1)} %bitcast.19), custom_call_target="tpu_custom_call" | custom-call | tf_op jit(solution)/shard_map/end_inner/pallas_call | solution.py:365
  98.8 5.4 %end_outer.1 = (f32[3,32,128]{2,1,0:T(8,128)}, f32[3,32,128]{2,1,0:T(8,128)}) custom-call(f32[9,48,128]{2,1,0:T(8,128)S(1)} %bitcast.18, f32[10,32,128]{2,1,0:T(8,128)S(1)} %pad_maximum_fusion.3.loc_ref, f32[3,48,128]{2,1,0:T(8,128)S(1)} %bitcast.25, f32[3,32,128]{2,1,0:T(8,128)S(1)} %get-tuple-element.6.speed_ref, f32[256,128]{1,0:T(8,128)S(1)} %bitcast.20, ...), custom_call_target="tpu_custom_call" | custom-call | tf_op jit(solution)/shard_map/end_outer/pallas_call | solution.py:365
  (8 shorter events, 0.1 us)
Async XLA Ops:
  2.5 5.9 %collective-permute-start = (f32[9,1,4,2,128]{4,3,2,1,0:T(2,128)S(1)}, f32[9,1,4,2,128]{4,3,2,1,0:T(2,128)S(1)}, u32[]{:S(2)}, u32[]{:S(2)}) collective-permute-start(f32[9,1,4,2,128]{4,3,2,1,0:T(2,128)S(1)} %get-tuple-element.16), channel_id=1, source_target_pairs={{0,32},{32,64},{64,96},{96,128},{128,160},{160,192},{192,224},{224... | collective-permute-start | bytes 110600 | tf_op jit(solution)/shard_map/ppermute | solution.py:43
  2.5 5.8 %collective-permute-start.1 = (f32[9,1,4,2,128]{4,3,2,1,0:T(2,128)S(1)}, f32[9,1,4,2,128]{4,3,2,1,0:T(2,128)S(1)}, u32[]{:S(2)}, u32[]{:S(2)}) collective-permute-start(f32[9,1,4,2,128]{4,3,2,1,0:T(2,128)S(1)} %get-tuple-element.17), channel_id=1, source_target_pairs={{32,0},{64,32},{96,64},{128,96},{160,128},{192,160},{224,192},{0,2... | collective-permute-start | bytes 110600 | tf_op jit(solution)/shard_map/ppermute | solution.py:44
  8.5 3.5 %copy-start = (f32[3,4,4,2,128]{4,3,2,1,0:T(2,128)S(1)}, f32[3,4,4,2,128]{4,3,2,1,0:T(2,128)}, u32[]{:S(2)}) copy-start(f32[3,4,4,2,128]{4,3,2,1,0:T(2,128)} %param.7) | copy-start | bytes 147460
  8.5 3.5 %copy-start.1 = (f32[3,4,4,2,128]{4,3,2,1,0:T(2,128)S(1)}, f32[3,4,4,2,128]{4,3,2,1,0:T(2,128)}, u32[]{:S(2)}) copy-start(f32[3,4,4,2,128]{4,3,2,1,0:T(2,128)} %param.6) | copy-start | bytes 147460
  8.5 3.5 %copy-start.2 = (f32[3,4,4,2,128]{4,3,2,1,0:T(2,128)S(1)}, f32[3,4,4,2,128]{4,3,2,1,0:T(2,128)}, u32[]{:S(2)}) copy-start(f32[3,4,4,2,128]{4,3,2,1,0:T(2,128)} %param.5) | copy-start | bytes 147460
  8.7 6.3 %collective-permute-start.2 = (f32[9,6,4,1,128]{4,3,2,1,0:T(1,128)S(1)}, f32[9,6,4,1,128]{4,3,2,1,0:T(1,128)S(1)}, u32[]{:S(2)}, u32[]{:S(2)}) collective-permute-start(f32[9,6,4,1,128]{4,3,2,1,0:T(1,128)S(1)} %get-tuple-element.12), channel_id=1, source_target_pairs={{0,1},{1,2},{2,3},{3,0},{4,5},{5,6},{6,7},{7,4},{8,9},{9,10},{10,1... | collective-permute-start | bytes 331784 | tf_op jit(solution)/shard_map/ppermute | solution.py:43
  10.2 4.7 %collective-permute-start.3 = (f32[9,6,4,1,128]{4,3,2,1,0:T(1,128)S(1)}, f32[9,6,4,1,128]{4,3,2,1,0:T(1,128)S(1)}, u32[]{:S(2)}, u32[]{:S(2)}) collective-permute-start(f32[9,6,4,1,128]{4,3,2,1,0:T(1,128)S(1)} %get-tuple-element.13), channel_id=1, source_target_pairs={{1,0},{2,1},{3,2},{0,3},{5,4},{6,5},{7,6},{4,7},{9,8},{10,9},{11,1... | collective-permute-start | bytes 331784 | tf_op jit(solution)/shard_map/ppermute | solution.py:44
  15.3 7.0 %copy-start.3 = (f32[4,4,2,128]{3,2,1,0:T(2,128)S(1)}, f32[4,4,2,128]{3,2,1,0:T(2,128)}, u32[]{:S(2)}) copy-start(f32[4,4,2,128]{3,2,1,0:T(2,128)} %param.8) | copy-start | bytes 49156
  15.4 24.7 %collective-permute-start.4 = (f32[9,6,1,4,128]{4,3,2,1,0:T(4,128)S(1)}, f32[9,6,1,4,128]{4,3,2,1,0:T(4,128)S(1)}, u32[]{:S(2)}, u32[]{:S(2)}) collective-permute-start(f32[9,6,1,4,128]{4,3,2,1,0:T(4,128)S(1)} %get-tuple-element.10), channel_id=1, source_target_pairs={{0,4},{4,8},{8,12},{12,16},{16,20},{20,24},{24,28},{28,0},{1,5},{5... | collective-permute-start | bytes 331784 | tf_op jit(solution)/shard_map/ppermute | solution.py:383
  22.1 17.9 %collective-permute-start.5 = (f32[9,6,1,4,128]{4,3,2,1,0:T(4,128)S(1)}, f32[9,6,1,4,128]{4,3,2,1,0:T(4,128)S(1)}, u32[]{:S(2)}, u32[]{:S(2)}) collective-permute-start(f32[9,6,1,4,128]{4,3,2,1,0:T(4,128)S(1)} %get-tuple-element.11), channel_id=1, source_target_pairs={{4,0},{8,4},{12,8},{16,12},{20,16},{24,20},{28,24},{0,28},{5,1},{9... | collective-permute-start | bytes 331784 | tf_op jit(solution)/shard_map/ppermute | solution.py:384
  45.5 4.9 %collective-permute-start.6 = (f32[3,1,4,2,128]{4,3,2,1,0:T(2,128)S(1)}, f32[3,1,4,2,128]{4,3,2,1,0:T(2,128)S(1)}, u32[]{:S(2)}, u32[]{:S(2)}) collective-permute-start(f32[3,1,4,2,128]{4,3,2,1,0:T(2,128)S(1)} %get-tuple-element.20), channel_id=1, source_target_pairs={{0,32},{32,64},{64,96},{96,128},{128,160},{160,192},{192,224},{224... | collective-permute-start | bytes 36872 | tf_op jit(solution)/shard_map/ppermute | solution.py:43
  45.5 4.9 %collective-permute-start.7 = (f32[3,1,4,2,128]{4,3,2,1,0:T(2,128)S(1)}, f32[3,1,4,2,128]{4,3,2,1,0:T(2,128)S(1)}, u32[]{:S(2)}, u32[]{:S(2)}) collective-permute-start(f32[3,1,4,2,128]{4,3,2,1,0:T(2,128)S(1)} %get-tuple-element.21), channel_id=1, source_target_pairs={{32,0},{64,32},{96,64},{128,96},{160,128},{192,160},{224,192},{0,2... | collective-permute-start | bytes 36872 | tf_op jit(solution)/shard_map/ppermute | solution.py:44
  50.5 15.2 %collective-permute-start.8 = (f32[3,6,4,1,128]{4,3,2,1,0:T(1,128)S(1)}, f32[3,6,4,1,128]{4,3,2,1,0:T(1,128)S(1)}, u32[]{:S(2)}, u32[]{:S(2)}) collective-permute-start(f32[3,6,4,1,128]{4,3,2,1,0:T(1,128)S(1)} %get-tuple-element.18), channel_id=1, source_target_pairs={{0,1},{1,2},{2,3},{3,0},{4,5},{5,6},{6,7},{7,4},{8,9},{9,10},{10,1... | collective-permute-start | bytes 110600 | tf_op jit(solution)/shard_map/ppermute | solution.py:43
  52.1 13.7 %collective-permute-start.9 = (f32[3,6,4,1,128]{4,3,2,1,0:T(1,128)S(1)}, f32[3,6,4,1,128]{4,3,2,1,0:T(1,128)S(1)}, u32[]{:S(2)}, u32[]{:S(2)}) collective-permute-start(f32[3,6,4,1,128]{4,3,2,1,0:T(1,128)S(1)} %get-tuple-element.19), channel_id=1, source_target_pairs={{1,0},{2,1},{3,2},{0,3},{5,4},{6,5},{7,6},{4,7},{9,8},{10,9},{11,1... | collective-permute-start | bytes 110600 | tf_op jit(solution)/shard_map/ppermute | solution.py:44
  53.8 27.1 %all-to-all-start = ((f32[256,1,128]{2,1,0:T(1,128)}), f32[256,1,128]{2,1,0:T(1,128)S(1)}, u32[]{:S(2)}, u32[]{:S(2)}) async-start(f32[256,1,128]{2,1,0:T(1,128)} %bitcast.9), calls=%async_computation | async-start | bytes 262144 | tf_op jit(solution)/shard_map/all_to_all | solution.py:403
  65.9 9.0 %collective-permute-start.10 = (f32[3,6,1,4,128]{4,3,2,1,0:T(4,128)S(1)}, f32[3,6,1,4,128]{4,3,2,1,0:T(4,128)S(1)}, u32[]{:S(2)}, u32[]{:S(2)}) collective-permute-start(f32[3,6,1,4,128]{4,3,2,1,0:T(4,128)S(1)} %get-tuple-element.14), channel_id=1, source_target_pairs={{0,4},{4,8},{8,12},{12,16},{16,20},{20,24},{24,28},{28,0},{1,5},{5... | collective-permute-start | bytes 110600 | tf_op jit(solution)/shard_map/ppermute | solution.py:383
  72.4 8.6 %collective-permute-start.11 = (f32[3,6,1,4,128]{4,3,2,1,0:T(4,128)S(1)}, f32[3,6,1,4,128]{4,3,2,1,0:T(4,128)S(1)}, u32[]{:S(2)}, u32[]{:S(2)}) collective-permute-start(f32[3,6,1,4,128]{4,3,2,1,0:T(4,128)S(1)} %get-tuple-element.15), channel_id=1, source_target_pairs={{4,0},{8,4},{12,8},{16,12},{20,16},{24,20},{28,24},{0,28},{5,1},{9... | collective-permute-start | bytes 110600 | tf_op jit(solution)/shard_map/ppermute | solution.py:384
